TPU v7x, 32 devices: a whole 2x2x4 slice. The times are simulated.
32 devices in a mesh: dp: 8 (over z, x), mlp: 4 (over y, core).
Axes of the slice: x: 2, y: 2, z: 4, core: 2. Of those that a mesh axis runs over, the one named last changes fastest.
Arguments:
- tokens: bfloat16 [32768, 768], P(('dp', 'mlp')), may hold values from -6 to 6
- cotangent: bfloat16 [32768, 768], P(('dp', 'mlp')), may hold values from -6 to 6
- vectors: float32 [14, 768], replicated
- vector_moments: float32 [14, 768], replicated, may hold values from 819.2 to 26214.4
- decays: float32 [2], replicated, may hold values from 0.9 to 0.98
- owner: int32 [4, 3], replicated, may hold values from 0 to 7, as said below
- master_slots: float32 [8, 4, 768, 768], P('dp', 'mlp'), as said below
- left_slots: float32 [8, 4, 768, 768], P('dp', 'mlp'), as said below
- right_slots: float32 [8, 4, 768, 768], P('dp', 'mlp'), as said below
- left_roots: float32 [8, 4, 768, 768], P('dp', 'mlp'), as said below
- right_roots: float32 [8, 4, 768, 768], P('dp', 'mlp'), as said below
- grid_height: int32 [128], P(('dp', 'mlp')), may hold values from 8 to 24, as said below
- grid_width: int32 [128], P(('dp', 'mlp')), may hold values from 8 to 24, as said below
- patch_rows: int32 [32768], P(('dp', 'mlp')), may hold values from 0 to 23, as said below
- patch_cols: int32 [32768], P(('dp', 'mlp')), may hold values from 0 to 23, as said below
- segment: int32 [32768], P(('dp', 'mlp')), may hold values from 0 to 3, as said below
Outputs:
- output: bfloat16 [32768, 768], P(('dp', 'mlp'))
- input_grad: float32 [32768, 768], P(('dp', 'mlp'))
- slot_grads: float32 [8, 4, 768, 768], P('dp', 'mlp')
- new_left: float32 [8, 4, 768, 768], P('dp', 'mlp')
- new_right: float32 [8, 4, 768, 768], P('dp', 'mlp')
- new_master: float32 [8, 4, 768, 768], P('dp', 'mlp')
- vector_grads: float32 [14, 768], P(None, 'mlp')
- new_vector_moments: float32 [14, 768], P(None, 'mlp')
- new_vectors: float32 [14, 768], P(None, 'mlp')
Inputs may be any that keep to these rules, and one draw needn't show every extreme that they name: `owner`: the entries of a row differ; block kind 0 of row m is the m-th of the query, key, value and output projections, kind 1 the m-th 768 columns of the up projection, kind 2 the m-th 768 rows of the down projection. `master_slots`: slot (owner[m,k], m) holds block kind k of row m; the other slots are unused. `left_slots`: symmetric and positive definite. `right_slots`: symmetric and positive definite. `left_roots`: symmetric and positive definite. `right_roots`: symmetric and positive definite. `grid_height`: each image is 16 patches along one side; the other sides of one device's images add up to 64. `grid_width`: as grid_height. `patch_rows`: each device's patches hold its images whole, one after another in the order of their numbers, each in raster order. `patch_cols`: as patch_rows. `segment`: never falls within a device's patches.
All inputs are finite; a program needn't handle non-finite values.
Results may differ from a plain program's by a relative error of at most 0.014.
Values may be sent and summed in bfloat16 or wider, within the bound.
A program may use at most 192 MiB of HBM per device.

v0:
```python
import math

import jax
import jax.numpy as jnp
from jax import lax
from jax.sharding import PartitionSpec as P

HEADS = 12
GRID_BASE = 16


NORM_EPSILON = 1e-06
GRAFT_EPSILON = 1e-06
STEP_EPSILON = 1e-08
RATE_MATRIX = 0.04
RATE_VECTOR = 0.02
MASKED_SCORE = -1e30


def layer_norm(values, gain_row, shift_row):
    centred = values - jnp.mean(values, axis=-1, keepdims=True)
    spread = jnp.mean(centred * centred, axis=-1, keepdims=True)
    return centred * lax.rsqrt(spread + NORM_EPSILON) * gain_row + shift_row


def exact_gelu(values):
    return jax.nn.gelu(values, approximate=False)


def rotate_pairs(flat_values, freq_row, rows_pos, cols_pos):
    tokens_here = flat_values.shape[0]
    values = flat_values.reshape(tokens_here, HEADS, -1)
    half_size = values.shape[-1] // 2
    middle = freq_row.shape[0] // 2
    freq_cols = freq_row[:middle].reshape(HEADS, half_size)
    freq_rows = freq_row[middle:].reshape(HEADS, half_size)
    angle_grid = (
        rows_pos[:, None, None] * freq_rows[None] + cols_pos[:, None, None] * freq_cols[None]
    )
    cosine = jnp.cos(angle_grid)
    sine_part = jnp.sin(angle_grid)
    first_half = values[..., :half_size]
    second = values[..., half_size:]
    turned = jnp.concatenate(
        [first_half * cosine - second * sine_part, second * cosine + first_half * sine_part],
        axis=-1,
    )
    return turned.reshape(tokens_here, -1)


def patch_positions(segment_ids, heights_in, widths_in, rows_in, cols_in):
    images_here = heights_in.shape[0]
    matches = segment_ids[:, None] == jnp.arange(images_here, dtype=jnp.int32)[None, :]
    heights = jnp.sum(jnp.where(matches, heights_in[None, :], 0), axis=1).astype(jnp.float32)
    widths = jnp.sum(jnp.where(matches, widths_in[None, :], 0), axis=1).astype(jnp.float32)
    rows_pos = rows_in.astype(jnp.float32) * GRID_BASE / heights
    cols_pos = cols_in.astype(jnp.float32) * GRID_BASE / widths
    return (rows_pos, cols_pos)


def heads_first(flat_values):
    return jnp.swapaxes(flat_values.reshape(flat_values.shape[0], HEADS, -1), 0, 1)


def tokens_first(stacked):
    return jnp.swapaxes(stacked, 0, 1).reshape(stacked.shape[1], -1)


def local(
    tokens,
    cotangent,
    vectors,
    vector_moments,
    decays,
    owner,
    master_slots,
    left_slots,
    right_slots,
    left_roots,
    right_roots,
    grid_height,
    grid_width,
    patch_rows,
    patch_cols,
    segment,
):
    dp_index = lax.axis_index("dp")
    mlp_index = lax.axis_index("mlp")
    groups_mlp = lax.axis_size("mlp")
    model_width = tokens.shape[1]
    rows_here = tokens.shape[0]
    owner_row = jnp.take(owner, mlp_index, axis=0)
    holds_block = owner_row == dp_index
    owned_blocks = jnp.where(holds_block[:, None, None], master_slots[0, 0][None], 0.0)
    blocks = lax.psum(owned_blocks, "dp")
    blocks_low = blocks.astype(jnp.bfloat16)
    up_rows = vectors[8 : 8 + groups_mlp]
    down_bias = vectors[8 + groups_mlp]
    freq_row = vectors[9 + groups_mlp]
    every_block = lax.all_gather(blocks_low[None], "mlp", axis=0, tiled=True)
    attention_weights = every_block[:, 0]
    up_weight = every_block[:, 1]
    down_weight = every_block[:, 2]
    up_bias = up_rows.reshape(-1)
    inputs = tokens.astype(jnp.float32)
    norm_one, norm_one_back = jax.vjp(layer_norm, inputs, vectors[0], vectors[1])
    norm_one_low = norm_one.astype(jnp.bfloat16)
    query_lin = (
        jnp.dot(norm_one_low, attention_weights[0], preferred_element_type=jnp.float32) + vectors[2]
    )
    key_lin = (
        jnp.dot(norm_one_low, attention_weights[1], preferred_element_type=jnp.float32) + vectors[3]
    )
    value_low = (
        jnp.dot(norm_one_low, attention_weights[2], preferred_element_type=jnp.float32) + vectors[4]
    ).astype(jnp.bfloat16)
    rows_pos, cols_pos = patch_positions(segment, grid_height, grid_width, patch_rows, patch_cols)

    def rotary_map(flat_values, freq_values):
        return rotate_pairs(flat_values, freq_values, rows_pos, cols_pos)

    query_rot, query_back = jax.vjp(rotary_map, query_lin, freq_row)
    key_rot, key_back = jax.vjp(rotary_map, key_lin, freq_row)
    query_heads = heads_first(query_rot.astype(jnp.bfloat16))
    key_heads = heads_first(key_rot.astype(jnp.bfloat16))
    value_heads = heads_first(value_low)
    same_image = segment[:, None] == segment[None, :]
    score_scale = 1.0 / math.sqrt(model_width // HEADS)

    def head_scores(query_head, key_head):
        scores = jnp.dot(query_head, key_head.T, preferred_element_type=jnp.float32) * score_scale
        return jnp.where(same_image, scores, MASKED_SCORE)

    def head_forward(pieces):
        query_head, key_head, value_head = pieces
        scores = head_scores(query_head, key_head)
        row_peak = jnp.max(scores, axis=1, keepdims=True)
        exponent = jnp.exp(scores - row_peak)
        row_total = jnp.sum(exponent, axis=1, keepdims=True)
        weights_low = (exponent / row_total).astype(jnp.bfloat16)
        attended = jnp.dot(weights_low, value_head, preferred_element_type=jnp.float32)
        return (attended, (row_peak + jnp.log(row_total))[:, 0])

    attended_heads, log_totals = lax.map(head_forward, (query_heads, key_heads, value_heads))
    attended_low = tokens_first(attended_heads).astype(jnp.bfloat16)
    branch_one = (
        jnp.dot(attended_low, attention_weights[3], preferred_element_type=jnp.float32) + vectors[5]
    )
    middle = inputs + branch_one
    norm_two, norm_two_back = jax.vjp(layer_norm, middle, vectors[6], vectors[7])
    norm_two_low = norm_two.astype(jnp.bfloat16)
    pre_act = (
        jnp.einsum(
            "td,mde->tme", norm_two_low, up_weight, preferred_element_type=jnp.float32
        ).reshape(rows_here, -1)
        + up_bias
    )
    activation, gelu_back = jax.vjp(exact_gelu, pre_act)
    activation_blocks = activation.astype(jnp.bfloat16).reshape(rows_here, groups_mlp, -1)
    branch_two = (
        jnp.einsum(
            "tme,med->td", activation_blocks, down_weight, preferred_element_type=jnp.float32
        )
        + down_bias
    )
    grad_act = jnp.einsum(
        "td,med->tme", cotangent, down_weight, preferred_element_type=jnp.float32
    ).reshape(rows_here, -1)
    grad_down = jnp.einsum(
        "tme,td->med", activation_blocks, cotangent, preferred_element_type=jnp.float32
    )
    grad_pre_blocks = gelu_back(grad_act)[0].astype(jnp.bfloat16).reshape(rows_here, groups_mlp, -1)
    grad_up = jnp.einsum(
        "td,tme->mde", norm_two_low, grad_pre_blocks, preferred_element_type=jnp.float32
    )
    up_grad_rows = jnp.sum(grad_pre_blocks, axis=0, dtype=jnp.float32)
    grad_norm_two = jnp.einsum(
        "tme,mde->td", grad_pre_blocks, up_weight, preferred_element_type=jnp.float32
    )
    output_low = (middle + branch_two).astype(jnp.bfloat16)
    grad_middle_norm, grad_gain_two, grad_shift_two = norm_two_back(grad_norm_two)
    grad_middle = cotangent.astype(jnp.float32) + grad_middle_norm
    grad_branch_low = grad_middle.astype(jnp.bfloat16)
    grad_out_bias = jnp.sum(grad_branch_low, axis=0, dtype=jnp.float32)
    grad_out_weight = jnp.dot(attended_low.T, grad_branch_low, preferred_element_type=jnp.float32)
    grad_attended_low = jnp.dot(
        grad_branch_low, attention_weights[3].T, preferred_element_type=jnp.float32
    ).astype(jnp.bfloat16)

    def head_backward(pieces):
        query_head, key_head, value_head, grad_head, log_total = pieces
        scores = head_scores(query_head, key_head)
        probs = jnp.exp(scores - log_total[:, None])
        grad_probs = jnp.dot(grad_head, value_head.T, preferred_element_type=jnp.float32)
        inner = jnp.sum(probs * grad_probs, axis=1, keepdims=True)
        grad_scores = (probs * (grad_probs - inner)).astype(jnp.bfloat16)
        grad_query = (
            jnp.dot(grad_scores, key_head, preferred_element_type=jnp.float32) * score_scale
        )
        grad_key = (
            jnp.dot(grad_scores.T, query_head, preferred_element_type=jnp.float32) * score_scale
        )
        grad_value = jnp.dot(
            probs.astype(jnp.bfloat16).T, grad_head, preferred_element_type=jnp.float32
        )
        return (grad_query, grad_key, grad_value)

    grad_queries, grad_keys, grad_values = lax.map(
        head_backward,
        (query_heads, key_heads, value_heads, heads_first(grad_attended_low), log_totals),
    )
    grad_query_lin, grad_freq_query = query_back(tokens_first(grad_queries))
    grad_key_lin, grad_freq_key = key_back(tokens_first(grad_keys))
    grad_query_low = grad_query_lin.astype(jnp.bfloat16)
    grad_key_low = grad_key_lin.astype(jnp.bfloat16)
    grad_value_low = tokens_first(grad_values).astype(jnp.bfloat16)
    grad_query_weight = jnp.dot(norm_one_low.T, grad_query_low, preferred_element_type=jnp.float32)
    grad_key_weight = jnp.dot(norm_one_low.T, grad_key_low, preferred_element_type=jnp.float32)
    grad_value_weight = jnp.dot(norm_one_low.T, grad_value_low, preferred_element_type=jnp.float32)
    grad_norm_one = jnp.dot(
        grad_query_low, attention_weights[0].T, preferred_element_type=jnp.float32
    )
    grad_norm_one = grad_norm_one + jnp.dot(
        grad_key_low, attention_weights[1].T, preferred_element_type=jnp.float32
    )
    grad_norm_one = grad_norm_one + jnp.dot(
        grad_value_low, attention_weights[2].T, preferred_element_type=jnp.float32
    )
    grad_input_norm, grad_gain_one, grad_shift_one = norm_one_back(grad_norm_one)
    input_grad = grad_middle + grad_input_norm
    head_rows = jnp.stack(
        [
            grad_gain_one,
            grad_shift_one,
            jnp.sum(grad_query_low, axis=0, dtype=jnp.float32),
            jnp.sum(grad_key_low, axis=0, dtype=jnp.float32),
            jnp.sum(grad_value_low, axis=0, dtype=jnp.float32),
            grad_out_bias,
            grad_gain_two,
            grad_shift_two,
        ]
    )
    tail_rows = jnp.stack(
        [jnp.sum(cotangent, axis=0, dtype=jnp.float32), grad_freq_query + grad_freq_key]
    )
    local_vectors = jnp.concatenate([head_rows, up_grad_rows, tail_rows], axis=0)
    vector_sum = lax.psum(local_vectors, ("dp", "mlp"))
    attention_grads = jnp.stack(
        [grad_query_weight, grad_key_weight, grad_value_weight, grad_out_weight]
    )
    attention_share, up_share, down_share = (
        lax.psum_scatter(
            attention_grads.astype(jnp.bfloat16), "mlp", scatter_dimension=0, tiled=True
        ).astype(jnp.float32),
        lax.psum_scatter(
            grad_up.astype(jnp.bfloat16), "mlp", scatter_dimension=0, tiled=True
        ).astype(jnp.float32),
        lax.psum_scatter(
            grad_down.astype(jnp.bfloat16), "mlp", scatter_dimension=0, tiled=True
        ).astype(jnp.float32),
    )
    grad_stack = jnp.concatenate([attention_share, up_share, down_share], axis=0)
    reduced = lax.psum(grad_stack, "dp")
    block_kind = jnp.sum(jnp.where(holds_block, jnp.arange(3, dtype=jnp.int32), 0))
    owns_block = jnp.any(holds_block)
    gradient = jnp.take(reduced, block_kind, axis=0)
    decay_matrix = decays[0]
    left_old = left_slots[0, 0]
    right_old = right_slots[0, 0]
    master_old = master_slots[0, 0]
    left_next = decay_matrix * left_old + (1.0 - decay_matrix) * jnp.dot(
        gradient, gradient.T, precision=lax.Precision.HIGHEST
    )
    right_next = decay_matrix * right_old + (1.0 - decay_matrix) * jnp.dot(
        gradient.T, gradient, precision=lax.Precision.HIGHEST
    )
    direction = jnp.dot(
        jnp.dot(left_roots[0, 0], gradient, precision=lax.Precision.HIGHEST),
        right_roots[0, 0],
        precision=lax.Precision.HIGHEST,
    )
    normed_step = direction * lax.rsqrt(jnp.mean(direction * direction) + GRAFT_EPSILON)
    master_next = master_old - RATE_MATRIX * normed_step
    slot_grad = jnp.where(owns_block, gradient, 0.0)[None, None]
    left_out = jnp.where(owns_block, left_next, left_old)[None, None]
    right_out = jnp.where(owns_block, right_next, right_old)[None, None]
    master_out = jnp.where(owns_block, master_next, master_old)[None, None]
    share_width = model_width // groups_mlp

    def own_columns(table):
        return lax.dynamic_slice_in_dim(table, mlp_index * share_width, share_width, 1)

    grad_share = own_columns(vector_sum)
    moment_old = own_columns(vector_moments)
    vector_old = own_columns(vectors)
    decay_vector = decays[1]
    moment_next = decay_vector * moment_old + (1.0 - decay_vector) * grad_share * grad_share
    vector_next = vector_old - RATE_VECTOR * grad_share / (jnp.sqrt(moment_next) + STEP_EPSILON)
    return (
        output_low,
        input_grad,
        slot_grad,
        left_out,
        right_out,
        master_out,
        grad_share,
        moment_next,
        vector_next,
    )


def solution(mesh):
    placed = (
        P(("dp", "mlp"), None),
        P(("dp", "mlp"), None),
        P(),
        P(),
        P(),
        P(),
        P("dp", "mlp", None, None),
        P("dp", "mlp", None, None),
        P("dp", "mlp", None, None),
        P("dp", "mlp", None, None),
        P("dp", "mlp", None, None),
        P(("dp", "mlp")),
        P(("dp", "mlp")),
        P(("dp", "mlp")),
        P(("dp", "mlp")),
        P(("dp", "mlp")),
    )
    return jax.shard_map(
        local,
        mesh=mesh,
        in_specs=placed,
        out_specs=(
            P(("dp", "mlp"), None),
            P(("dp", "mlp"), None),
            P("dp", "mlp", None, None),
            P("dp", "mlp", None, None),
            P("dp", "mlp", None, None),
            P("dp", "mlp", None, None),
            P(None, "mlp"),
            P(None, "mlp"),
            P(None, "mlp"),
        ),
        check_vma=False,
    )
```

profile of v0, /device:TPU:0, one launch (start us, length us, event | category | flops | bytes accessed | tf_op | source)
XLA Modules:
  0.0 1202.3 jit_solution(14143546167382789815)
XLA Ops:
  8.8 5.2 broadcast_select_fusion
  14.0 278.3 %all-reduce.12 = bf16[3,768,768]{2,1,0:T(8,128)(2,1)} all-reduce(f32[3,768,768]{2,1,0:T(8,128)} %broadcast_select_fusion), channel_id=1, replica_groups=mesh['dp'=8,'mlp'=4] {'dp'}, use_global_device_ids=true, to_apply=%region_2.3 | all-reduce | flops 1769472 | bytes 10616832 | tf_op jit(solution)/shard_map/psum | solution.py:95
  303.2 78.7 %all-gather.3.cloned.1.call-done = bf16[12,768,768]{2,1,0:T(8,128)(2,1)} async-done(((bf16[3,768,768]{2,1,0:T(8,128)(2,1)}), bf16[12,768,768]{2,1,0:T(8,128)(2,1)}) %all-gather.3.cloned.1.call-update) | async-done | bytes 14155792 | tf_op jit(solution)/shard_map/all_gather | solution.py:100
  381.8 4.9 slice_bitcast_fusion.3
  389.7 3.8 convolution_add_fusion.1
  393.6 7.7 subtract_convert_fusion
  402.5 4.1 copy.102
  409.1 4.1 copy.103
  413.2 4.5 add_convert_fusion.4
  417.7 4.1 copy.101
  421.8 85.7 %while.32 = (s32[]{:T(128)}, bf16[12,1024,64]{1,2,0:T(8,128)(2,1)}, f32[12,1024]{1,0:T(8,128)}, bf16[12,1024,64]{2,1,0:T(8,128)(2,1)}, bf16[12,1024,64]{2,1,0:T(...) while((s32[]{:T(128)}, bf16[12,1024,64]{1,2,0:T(8,128)(2,1)}, ...), condition=%wide.region_8.9_spmd.clone.clone, body=%wide.region_5.8_spmd.clone.sunk.clone | while | flops 284163072 | bytes 13695065 | solution.py:144
  431.7 3.0 fusion.195
  453.2 3.0 fusion.195
  467.4 3.0 fusion.195
  481.7 3.0 fusion.195
  496.0 3.0 fusion.195
  507.5 10.2 fusion.64
  517.7 12.7 %copy.133 = f32[1024,3072]{1,0:T(8,128)} copy(f32[1024,3072]{0,1:T(8,128)} %bitcast.277) | data formatting | bytes 25165824 | tf_op jit(solution)/shard_map/reshape | solution.py:168
  530.3 6.6 copy.105
  537.0 4.0 fusion.140
  544.0 40.9 %convert_reduce_fusion = (f32[3072]{0:T(1024)}, bf16[1024,3072]{1,0:T(8,128)(2,1)}, f32[1024,3072]{1,0:T(8,128)}, f32[1024,3072]{1,0:T(8,128)}) fusion(f32[1024,3072]{1,0:T(8,128)S(1)} %copy-done.14, f32[3072]{0:T(1024)S(1)} %add.236, bf16[3072,768]{1,0:T(8,128)(2,1)} %bitcast.289, f32[1024,768]{0,1:T(8,128)S(1)} %get-tuple-element.370, ...), kind=kOutput, calls=%fused_computation.58 | convolution fusion | flops 5071696896 | bytes 51943424 | tf_op jit(solution)/shard_map/td,mde->tme/dot_general | solution.py:153
  584.9 12.8 %multiply_convert_fusion.1 = bf16[1024,3072]{1,0:T(8,128)(2,1)} fusion(f32[1024,3072]{1,0:T(8,128)} %get-tuple-element.336, f32[1024,3072]{1,0:T(8,128)} %get-tuple-element.371, f32[3072]{0:T(1024)S(1)} %add.236), kind=kLoop, calls=%fused_computation.60 | loop fusion | flops 12582912 | bytes 31469568 | tf_op jit(solution)/shard_map/convert_element_type | solution.py:159
  597.8 8.6 copy.137
  606.4 9.0 convolution_convert_fusion
  618.0 8.8 copy.138
  626.8 9.9 fusion.141
  636.7 3.5 copy.112
  640.2 3.9 multiply_reduce_fusion.1
  647.4 4.4 convolution_convert_fusion.1
  651.8 4.1 copy.113
  655.9 10.4 convert_bitcast_fusion
  667.0 159.3 %while.33 = (s32[]{:T(128)}, f32[12,1024,64]{1,2,0:T(8,128)}, f32[12,1024,64]{1,2,0:T(8,128)}, bf16[12,1024,64]{1,2,0:T(8,128)(2,1)}, bf16[12,1024,64]{2,1,0:T(8...) while((s32[]{:T(128)}, f32[12,1024,64]{1,2,0:T(8,128)}, ...), condition=%wide.region_15.16_spmd.clone.clone, body=%wide.region_13.15_spmd.clone.sunk.clone | while | flops 681704448 | bytes 34112624 | solution.py:208
  826.3 12.0 multiply_add_fusion.1
  840.7 7.8 multiply_add_fusion
  860.6 48.4 %reduce-scatter.4.cloned.1.call-done = bf16[1,768,768]{2,1,0:T(8,128)(2,1)} async-done(((bf16[4,768,768]{2,1,0:T(8,128)(2,1)}), bf16[1,768,768]{2,1,0:T(8,128)(2,1)}) %reduce-scatter.4.cloned.1.call-update) | async-done | bytes 1179664 | tf_op jit(solution)/shard_map/reduce_scatter | solution.py:252
  909.0 5.3 maximum_convert_fusion
  919.4 10.5 fusion.75
  932.5 3.3 fusion.114
  938.6 3.1 fusion.133
  944.2 3.3 convert_reduce_fusion.2
  947.5 3.6 copy.125
  955.9 45.1 %psum.23 = f32[14,768]{1,0:T(8,128)S(1)} all-reduce(f32[14,768]{1,0:T(8,128)S(1)} %concatenate.21), channel_id=1, replica_groups=mesh['dp'=8,'mlp'=4] {'dp','mlp'}, use_global_device_ids=true, to_apply=%region_39.40 | all-reduce | flops 10752 | bytes 86016 | tf_op jit(solution)/shard_map/psum | solution.py:247
  1003.1 143.9 %all-reduce.11.cloned.1.call-done = f32[3,768,768]{2,1,0:T(8,128)} async-done(((f32[3,768,768]{2,1,0:T(8,128)}), f32[3,768,768]{2,1,0:T(8,128)}) %all-reduce.11.cloned.1.call-update) | async-done | bytes 7077904 | tf_op jit(solution)/shard_map/psum | solution.py:263
  1147.1 13.6 %fusion.79 = f32[768,768]{1,0:T(8,128)S(1)} fusion(f32[1,1,768,768]{3,2,1,0:T(8,128)} %param.29, f32[3,768,768]{2,1,0:T(8,128)} %all-reduce.11.cloned.1.call-done, s32[]{:T(128)S(6)} %select_n.95, pred[]{:T(512)S(6)} %and.13), kind=kOutput, calls=%fused_computation.124 | convolution fusion | flops 5436407808 | bytes 7077893 | tf_op jit(solution)/shard_map/dot_general | solution.py:278
  1160.7 8.7 multiply_reduce_fusion.4
  1170.1 5.0 fusion.76
  1177.5 8.9 fusion.84
  1186.4 9.2 fusion.82
  (331 shorter events, 291.6 us)
Async XLA Ops:
  7.2 1153.5 %copy-start = (f32[1,1,768,768]{3,2,1,0:T(8,128)S(1)}, f32[1,1,768,768]{3,2,1,0:T(8,128)}, u32[]{:S(2)}) copy-start(f32[1,1,768,768]{3,2,1,0:T(8,128)} %param.30) | copy-start | bytes 7077892
  7.2 374.6 %all-gather.3.cloned.1.call-start = ((), (), s32[]{:S(2)}) async-start(), calls=%async_computation.7 | async-start | bytes 17694720 | tf_op jit(solution)/shard_map/all_gather | solution.py:100
  292.3 568.3 %reduce-scatter.8.cloned.1.call-start = ((), (), s32[]{:S(2)}) async-start(), calls=%async_computation.5 | async-start | bytes 5898240 | tf_op jit(solution)/shard_map/reduce_scatter | solution.py:258
  293.7 3.8 copy-start.38
  293.7 4.0 slice-start
  293.7 4.0 copy-start.20
  293.7 4.0 copy-start.53
  293.7 4.0 copy-start.54
  294.8 8.3 copy-start.50
  294.8 8.3 copy-start.51
  297.5 96.0 %copy-start.28 = (f32[12,32]{1,0:T(8,128)}, f32[12,32]{1,0:T(8,128)S(1)}, u32[]{:S(2)}) copy-start(f32[12,32]{1,0:T(8,128)S(1)} %mul.390) | copy-start | bytes 4612
  297.6 95.9 %copy-start.30 = (f32[12,32]{1,0:T(8,128)}, f32[12,32]{1,0:T(8,128)S(1)}, u32[]{:S(2)}) copy-start(f32[12,32]{1,0:T(8,128)S(1)} %mul.385) | copy-start | bytes 4612
  298.4 114.8 %copy-start.40 = (f32[768]{0:T(1024)}, f32[768]{0:T(1024)S(1)}, u32[]{:S(2)}) copy-start(f32[768]{0:T(1024)S(1)} %get-tuple-element.290) | copy-start | bytes 9220
  298.4 114.8 %copy-start.48 = (f32[768]{0:T(1024)}, f32[768]{0:T(1024)S(1)}, u32[]{:S(2)}) copy-start(f32[768]{0:T(1024)S(1)} %get-tuple-element.289) | copy-start | bytes 9220
  300.4 112.8 %copy-start.32 = (f32[1024]{0:T(1024)}, f32[1024]{0:T(1024)S(1)}, u32[]{:S(2)}) copy-start(f32[1024]{0:T(1024)S(1)} %broadcast_multiply_fusion.1) | copy-start | bytes 12292
  302.5 110.7 %copy-start.42 = (f32[1024]{0:T(1024)}, f32[1024]{0:T(1024)S(1)}, u32[]{:S(2)}) copy-start(f32[1024]{0:T(1024)S(1)} %fusion.118) | copy-start | bytes 12292
  303.1 90.4 %copy-start.34 = (f32[1024]{0:T(1024)}, f32[1024]{0:T(1024)S(1)}, u32[]{:S(2)}) copy-start(f32[1024]{0:T(1024)S(1)} %get-tuple-element.377) | copy-start | bytes 12292
  303.1 90.4 %copy-start.36 = (f32[1024]{0:T(1024)}, f32[1024]{0:T(1024)S(1)}, u32[]{:S(2)}) copy-start(f32[1024]{0:T(1024)S(1)} %get-tuple-element.378) | copy-start | bytes 12292
  381.8 4.9 copy-start.1
  389.7 3.9 copy-start.15
  393.5 7.8 copy-start.17
  537.0 7.0 copy-start.14
  541.0 43.9 %copy-start.4 = (f32[1024,768]{0,1:T(8,128)}, f32[1024,768]{0,1:T(8,128)S(1)}, u32[]{:S(2)}) copy-start(f32[1024,768]{0,1:T(8,128)S(1)} %get-tuple-element.370) | copy-start | bytes 9437188
  615.4 245.2 %reduce-scatter.6.cloned.1.call-start = ((), (), s32[]{:S(2)}) async-start(), calls=%async_computation.4 | async-start | bytes 5898240 | tf_op jit(solution)/shard_map/reduce_scatter | solution.py:255
  640.2 3.9 copy-start.5
  640.2 4.7 copy-start.8
  647.4 4.4 copy-start.23
  666.3 242.7 %reduce-scatter.4.cloned.1.call-start = ((), (), s32[]{:S(2)}) async-start(), calls=%async_computation.3 | async-start | bytes 5898240 | tf_op jit(solution)/shard_map/reduce_scatter | solution.py:252
  667.0 159.3 %copy-start.29 = (f32[12,32]{1,0:T(8,128)S(1)}, f32[12,32]{1,0:T(8,128)}, u32[]{:S(2)}) copy-start(f32[12,32]{1,0:T(8,128)} %copy-done.28) | copy-start | bytes 4612
  667.0 159.3 %copy-start.31 = (f32[12,32]{1,0:T(8,128)S(1)}, f32[12,32]{1,0:T(8,128)}, u32[]{:S(2)}) copy-start(f32[12,32]{1,0:T(8,128)} %copy-done.30) | copy-start | bytes 4612
  667.0 159.3 %copy-start.35 = (f32[1024]{0:T(1024)S(1)}, f32[1024]{0:T(1024)}, u32[]{:S(2)}) copy-start(f32[1024]{0:T(1024)} %copy-done.34) | copy-start | bytes 12292
  667.0 159.3 %copy-start.37 = (f32[1024]{0:T(1024)S(1)}, f32[1024]{0:T(1024)}, u32[]{:S(2)}) copy-start(f32[1024]{0:T(1024)} %copy-done.36) | copy-start | bytes 12292
  826.3 12.3 %copy-start.18 = (f32[12,1024,64]{1,2,0:T(8,128)S(1)}, f32[12,1024,64]{1,2,0:T(8,128)}, u32[]{:S(2)}) copy-start(f32[12,1024,64]{1,2,0:T(8,128)} %get-tuple-element.104) | copy-start | bytes 9437188
  838.3 2.5 copy-start.16
  838.5 17.7 %copy-start.25 = (bf16[1024,12,64]{0,2,1:T(8,128)(2,1)}, bf16[1024,12,64]{0,2,1:T(8,128)(2,1)S(1)}, u32[]{:S(2)}) copy-start(bf16[1024,12,64]{0,2,1:T(8,128)(2,1)S(1)} %get-tuple-element.342) | copy-start | bytes 4718596
  850.5 4.1 copy-start.26
  850.5 2.4 copy-start.10
  850.5 2.4 copy-start.33
  860.3 286.7 %all-reduce.11.cloned.1.call-start = ((), (), s32[]{:S(2)}) async-start(), calls=%async_computation.6 | async-start | bytes 14155776 | tf_op jit(solution)/shard_map/psum | solution.py:263
  914.4 5.1 copy-start.47
  932.5 3.3 copy-start.27
  935.7 2.8 copy-start.3
  935.8 2.8 copy-start.11
  938.6 3.2 copy-start.45
  947.5 5.5 copy-start.46
  951.0 50.0 %copy-start.39 = (f32[14,768]{1,0:T(8,128)S(1)}, f32[14,768]{1,0:T(8,128)}, u32[]{:S(2)}) copy-start(f32[14,768]{1,0:T(8,128)} %param.22) | copy-start | bytes 129028
  1170.1 5.0 copy-start.19
  1177.5 8.9 copy-start.56
  (15 other events, 26.7 us)
Sparse Core Ops, SparseCore 0:
  292.4 89.3 all-gather.2
  615.5 47.9 reduce-scatter.7
  666.4 48.3 reduce-scatter.5
  860.4 48.5 reduce-scatter.3
  914.5 232.5 all-reduce.10
where the time goes:
time: 1220 us; the launch traced here: 1200 us
  matrix products  359 us (29%)
  blocking collectives  323 us (26%)
  waiting for transfers between devices  271 us (22%)
  local copies, waits for them, and re-layouts  115 us (9%)
  other arithmetic  115 us (9%)
  between operations  18.4 us (2%)
    psum x1, blocking collectives, local(): blocks = lax.psum(owned_blocks, 'dp')  278 us
    psum x1, waiting for transfers between devices, local(): reduced = lax.psum(grad_stack, 'dp')  144 us
    all_gather x1, waiting for transfers between devices, local(): every_block = lax.all_gather(blocks_low[None], 'mlp', axis=0, tiled=True)  78.7 us
    dot_general x24, matrix products, head_scores(): jnp.dot(query_head, key_head.T, preferred_element_type=jnp.float32)  52.2 us
    reduce_scatter x1, waiting for transfers between devices, local(): lax.psum_scatter(attention_grads.astype(jnp.bfloat16), 'mlp', scatter_dim...  48.4 us
    psum x1, blocking collectives, local(): vector_sum = lax.psum(local_vectors, ('dp', 'mlp'))  45.1 us
    dot_general x1, matrix products, local(): jnp.einsum('td,mde->tme', norm_two_low, up_weight, preferred_element_type...  40.9 us
    dot_general x12, matrix products, head_forward(): jnp.dot(weights_low, value_head, preferred_element_type=jnp.float32)  35.5 us
  transfers between devices with their start and end apart: 5, of which 3 were waited for; matrix products, arithmetic and copies ran while one was open for 24% of the time, Pallas kernels for 0%

commit v1 on v0

v1 whole, which is shorter than its diff:
```python
import functools
import math

import jax
import jax.numpy as jnp
from jax import lax
from jax.experimental import pallas as pl
from jax.experimental.pallas import tpu as pltpu
from jax.sharding import PartitionSpec as P

HEADS = 12
GRID_BASE = 16
NORM_EPSILON = 1e-06
GRAFT_EPSILON = 1e-06
STEP_EPSILON = 1e-08
RATE_MATRIX = 0.04
RATE_VECTOR = 0.02
MASK_SHIFT = -(2.0**100)
BLOCK = 128
TILE = 256
F32 = jnp.float32
BF = jnp.bfloat16
VMEM_LIMIT = 60 * 1024 * 1024


def dot(left, right, left_dim, right_dim, precision=None):
    return lax.dot_general(
        left,
        right,
        (((left_dim,), (right_dim,)), ((), ())),
        preferred_element_type=F32,
        precision=precision,
    )


def normed(values):
    mean = jnp.mean(values, axis=-1, keepdims=True)
    centred = values - mean
    spread = jnp.mean(centred * centred, axis=-1, keepdims=True)
    scale = lax.rsqrt(spread + NORM_EPSILON)
    return centred * scale, scale


def norm_back(grad, unit, scale, gain):
    scaled = grad * gain
    first = jnp.mean(scaled, axis=-1, keepdims=True)
    second = jnp.mean(scaled * unit, axis=-1, keepdims=True)
    return scale * (scaled - first - unit * second)


def fold_rows(values):
    return jnp.sum(values.reshape(values.shape[0] // 8, 8, values.shape[1]), axis=0)


def project_kernel(
    x_ref, pos_ref, vec_ref, turned_ref, weight_ref,
    n1_ref, q_ref, k_ref, v_ref, cos_ref, sin_ref, qmark_ref, kmark_ref,
):
    unit, _ = normed(x_ref[...].astype(F32))
    n1 = (unit * vec_ref[0:1, :] + vec_ref[1:2, :]).astype(BF)
    n1t = n1.T
    n1_ref[...] = n1t
    px = pos_ref[0:1, :]
    py = pos_ref[1:2, :]
    half = cos_ref.shape[0]
    last = turned_ref.shape[1] - 1
    angle = turned_ref[half:, last:] * py + turned_ref[:half, last:] * px
    cosine = jnp.cos(angle)
    sine = jnp.sin(angle)
    cos_ref[...] = cosine
    sin_ref[...] = sine
    seg = pos_ref[2:3, :].astype(jnp.int32)
    row = lax.broadcasted_iota(jnp.int32, qmark_ref.shape, 0)
    qmark_ref[...] = jnp.where(row == seg, 1.0, 0.0).astype(BF)
    kmark_ref[...] = jnp.where(row == seg, 0.0, MASK_SHIFT).astype(BF)
    part = half // HEADS
    for index, (out, scale) in enumerate(((q_ref, 0.125), (k_ref, 1.0))):
        flat = dot(weight_ref[index], n1t, 0, 0) + turned_ref[:, 2 + index : 3 + index]
        for head in range(HEADS):
            low, mid = 2 * part * head, 2 * part * head + part
            a = flat[low:mid]
            b = flat[mid : mid + part]
            c = cosine[part * head : part * (head + 1)]
            s = sine[part * head : part * (head + 1)]
            out[low:mid, :] = (a * c - b * s).astype(BF) * jnp.asarray(scale, BF)
            out[mid : mid + part, :] = (b * c + a * s).astype(BF) * jnp.asarray(scale, BF)
    v_ref[...] = (dot(weight_ref[2], n1t, 0, 0) + turned_ref[:, 4:5]).astype(BF)


def project(x, pos, vec, turned, weights):
    rows, width = x.shape
    half = width // 2
    whole = lambda a: pl.BlockSpec(a.shape, lambda i: (0,) * a.ndim)
    col = lambda n: pl.BlockSpec((n, TILE), lambda i: (0, i))
    out = lambda n, d: jax.ShapeDtypeStruct((n, rows), d)
    return pl.pallas_call(
        project_kernel,
        grid=(rows // TILE,),
        in_specs=[
            pl.BlockSpec((TILE, width), lambda i: (i, 0)),
            col(8),
            whole(vec),
            whole(turned),
            whole(weights),
        ],
        out_specs=[col(width)] * 4 + [col(half)] * 2 + [col(16)] * 2,
        out_shape=[out(width, BF)] * 4 + [out(half, F32)] * 2 + [out(16, BF)] * 2,
        compiler_params=pltpu.CompilerParams(vmem_limit_bytes=VMEM_LIMIT),
        name="project",
    )(x, pos, vec, turned, weights)


def key_window(height_ref, width_ref, block):
    first = block * BLOCK
    last = first + BLOCK - 1
    start = jnp.int32(0)
    low = jnp.int32(0)
    high = jnp.int32(0)
    for image in range(height_ref.shape[0]):
        end = start + height_ref[image] * width_ref[image]
        low = jnp.where((start <= first) & (first < end), start, low)
        high = jnp.where((start <= last) & (last < end), end, high)
        start = end
    base = low // BLOCK
    return base, (high + BLOCK - 1) // BLOCK - base


def attend_kernel(height_ref, width_ref, q_ref, k_ref, v_ref, qmark_ref, kmark_ref, o_ref, log_ref):
    tokens = q_ref.shape[1]
    blocks = tokens // BLOCK
    size = q_ref.shape[0] // HEADS
    group = 4

    def one(block, part, base, count):
        here = pl.ds(pl.multiple_of(block * BLOCK, BLOCK), BLOCK)
        keys = pl.ds(pl.multiple_of(base * BLOCK, BLOCK), BLOCK * count)
        qmark = qmark_ref[:, here]
        kmark = kmark_ref[:, keys]
        for j in range(group):
            head = part * group + j
            rows = pl.ds(pl.multiple_of(head * size, size), size)
            q = jnp.concatenate([q_ref[rows, here], qmark], axis=0)
            k = jnp.concatenate([k_ref[rows, keys], kmark], axis=0)
            scores = dot(k, q, 0, 0)
            peak = jnp.max(scores, axis=0, keepdims=True)
            powers = jnp.exp(scores - peak)
            total = jnp.sum(powers, axis=0, keepdims=True)
            mixed = dot(v_ref[rows, keys], powers.astype(BF), 1, 0)
            o_ref[rows, here] = (mixed * (1.0 / total)).astype(BF)
            log_ref[pl.ds(pl.multiple_of(head * 8, 8), 8), here] = jnp.broadcast_to(
                peak + jnp.log(total), (8, BLOCK)
            )

    def step(block, carry):
        base, count = key_window(height_ref, width_ref, block)
        for n in range(1, blocks + 1):

            @pl.when(count == n)
            def _():
                def inner(part, c):
                    one(block, part, base, n)
                    return c

                lax.fori_loop(0, HEADS // group, inner, 0)

        return carry

    lax.fori_loop(0, blocks, step, 0)


def attend(heights, widths, q, k, v, qmark, kmark):
    smem = pl.BlockSpec(memory_space=pltpu.SMEM)
    vmem = pl.BlockSpec(memory_space=pltpu.VMEM)
    return pl.pallas_call(
        attend_kernel,
        in_specs=[smem, smem] + [vmem] * 5,
        out_specs=[vmem, vmem],
        out_shape=[
            jax.ShapeDtypeStruct(q.shape, BF),
            jax.ShapeDtypeStruct((8 * HEADS, q.shape[1]), F32),
        ],
        compiler_params=pltpu.CompilerParams(vmem_limit_bytes=VMEM_LIMIT),
        name="attend",
    )(heights, widths, q, k, v, qmark, kmark)


def attend_back_kernel(
    height_ref, width_ref, q_ref, k_ref, v_ref, qmark_ref, kmark_ref, log_ref, do_ref,
    pos_ref, cos_ref, sin_ref,
    dq_ref, dk_ref, dv_ref, freq_ref, bias_ref,
    gq_ref, gk_ref, gv_ref, turn_ref,
):
    tokens = q_ref.shape[1]
    blocks = tokens // BLOCK
    size = q_ref.shape[0] // HEADS
    half = size // 2
    group = 2
    gk_ref[...] = jnp.zeros_like(gk_ref)
    gv_ref[...] = jnp.zeros_like(gv_ref)

    def one(block, part, base, count):
        here = pl.ds(pl.multiple_of(block * BLOCK, BLOCK), BLOCK)
        keys = pl.ds(pl.multiple_of(base * BLOCK, BLOCK), BLOCK * count)
        qmark = qmark_ref[:, here]
        kmark = kmark_ref[:, keys]
        for j in range(group):
            head = part * group + j
            rows = pl.ds(pl.multiple_of(head * size, size), size)
            q = q_ref[rows, here]
            k = k_ref[rows, keys]
            do = do_ref[rows, here]
            scores = dot(
                jnp.concatenate([k, kmark], axis=0), jnp.concatenate([q, qmark], axis=0), 0, 0
            )
            log_row = log_ref[pl.ds(pl.multiple_of(head * 8, 8), 8), here][0:1]
            probs = jnp.exp(scores - log_row)
            dp = dot(v_ref[rows, keys], do, 0, 0)
            inner = jnp.sum(probs * dp, axis=0, keepdims=True)
            ds = (probs * (dp - inner)).astype(BF)
            gq_ref[rows, here] = dot(k, ds, 1, 0) * 0.125
            gk_ref[rows, keys] += dot(q, ds, 1, 1)
            gv_ref[rows, keys] += dot(do, probs.astype(BF), 1, 1)

    def step(block, carry):
        base, count = key_window(height_ref, width_ref, block)
        for n in range(1, blocks + 1):

            @pl.when(count == n)
            def _():
                def inner(part, c):
                    one(block, part, base, n)
                    return c

                lax.fori_loop(0, HEADS // group, inner, 0)

        return carry

    lax.fori_loop(0, blocks, step, 0)

    def unturn(head, carry):
        low = pl.ds(pl.multiple_of(head * size, size), half)
        high = pl.ds(pl.multiple_of(head * size + half, half), half)
        table = pl.ds(pl.multiple_of(head * half, half), half)
        c = cos_ref[table, :]
        s = sin_ref[table, :]
        turn = None
        for grad_ref, rot_ref, scale, out_ref in (
            (gq_ref, q_ref, 8.0, dq_ref),
            (gk_ref, k_ref, 1.0, dk_ref),
        ):
            ga = grad_ref[low, :]
            gb = grad_ref[high, :]
            out_ref[low, :] = (ga * c + gb * s).astype(BF)
            out_ref[high, :] = (gb * c - ga * s).astype(BF)
            ra = rot_ref[low, :].astype(F32) * scale
            rb = rot_ref[high, :].astype(F32) * scale
            piece = gb * ra - ga * rb
            turn = piece if turn is None else turn + piece
        turn_ref[table, :] = turn
        both = pl.ds(pl.multiple_of(head * size, size), size)
        dv_ref[both, :] = gv_ref[both, :].astype(BF)
        return carry

    lax.fori_loop(0, HEADS, unturn, 0)
    freq_ref[...] = dot(pos_ref[...], turn_ref[...], 1, 1, lax.Precision.HIGHEST)
    ones = jnp.ones((8, tokens), BF)
    for index, ref in enumerate((dq_ref, dk_ref, dv_ref)):
        bias_ref[8 * index : 8 * index + 8, :] = dot(ones, ref[...], 1, 1)


def attend_back(heights, widths, q, k, v, qmark, kmark, log_totals, do, pos, cosine, sine):
    smem = pl.BlockSpec(memory_space=pltpu.SMEM)
    vmem = pl.BlockSpec(memory_space=pltpu.VMEM)
    width, tokens = q.shape
    return pl.pallas_call(
        attend_back_kernel,
        in_specs=[smem, smem] + [vmem] * 10,
        out_specs=[vmem] * 5,
        out_shape=[jax.ShapeDtypeStruct(q.shape, BF)] * 3
        + [
            jax.ShapeDtypeStruct((8, width // 2), F32),
            jax.ShapeDtypeStruct((24, width), F32),
        ],
        scratch_shapes=[pltpu.VMEM(q.shape, F32)] * 3 + [pltpu.VMEM((width // 2, tokens), F32)],
        compiler_params=pltpu.CompilerParams(vmem_limit_bytes=VMEM_LIMIT),
        name="attend_back",
    )(heights, widths, q, k, v, qmark, kmark, log_totals, do, pos, cosine, sine)


def middle_kernel(
    x_ref, g_ref, o_ref, vec_ref, wo_ref, up_ref, down_ref,
    y_ref, dh_ref, do_ref, dwo_ref, dup_ref, ddown_ref, rows_ref, dc_ref,
    h_ref, n2_ref, n2t_ref, acc_ref, dn_ref, a_ref, dz_ref, dr_ref,
):
    groups = vec_ref.shape[0] - 10
    step = pl.program_id(0)
    tokens, width = x_ref.shape
    tiles = tokens // TILE

    def tile(i):
        return pl.ds(pl.multiple_of(i * TILE, TILE), TILE)

    @pl.when(step == 0)
    def _():
        def first(i, c):
            t = tile(i)
            branch = dot(o_ref[:, t], wo_ref[...], 0, 0) + vec_ref[5:6, :]
            h = x_ref[t, :].astype(F32) + branch
            h_ref[t, :] = h
            unit, _ = normed(h)
            n2 = (unit * vec_ref[6:7, :] + vec_ref[7:8, :]).astype(BF)
            n2_ref[t, :] = n2
            n2t_ref[:, t] = n2.T
            acc_ref[t, :] = h + vec_ref[8 + groups : 9 + groups, :]
            dn_ref[t, :] = jnp.zeros((TILE, width), F32)
            return c

        lax.fori_loop(0, tiles, first, 0)

    up_bias = vec_ref[pl.ds(8 + step, 1), :]

    def second(i, c):
        t = tile(i)
        z = dot(n2_ref[t, :], up_ref[0], 1, 0) + up_bias
        cdf = 0.5 * (1.0 + lax.erf(z * math.sqrt(0.5)))
        a = (z * cdf).astype(BF)
        a_ref[t, :] = a
        acc_ref[t, :] += dot(a, down_ref[0], 1, 0)
        da = dot(g_ref[t, :], down_ref[0], 1, 1)
        slope = cdf + z * (jnp.exp(-0.5 * z * z) * (1.0 / math.sqrt(2.0 * math.pi)))
        dz = (da * slope).astype(BF)
        dz_ref[t, :] = dz
        dn_ref[t, :] += dot(dz, up_ref[0], 1, 1)
        return c

    lax.fori_loop(0, tiles, second, 0)
    dc_ref[0] = dot(jnp.ones((8, tokens), BF), dz_ref[...], 1, 0)
    dup_ref[0] = dot(n2t_ref[...], dz_ref[...], 1, 0).astype(BF)
    ddown_ref[0] = dot(a_ref[...], g_ref[...], 0, 0).astype(BF)

    @pl.when(step == groups - 1)
    def _():
        rows_ref[...] = jnp.zeros_like(rows_ref)

        def third(i, c):
            t = tile(i)
            y_ref[t, :] = acc_ref[t, :].astype(BF)
            g = g_ref[t, :].astype(F32)
            unit, scale = normed(h_ref[t, :])
            dn = dn_ref[t, :]
            dh = g + norm_back(dn, unit, scale, vec_ref[6:7, :])
            dh_ref[t, :] = dh
            dr = dh.astype(BF)
            dr_ref[t, :] = dr
            do_ref[:, t] = dot(wo_ref[...], dr, 1, 1).astype(BF)
            rows_ref[0:8, :] += fold_rows(dr.astype(F32))
            rows_ref[8:16, :] += fold_rows(dn * unit)
            rows_ref[16:24, :] += fold_rows(dn)
            rows_ref[24:32, :] += fold_rows(g)
            return c

        lax.fori_loop(0, tiles, third, 0)
        dwo_ref[...] = dot(o_ref[...], dr_ref[...], 1, 0).astype(BF)


def middle_part(x, g, o, vec, wo, up, down):
    tokens, width = x.shape
    groups = up.shape[0]
    whole = lambda s: pl.BlockSpec(s, lambda i: (0,) * len(s))
    block = pl.BlockSpec((1, width, width), lambda i: (i, 0, 0))
    return pl.pallas_call(
        middle_kernel,
        grid=(groups,),
        in_specs=[
            whole(x.shape),
            whole(g.shape),
            whole(o.shape),
            whole(vec.shape),
            whole(wo.shape),
            block,
            block,
        ],
        out_specs=[
            whole((tokens, width)),
            whole((tokens, width)),
            whole((width, tokens)),
            whole((width, width)),
            block,
            block,
            whole((32, width)),
            pl.BlockSpec((1, 8, width), lambda i: (i, 0, 0)),
        ],
        out_shape=[
            jax.ShapeDtypeStruct((tokens, width), BF),
            jax.ShapeDtypeStruct((tokens, width), F32),
            jax.ShapeDtypeStruct((width, tokens), BF),
            jax.ShapeDtypeStruct((width, width), BF),
            jax.ShapeDtypeStruct((groups, width, width), BF),
            jax.ShapeDtypeStruct((groups, width, width), BF),
            jax.ShapeDtypeStruct((32, width), F32),
            jax.ShapeDtypeStruct((groups, 8, width), F32),
        ],
        scratch_shapes=[
            pltpu.VMEM((tokens, width), F32),
            pltpu.VMEM((tokens, width), BF),
            pltpu.VMEM((width, tokens), BF),
            pltpu.VMEM((tokens, width), F32),
            pltpu.VMEM((tokens, width), F32),
            pltpu.VMEM((tokens, width), BF),
            pltpu.VMEM((tokens, width), BF),
            pltpu.VMEM((tokens, width), BF),
        ],
        compiler_params=pltpu.CompilerParams(vmem_limit_bytes=VMEM_LIMIT),
        name="middle",
    )(x, g, o, vec, wo, up, down)


def final_kernel(
    x_ref, dh_ref, n1_ref, dq_ref, dk_ref, dv_ref, vec_ref, weight_ref,
    dx_ref, dw_ref, rows_ref,
):
    tokens, width = x_ref.shape
    for index, ref in enumerate((dq_ref, dk_ref, dv_ref)):
        dw_ref[index] = dot(n1_ref[...], ref[...], 1, 1).astype(BF)
    rows_ref[...] = jnp.zeros_like(rows_ref)

    def loop(i, c):
        t = pl.ds(pl.multiple_of(i * TILE, TILE), TILE)
        dn = dot(dq_ref[:, t], weight_ref[0], 0, 1)
        dn += dot(dk_ref[:, t], weight_ref[1], 0, 1)
        dn += dot(dv_ref[:, t], weight_ref[2], 0, 1)
        unit, scale = normed(x_ref[t, :].astype(F32))
        dx_ref[t, :] = dh_ref[t, :] + norm_back(dn, unit, scale, vec_ref[0:1, :])
        rows_ref[0:8, :] += fold_rows(dn * unit)
        rows_ref[8:16, :] += fold_rows(dn)
        return c

    lax.fori_loop(0, tokens // TILE, loop, 0)


def final_part(x, dh, n1, dq, dk, dv, vec, weights):
    tokens, width = x.shape
    vmem = pl.BlockSpec(memory_space=pltpu.VMEM)
    return pl.pallas_call(
        final_kernel,
        in_specs=[vmem] * 8,
        out_specs=[vmem] * 3,
        out_shape=[
            jax.ShapeDtypeStruct((tokens, width), F32),
            jax.ShapeDtypeStruct((3, width, width), BF),
            jax.ShapeDtypeStruct((16, width), F32),
        ],
        compiler_params=pltpu.CompilerParams(vmem_limit_bytes=VMEM_LIMIT),
        name="final",
    )(x, dh, n1, dq, dk, dv, vec, weights)


def halves(values):
    high = values.astype(BF)
    return high, (values - high.astype(F32)).astype(BF)


def dot_fine(left, right):
    left_high, left_low = halves(left)
    right_high, right_low = halves(right)
    return (
        dot(left_high, right_low, 1, 0)
        + dot(left_low, right_high, 1, 0)
        + dot(left_high, right_high, 1, 0)
    )


def update_kernel(
    keep_ref, decay_ref, grad_ref, left_ref, right_ref, lroot_ref, rroot_ref, master_ref,
    slot_ref, newleft_ref, newright_ref, newmaster_ref,
):
    @pl.when(keep_ref[0] == 0)
    def _():
        slot_ref[...] = jnp.zeros_like(slot_ref)
        newleft_ref[...] = left_ref[...]
        newright_ref[...] = right_ref[...]
        newmaster_ref[...] = master_ref[...]

    @pl.when(keep_ref[0] != 0)
    def _():
        decay = decay_ref[0]
        grad = grad_ref[...].astype(F32)
        slot_ref[...] = grad
        low = grad.astype(BF)
        newleft_ref[...] = decay * left_ref[...] + (1.0 - decay) * dot(low, low, 1, 1)
        newright_ref[...] = decay * right_ref[...] + (1.0 - decay) * dot(low, low, 0, 0)
        inner = dot_fine(lroot_ref[...], grad)
        direction = dot_fine(inner, rroot_ref[...])
        size = direction.shape[0] * direction.shape[1]
        mean = jnp.sum(direction * direction, keepdims=True) * (1.0 / size)
        newmaster_ref[...] = master_ref[...] - RATE_MATRIX * direction * lax.rsqrt(
            mean + GRAFT_EPSILON
        )


def update(owns, decays, grad, left, right, lroot, rroot, master):
    smem = pl.BlockSpec(memory_space=pltpu.SMEM)
    vmem = pl.BlockSpec(memory_space=pltpu.VMEM)
    return pl.pallas_call(
        update_kernel,
        in_specs=[smem, smem] + [vmem] * 6,
        out_specs=[vmem] * 4,
        out_shape=[jax.ShapeDtypeStruct(left.shape, F32)] * 4,
        compiler_params=pltpu.CompilerParams(vmem_limit_bytes=VMEM_LIMIT),
        name="update",
    )(owns, decays, grad, left, right, lroot, rroot, master)


def positions(segment, heights, widths, patch_rows, patch_cols):
    images = heights.shape[0]
    matches = segment[None, :] == jnp.arange(images, dtype=jnp.int32)[:, None]
    tall = jnp.sum(jnp.where(matches, heights[:, None], 0), axis=0).astype(F32)
    wide = jnp.sum(jnp.where(matches, widths[:, None], 0), axis=0).astype(F32)
    py = patch_rows.astype(F32) * GRID_BASE / tall
    px = patch_cols.astype(F32) * GRID_BASE / wide
    zero = jnp.zeros_like(px)
    return jnp.stack([px, py, segment.astype(F32), zero, zero, zero, zero, zero])


def local(
    tokens, cotangent, vectors, vector_moments, decays, owner, master_slots, left_slots,
    right_slots, left_roots, right_roots, grid_height, grid_width, patch_rows, patch_cols, segment,
):
    dp_index = lax.axis_index("dp")
    mlp_index = lax.axis_index("mlp")
    n_dp = lax.axis_size("dp")
    n_mlp = lax.axis_size("mlp")
    width = tokens.shape[1]
    share = width // n_dp
    owner_row = jnp.take(owner, mlp_index, axis=0)
    holds = owner_row == dp_index
    master = master_slots[0, 0]
    pieces = lax.all_to_all(master.astype(BF).reshape(n_dp, share, width), "dp", 0, 0, tiled=True)
    mine = jnp.take(pieces, owner_row, axis=0)
    every = lax.all_gather(mine[None], ("dp", "mlp"), axis=0, tiled=True)
    blocks = every.reshape(n_dp, n_mlp, 3, share, width).transpose(2, 1, 0, 3, 4)
    blocks = blocks.reshape(3, n_mlp, width, width)
    attention = blocks[0]
    turned = vectors.T
    pos = positions(segment, grid_height, grid_width, patch_rows, patch_cols)
    n1t, q, k, v, cosine, sine, qmark, kmark = project(tokens, pos, vectors, turned, attention)
    o, log_totals = attend(grid_height, grid_width, q, k, v, qmark, kmark)
    output, dh, do, dwo, dup, ddown, mid_rows, dc = middle_part(
        tokens, cotangent, o, vectors, attention[3], blocks[1], blocks[2]
    )
    dq, dk, dv, freq, bias = attend_back(
        grid_height, grid_width, q, k, v, qmark, kmark, log_totals, do, pos, cosine, sine
    )
    input_grad, dwqkv, fin_rows = final_part(tokens, dh, n1t, dq, dk, dv, vectors, attention)

    attention_grads = jnp.concatenate([dwqkv, dwo[None]], axis=0)
    grads = jnp.stack([attention_grads, dup, ddown], axis=1)
    grads = grads.reshape(n_mlp, 3, n_dp, share, width).transpose(2, 0, 1, 3, 4)
    grads = grads.reshape(n_dp * n_mlp * 3, share, width)
    reduced = lax.psum_scatter(grads, ("dp", "mlp"), scatter_dimension=0, tiled=True)
    takers = owner_row[None, :] == jnp.arange(n_dp, dtype=jnp.int32)[:, None]
    kind_of = jnp.sum(jnp.where(takers, jnp.arange(3, dtype=jnp.int32)[None, :], 0), axis=1)
    gradient = lax.all_to_all(jnp.take(reduced, kind_of, axis=0), "dp", 0, 0, tiled=True)
    gradient = gradient.reshape(width, width)
    owns = jnp.any(holds).astype(jnp.int32).reshape(1)
    slot_grad, left_out, right_out, master_out = update(
        owns, decays, gradient, left_slots[0, 0], right_slots[0, 0], left_roots[0, 0],
        right_roots[0, 0], master,
    )

    eights = lambda rows: jnp.sum(rows.reshape(-1, 8, width), axis=1)
    fin = eights(fin_rows)
    mid = eights(mid_rows)
    local_vectors = jnp.concatenate(
        [
            fin,
            bias[0::8],
            mid[0:3],
            dc[:, 0, :],
            mid[3:4],
            freq[0:2].reshape(1, width),
        ],
        axis=0,
    )
    total = lax.psum(local_vectors, ("dp", "mlp"))
    cut = width // n_mlp
    own = lambda table: lax.dynamic_slice_in_dim(table, mlp_index * cut, cut, 1)
    grad_share = own(total)
    decay = decays[1]
    moment_next = decay * own(vector_moments) + (1.0 - decay) * grad_share * grad_share
    vector_next = own(vectors) - RATE_VECTOR * grad_share / (jnp.sqrt(moment_next) + STEP_EPSILON)
    lift = lambda a: a[None, None]
    return (
        output, input_grad, lift(slot_grad), lift(left_out), lift(right_out), lift(master_out),
        grad_share, moment_next, vector_next,
    )


def solution(mesh):
    both = P(("dp", "mlp"))
    flat = P(("dp", "mlp"), None)
    slots = P("dp", "mlp", None, None)
    split = P(None, "mlp")
    return jax.shard_map(
        local,
        mesh=mesh,
        in_specs=(flat, flat, P(), P(), P(), P(), slots, slots, slots, slots, slots)
        + (both,) * 5,
        out_specs=(flat, flat, slots, slots, slots, slots, split, split, split),
        check_vma=False,
    )
```

time: 1220 us -> 602 us (0.49)
  matrix products: 359 us -> 0 us
  blocking collectives: 323 us -> 42.5 us
  Pallas kernels: 0 us -> 193 us
  other arithmetic: 115 us -> 18.8 us
  local copies, waits for them, and re-layouts: 115 us -> 24 us
  waiting for transfers between devices: 271 us -> 288 us
    dot_general x106 -> x0, matrix products: 359 us -> none  [the longest x24 52.2 us: head_scores(): jnp.dot(query_head, key_head.T, preferred_element_type=jnp.float32)]
    psum x2 -> x1, blocking collectives: 323 us -> 42.5 us  [local(): total = lax.psum(local_vectors, ('dp', 'mlp'))]
    pallas_call x0 -> x6, Pallas kernels: none -> 193 us  [the longest x1 52.6 us: middle_part(): pl.pallas_call(middle_kernel, grid=(groups,), in_specs=[whole(x.shape), w...]
    psum x1 -> x0, waiting for transfers between devices: 144 us -> none  [local(): reduced = lax.psum(grad_stack, 'dp')]
    reduce_scatter x3 -> x1, waiting for transfers between devices: 48.4 us -> 161 us  [local(): lax.psum_scatter(grads, ('dp', 'mlp'), scatter_dimension=0, tiled=True)]
    reshape x13 -> x0, local copies, waits for them, and re-layouts: 38.6 us -> none  [the longest x1 12.7 us: local(): grad_act = jnp.einsum('td,med->tme', cotangent, down_weight, preferred_el...]
    reduce_sum x26 -> x4, other arithmetic: 32.9 us -> 0.24 us  [the longest x1 0.09 us: positions(): tall = jnp.sum(jnp.where(matches, heights[:, None], 0), axis=0).astype(F32)]
    unnamed x121 -> x26, local copies, waits for them, and re-layouts: 33.5 us -> 2.77 us
  transfers between devices with their start and end apart: 5 -> 4, of which waited for: 3 -> 3; matrix products, arithmetic and copies ran while one was open for 24% -> 1% of each run, Pallas kernels for 0% -> 0%
where the time goes in v1:
time: 602 us; the launch traced here: 594 us
  waiting for transfers between devices  288 us (48%)
  Pallas kernels  193 us (32%)
  blocking collectives  42.5 us (7%)
  local copies, waits for them, and re-layouts  24 us (4%)
  other arithmetic  18.8 us (3%)
  between operations  16 us (3%)
  starting transfers between devices  12.1 us (2%)
    reduce_scatter x1, waiting for transfers between devices, local(): lax.psum_scatter(grads, ('dp', 'mlp'), scatter_dimension=0, tiled=True)  161 us
    all_gather x1, waiting for transfers between devices, local(): every = lax.all_gather(mine[None], ('dp', 'mlp'), axis=0, tiled=True)  99.9 us
    pallas_call x1, Pallas kernels, middle_part(): pl.pallas_call(middle_kernel, grid=(groups,), in_specs=[whole(x.shape), w...  52.6 us
    pallas_call x1, Pallas kernels, attend_back(): pl.pallas_call(attend_back_kernel, in_specs=[smem, smem] + [vmem] * 10, o...  52.4 us
    psum x1, blocking collectives, local(): total = lax.psum(local_vectors, ('dp', 'mlp'))  42.5 us
    pallas_call x1, Pallas kernels, attend(): pl.pallas_call(attend_kernel, in_specs=[smem, smem] + [vmem] * 5, out_spe...  32.9 us
    all_to_all x1, waiting for transfers between devices, local(): lax.all_to_all(master.astype(BF).reshape(n_dp, share, width), 'dp', 0, 0,...  27.2 us
    pallas_call x1, Pallas kernels, update(): pl.pallas_call(update_kernel, in_specs=[smem, smem] + [vmem] * 6, out_spe...  21.6 us
  transfers between devices with their start and end apart: 4, of which 3 were waited for; matrix products, arithmetic and copies ran while one was open for 1% of the time, Pallas kernels for 0%

profile of v1, /device:TPU:0, one launch (start us, length us, event | category | flops | bytes accessed | tf_op | source)
XLA Modules:
  0.0 594.5 jit_solution(4153478617595817922)
XLA Ops:
  7.2 2.8 convert_element_type.28
  10.0 0.0 copy-start.8
  10.0 0.0 copy-start.9
  10.0 7.4 %all-to-all-start = ((bf16[8,96,768]{2,1,0:T(8,128)(2,1)}), bf16[8,96,768]{2,1,0:T(8,128)(2,1)S(1)}, u32[]{:S(2)}, u32[]{:S(2)}) async-start(bf16[8,96,768]{2,1,0:T(8,128)(2,1)} %bitcast.5), calls=%async_computation | async-start | bytes 2359296 | tf_op jit(solution)/shard_map/all_to_all | solution.py:538
  17.4 0.0 all-gather.2.cloned.1.call-start
  17.5 1.3 compare_reduce_fusion
  18.8 27.2 %all-to-all-done = bf16[8,96,768]{2,1,0:T(8,128)(2,1)S(1)} async-done(((bf16[8,96,768]{2,1,0:T(8,128)(2,1)}), bf16[8,96,768]{2,1,0:T(8,128)(2,1)S(1)}, u32[]{:S(2)}, u32[]{:S(2)}) %all-to-all-start) | async-done | bytes 1179680 | tf_op jit(solution)/shard_map/all_to_all | solution.py:538
  46.0 0.6 gather_fusion
  46.6 0.9 bitcast_select_fusion
  47.5 0.0 all-gather.2.cloned.1.call-update
  47.5 0.0 reduce-scatter.2.cloned.1.call-start
  47.5 0.0 copy-done.5
  47.6 0.0 copy-done.2
  47.6 1.0 copy.43
  48.5 0.0 copy-done.7
  48.5 0.1 select_reduce_fusion
  48.7 0.6 stack.29.pos_ref
  49.3 99.9 %all-gather.2.cloned.1.call-done = bf16[32,3,96,768]{3,2,1,0:T(8,128)(2,1)} async-done(((bf16[1,3,96,768]{3,2,1,0:T(8,128)(2,1)}), bf16[32,3,96,768]{3,2,1,0:T(8,128)(2,1)}) %all-gather.2.cloned.1.call-update) | async-done | bytes 14155792 | tf_op jit(solution)/shard_map/all_gather | solution.py:540
  149.2 5.9 fusion.4
  155.1 2.4 slice.57
  157.5 2.5 copy.44
  160.0 2.5 copy.45
  162.6 2.6 copy.46
  165.2 16.6 %project.1 = (bf16[768,1024]{1,0:T(8,128)(2,1)}, bf16[768,1024]{1,0:T(8,128)(2,1)}, bf16[768,1024]{1,0:T(8,128)(2,1)}, bf16[768,1024]{1,0:T(8,128)(2,1)}, f32[38...) custom-call(bf16[1024,768]{1,0:T(8,128)(2,1)} %x_ref.5, ...), custom_call_target="tpu_custom_call" | custom-call | tf_op jit(solution)/shard_map/project/pallas_call | solution.py:96
  181.8 32.9 %attend.1 = (bf16[768,1024]{1,0:T(8,128)(2,1)}, f32[96,1024]{1,0:T(8,128)}) custom-call(s32[4]{0:T(128)} %height_ref.3, s32[4]{0:T(128)} %width_ref.3, bf16[768,1024]{1,0:T(8,128)(2,1)} %get-tuple-element.39.q_ref, bf16[768,1024]{1,0:T(8,128)(2,1)} %get-tuple-element.40.k_ref, bf16[768,1024]{1,0:T(8,128)(2,1)} %get-tuple-element.41.v_ref, ...), custom_call_target="tpu_custom_call" | custom-call | tf_op jit(solution)/shard_map/attend/pallas_call | solution.py:174
  214.7 52.6 %middle.1 = (bf16[1024,768]{1,0:T(8,128)(2,1)}, f32[1024,768]{1,0:T(8,128)}, bf16[768,1024]{1,0:T(8,128)(2,1)}, bf16[768,768]{1,0:T(8,128)(2,1)}, bf16[4,768,768...) custom-call(bf16[1024,768]{1,0:T(8,128)(2,1)} %x_ref.5, ...), custom_call_target="tpu_custom_call" | custom-call | tf_op jit(solution)/shard_map/middle/pallas_call | solution.py:371
  267.3 52.4 %attend_back.1 = (bf16[768,1024]{1,0:T(8,128)(2,1)}, bf16[768,1024]{1,0:T(8,128)(2,1)}, bf16[768,1024]{1,0:T(8,128)(2,1)}, f32[8,384]{1,0:T(8,128)}, f32[24,768]{1,0:T(8,128)}) custom-call(s32[4]{0:T(128)} %height_ref.3, s32[4]{0:T(128)} %width_ref.3, bf16[768,1024]{1,0:T(8,128)(2,1)} %get-tuple-element.39.q_ref, bf16[768,1024]{1,0:T(8,128)(2,1)} %get-tuple-element.40.k_ref, ...), custom_call_target="tpu_custom_call" | custom-call | tf_op jit(solution)/shard_map/attend_back/pallas_call | solution.py:275
  319.7 16.8 %final.1 = (f32[1024,768]{1,0:T(8,128)}, bf16[3,768,768]{2,1,0:T(8,128)(2,1)}, f32[16,768]{1,0:T(8,128)}) custom-call(bf16[1024,768]{1,0:T(8,128)(2,1)} %x_ref.5, f32[1024,768]{1,0:T(8,128)} %get-tuple-element.46.dh_ref, bf16[768,1024]{1,0:T(8,128)(2,1)} %get-tuple-element.47.n1_ref, bf16[768,1024]{1,0:T(8,128)(2,1)} %get-tuple-element.52.dq_ref, ...), custom_call_target="tpu_custom_call" | custom-call | tf_op jit(solution)/shard_map/final/pallas_call | solution.py:444
  336.5 10.2 %pad_maximum_fusion = bf16[4,3,8,96,768]{4,3,1,0,2:T(8,128)(2,1)} fusion(bf16[1,1,8,96,768]{4,3,1,0,2:T(8,128)(2,1)S(1)} %bitcast.76, bf16[3,1,8,96,768]{4,3,2,0,1:T(8,128)(2,1)} %bitcast.70, bf16[4,1,8,96,768]{4,3,2,0,1:T(8,128)(2,1)} %bitcast.68, bf16[4,1,8,96,768]{4,3,2,0,1:T(8,128)(2,1)} %bitcast.69), kind=kLoop, calls=%fused_computation.2 | loop fusion | flops 56623104 | bytes 28311552 | tf_op jit(solution)/shard_map/stack | solution.py:557
  346.7 0.0 reduce-scatter.2.cloned.1.call-update
  346.7 0.1 select_reduce_fusion.2
  346.8 0.0 copy-start.10
  346.9 0.0 copy-start.4
  346.9 161.1 %reduce-scatter.2.cloned.1.call-done = bf16[3,96,768]{2,1,0:T(8,128)(2,1)} async-done(((bf16[96,96,768]{2,1,0:T(8,128)(2,1)}), bf16[3,96,768]{2,1,0:T(8,128)(2,1)}) %reduce-scatter.2.cloned.1.call-update) | async-done | bytes 442384 | tf_op jit(solution)/shard_map/reduce_scatter | solution.py:560
  507.9 1.6 gather_fusion.1
  509.6 1.2 broadcast_select_fusion
  510.8 4.6 all-to-all-start.1
  516.0 0.0 copy-done.10
  516.0 0.6 slice.44
  517.3 0.9 slice.39
  518.2 0.9 slice.41
  519.1 0.7 slice_bitcast_fusion
  519.9 0.1 concatenate.15
  519.9 42.5 %psum.7 = f32[14,768]{1,0:T(8,128)S(1)} all-reduce(f32[14,768]{1,0:T(8,128)S(1)} %concatenate.15), channel_id=1, replica_groups=mesh['dp'=8,'mlp'=4] {'dp','mlp'}, use_global_device_ids=true, to_apply=%region_7.8 | all-reduce | flops 10752 | bytes 86016 | tf_op jit(solution)/shard_map/psum | solution.py:585
  562.4 2.1 divide_subtract_fusion
  564.5 0.0 all-to-all-done.1
  564.5 1.0 copy-done
  565.5 21.6 %update.1 = (f32[768,768]{1,0:T(8,128)}, f32[768,768]{1,0:T(8,128)}, f32[768,768]{1,0:T(8,128)}, f32[768,768]{1,0:T(8,128)}) custom-call(s32[1]{0:T(128)} %bitcast.16.keep_ref, f32[2]{0:T(128)} %decay_ref.1, bf16[768,768]{1,0:T(8,128)(2,1)} %bitcast.66, f32[768,768]{1,0:T(8,128)} %bitcast.71, f32[768,768]{1,0:T(8,128)} %bitcast.72, f32[768,768]{1,0:T(8,128)} %bitcast.73, ...), custom_call_target="tpu_custom_call" | custom-call | tf_op jit(solution)/shard_map/update/pallas_call | solution.py:504
  (28 shorter events, 0.2 us)
Async XLA Ops:
  10.0 37.6 %copy-start.5 = (s32[1024]{0:T(1024)S(1)}, s32[1024]{0:T(1024)}, u32[]{:S(2)}) copy-start(s32[1024]{0:T(1024)} %param.31) | copy-start | bytes 12292
  10.0 37.6 %copy-start.2 = (f32[14,768]{1,0:T(8,128)S(1)}, f32[14,768]{1,0:T(8,128)}, u32[]{:S(2)}) copy-start(f32[14,768]{1,0:T(8,128)} %vec_ref.5) | copy-start | bytes 129028
  10.0 38.6 %copy-start.6 = (s32[4]{0:T(128)S(1)}, s32[4]{0:T(128)}, u32[]{:S(2)}) copy-start(s32[4]{0:T(128)} %height_ref.3) | copy-start | bytes 52
  10.0 38.6 %copy-start.7 = (s32[4]{0:T(128)S(1)}, s32[4]{0:T(128)}, u32[]{:S(2)}) copy-start(s32[4]{0:T(128)} %width_ref.3) | copy-start | bytes 52
  10.0 38.7 %copy-start.8 = (s32[1024]{0:T(1024)S(1)}, s32[1024]{0:T(1024)}, u32[]{:S(2)}) copy-start(s32[1024]{0:T(1024)} %param.29) | copy-start | bytes 12292
  10.0 38.7 %copy-start.9 = (s32[1024]{0:T(1024)S(1)}, s32[1024]{0:T(1024)}, u32[]{:S(2)}) copy-start(s32[1024]{0:T(1024)} %param.30) | copy-start | bytes 12292
  10.0 36.0 %all-to-all-start = ((bf16[8,96,768]{2,1,0:T(8,128)(2,1)}), bf16[8,96,768]{2,1,0:T(8,128)(2,1)S(1)}, u32[]{:S(2)}, u32[]{:S(2)}) async-start(bf16[8,96,768]{2,1,0:T(8,128)(2,1)} %bitcast.5), calls=%async_computation | async-start | bytes 2359296 | tf_op jit(solution)/shard_map/all_to_all | solution.py:538
  17.4 131.8 %all-gather.2.cloned.1.call-start = ((), (), s32[]{:S(2)}) async-start(), calls=%async_computation.3 | async-start | bytes 14598144 | tf_op jit(solution)/shard_map/all_gather | solution.py:540
  47.5 460.5 %reduce-scatter.2.cloned.1.call-start = ((), (), s32[]{:S(2)}) async-start(), calls=%async_computation.4 | async-start | bytes 14598144 | tf_op jit(solution)/shard_map/reduce_scatter | solution.py:560
  319.7 16.8 %copy-start.1 = (bf16[768,768]{1,0:T(8,128)(2,1)S(1)}, bf16[768,768]{1,0:T(8,128)(2,1)}, u32[]{:S(2)}) copy-start(bf16[768,768]{1,0:T(8,128)(2,1)} %get-tuple-element.57) | copy-start | bytes 3538948
  346.8 169.2 %copy-start.10 = (f32[2]{0:T(128)S(1)}, f32[2]{0:T(128)}, u32[]{:S(2)}) copy-start(f32[2]{0:T(128)} %decay_ref.1) | copy-start | bytes 28
  346.8 172.2 %copy-start.3 = (f32[32,768]{1,0:T(8,128)S(1)}, f32[32,768]{1,0:T(8,128)}, u32[]{:S(2)}) copy-start(f32[32,768]{1,0:T(8,128)} %get-tuple-element.66) | copy-start | bytes 294916
  346.9 173.0 %copy-start.4 = (f32[16,768]{1,0:T(8,128)S(1)}, f32[16,768]{1,0:T(8,128)}, u32[]{:S(2)}) copy-start(f32[16,768]{1,0:T(8,128)} %get-tuple-element.64) | copy-start | bytes 147460
  510.8 53.7 %all-to-all-start.1 = ((bf16[8,96,768]{2,1,0:T(8,128)(2,1)}), bf16[8,96,768]{2,1,0:T(8,128)(2,1)S(1)}, u32[]{:S(2)}, u32[]{:S(2)}) async-start(bf16[8,96,768]{2,1,0:T(8,128)(2,1)} %broadcast_select_fusion), calls=%async_computation.2 | async-start | bytes 2359296 | tf_op jit(solution)/shard_map/all_to_all | solution.py:563
  564.5 1.0 copy-start
Sparse Core Ops, SparseCore 0:
  47.6 101.5 all-gather.1
  346.8 161.0 reduce-scatter.1

commit v2 on v1

--- a/solution.py
+++ b/solution.py
@@ -18,6 +18,7 @@
 MASK_SHIFT = -(2.0**100)
 BLOCK = 128
 TILE = 256
+PARTS = 2
 F32 = jnp.float32
 BF = jnp.bfloat16
 VMEM_LIMIT = 60 * 1024 * 1024
@@ -50,6 +51,223 @@
 
 def fold_rows(values):
     return jnp.sum(values.reshape(values.shape[0] // 8, 8, values.shape[1]), axis=0)
+
+
+def place():
+    d = lax.axis_index("dp")
+    m = lax.axis_index("mlp")
+    return d // 2, d % 2, m // 2, m % 2
+
+
+def at(z, x, y, c):
+    return (2 * z + x, 2 * y + c)
+
+
+def greet(peers):
+    barrier = pltpu.get_barrier_semaphore()
+    for peer in peers:
+        pl.semaphore_signal(barrier, inc=1, device_id=peer, device_id_type=pl.DeviceIdType.MESH)
+    pl.semaphore_wait(barrier, len(peers))
+
+
+class Mail:
+    def __init__(self, sems):
+        self.sems = sems
+        self.like = []
+
+    def send(self, source, target, arrival, peer, like):
+        slot = len(self.like)
+        pltpu.make_async_remote_copy(
+            src_ref=source,
+            dst_ref=target,
+            send_sem=self.sems.at[slot],
+            recv_sem=arrival,
+            device_id=peer,
+            device_id_type=pl.DeviceIdType.MESH,
+        ).start()
+        self.like.append(like)
+        return slot
+
+    def settle(self, slot):
+        arrived(self.like[slot], self.sems.at[slot])
+        self.like[slot] = None
+
+    def finish(self):
+        for slot, like in enumerate(self.like):
+            if like is not None:
+                self.settle(slot)
+
+
+def arrived(target, arrival):
+    pltpu.make_async_copy(target, target, arrival).wait()
+
+
+def enter_kernel(
+    owner_ref, slot_ref, x_ref, pos_ref, vec_ref, turned_ref,
+    n1_ref, q_ref, k_ref, v_ref, cos_ref, sin_ref, qmark_ref, kmark_ref, weight_ref, zone_ref,
+    land_ref, mine_ref, att_ref, zland_ref,
+    land_sem, zone_sem, att_sem, send_sem, local_sem,
+):
+    z, x, y, c = place()
+    m = 2 * y + c
+    d = 2 * z + x
+    n_dp = land_ref.shape[0]
+    right_x, right_y, partner = at(z, 1 - x, y, c), at(z, x, 1 - y, c), at(z, x, y, 1 - c)
+    dp_peers = [((d + off) % n_dp, m) for off in range(1, n_dp)]
+    greet(dp_peers + [right_y, partner])
+    mail = Mail(send_sem)
+    piece = mine_ref.at[0]
+    own = pltpu.make_async_copy(slot_ref.at[d], land_ref.at[d], local_sem.at[0])
+    own.start()
+    for peer in dp_peers:
+        mail.send(slot_ref.at[peer[0]], land_ref.at[d], land_sem.at[d], peer, piece)
+
+    tokens = x_ref.shape[0]
+    half = cos_ref.shape[0]
+    last = turned_ref.shape[1] - 1
+    tiles = tokens // TILE
+
+    def prepare(i, carry):
+        t = pl.ds(pl.multiple_of(i * TILE, TILE), TILE)
+        unit, _ = normed(x_ref[t, :].astype(F32))
+        n1_ref[:, t] = (unit * vec_ref[0:1, :] + vec_ref[1:2, :]).astype(BF).T
+        angle = turned_ref[half:, last:] * pos_ref[1:2, t] + turned_ref[:half, last:] * pos_ref[0:1, t]
+        cos_ref[:, t] = jnp.cos(angle)
+        sin_ref[:, t] = jnp.sin(angle)
+        seg = pos_ref[2:3, t].astype(jnp.int32)
+        row = lax.broadcasted_iota(jnp.int32, (qmark_ref.shape[0], TILE), 0)
+        qmark_ref[:, t] = jnp.where(row == seg, 1.0, 0.0).astype(BF)
+        kmark_ref[:, t] = jnp.where(row == seg, 0.0, MASK_SHIFT).astype(BF)
+        return carry
+
+    lax.fori_loop(0, tiles, prepare, 0)
+
+    own.wait()
+    for off in range(1, n_dp):
+        source = (d + off) % n_dp
+        arrived(land_ref.at[source], land_sem.at[source])
+    for kind in range(3):
+        mine_ref[kind] = land_ref[owner_ref[m, kind]]
+
+    def spread_z(source, target, sem):
+        for off in range(1, 4):
+            mail.send(source, target, sem, at((z + off) % 4, x, y, c), piece)
+
+    spread_z(mine_ref.at[0], att_ref.at[m, d], att_sem.at[m, d])
+    for peer in (right_x, right_y, partner):
+        mail.send(mine_ref.at[0], att_ref.at[m, d], att_sem.at[m, d], peer, piece)
+    keep = pltpu.make_async_copy(mine_ref.at[0], att_ref.at[m, d], local_sem.at[1])
+    keep.start()
+    for off in (1, 3, 2):
+        e = 2 * ((z + off) % 4) + x
+        arrived(att_ref.at[m, e], att_sem.at[m, e])
+        for peer in (right_x, right_y, partner):
+            mail.send(att_ref.at[m, e], att_ref.at[m, e], att_sem.at[m, e], peer, piece)
+    keeps = []
+    for kind in range(2):
+        spread_z(mine_ref.at[1 + kind], zland_ref.at[kind, z], zone_sem.at[kind, z])
+        copy = pltpu.make_async_copy(
+            mine_ref.at[1 + kind], zland_ref.at[kind, z], local_sem.at[2 + kind]
+        )
+        copy.start()
+        keeps.append(copy)
+    m_y = 2 * (1 - y) + c
+    for part in range(4):
+        e = 2 * part + 1 - x
+        arrived(att_ref.at[m, e], att_sem.at[m, e])
+        if part < 2:
+            mail.send(att_ref.at[m, e], att_ref.at[m, e], att_sem.at[m, e], right_y, piece)
+        mail.send(att_ref.at[m, e], att_ref.at[m, e], att_sem.at[m, e], partner, piece)
+        f = 2 * part + x
+        arrived(att_ref.at[m_y, f], att_sem.at[m_y, f])
+        if part >= 2:
+            mail.send(att_ref.at[m_y, f], att_ref.at[m_y, f], att_sem.at[m_y, f], right_x, piece)
+        mail.send(att_ref.at[m_y, f], att_ref.at[m_y, f], att_sem.at[m_y, f], partner, piece)
+    for part in range(4):
+        e = 2 * part + 1 - x
+        arrived(att_ref.at[m_y, e], att_sem.at[m_y, e])
+        mail.send(att_ref.at[m_y, e], att_ref.at[m_y, e], att_sem.at[m_y, e], partner, piece)
+    for step in range(2):
+        other = 2 * step + 1 - c
+        for e in range(n_dp):
+            arrived(att_ref.at[other, e], att_sem.at[other, e])
+    keep.wait()
+    out = pltpu.make_async_copy(att_ref, weight_ref, local_sem.at[4])
+    out.start()
+
+    part = half // HEADS
+    width = x_ref.shape[1]
+
+    def weight(index):
+        return att_ref[index].reshape(width, width)
+
+    def rotate(i, carry):
+        t = pl.ds(pl.multiple_of(i * TILE, TILE), TILE)
+        n1t = n1_ref[:, t]
+        cosine = cos_ref[:, t]
+        sine = sin_ref[:, t]
+        for index, (ref, scale) in enumerate(((q_ref, 0.125), (k_ref, 1.0))):
+            flat = dot(weight(index), n1t, 0, 0) + turned_ref[:, 2 + index : 3 + index]
+            for head in range(HEADS):
+                low, mid = 2 * part * head, 2 * part * head + part
+                a = flat[low:mid]
+                b = flat[mid : mid + part]
+                cs = cosine[part * head : part * (head + 1)]
+                sn = sine[part * head : part * (head + 1)]
+                ref[low:mid, t] = (a * cs - b * sn).astype(BF) * jnp.asarray(scale, BF)
+                ref[mid : mid + part, t] = (b * cs + a * sn).astype(BF) * jnp.asarray(scale, BF)
+        v_ref[:, t] = (dot(weight(2), n1t, 0, 0) + turned_ref[:, 4:5]).astype(BF)
+        return carry
+
+    lax.fori_loop(0, tiles, rotate, 0)
+    for kind in range(2):
+        keeps[kind].wait()
+        for off in range(1, 4):
+            e = (z + off) % 4
+            arrived(zland_ref.at[kind, e], zone_sem.at[kind, e])
+    last_out = pltpu.make_async_copy(zland_ref, zone_ref, local_sem.at[5])
+    last_out.start()
+    out.wait()
+    last_out.wait()
+    mail.finish()
+
+
+def enter(owner, slot, x, pos, vec, turned):
+    rows, width = x.shape
+    half = width // 2
+    n_dp, share, _ = slot.shape
+    n_mlp = owner.shape[0]
+    smem = pl.BlockSpec(memory_space=pltpu.SMEM)
+    vmem = pl.BlockSpec(memory_space=pltpu.VMEM)
+    hbm = pl.BlockSpec(memory_space=pl.ANY)
+    out = lambda n, dtype: jax.ShapeDtypeStruct((n, rows), dtype)
+    return pl.pallas_call(
+        enter_kernel,
+        in_specs=[smem, hbm, vmem, vmem, vmem, vmem],
+        out_specs=[vmem] * 8 + [hbm] * 2,
+        out_shape=[out(width, BF)] * 4
+        + [out(half, F32)] * 2
+        + [out(16, BF)] * 2
+        + [
+            jax.ShapeDtypeStruct((n_mlp, n_dp, share, width), BF),
+            jax.ShapeDtypeStruct((2, 4, share, width), BF),
+        ],
+        scratch_shapes=[
+            pltpu.VMEM((n_dp, share, width), BF),
+            pltpu.VMEM((3, share, width), BF),
+            pltpu.VMEM((n_mlp, n_dp, share, width), BF),
+            pltpu.VMEM((2, 4, share, width), BF),
+            pltpu.SemaphoreType.DMA((n_dp,)),
+            pltpu.SemaphoreType.DMA((2, 4)),
+            pltpu.SemaphoreType.DMA((n_mlp, n_dp)),
+            pltpu.SemaphoreType.DMA((64,)),
+            pltpu.SemaphoreType.DMA((6,)),
+        ],
+        compiler_params=pltpu.CompilerParams(
+            vmem_limit_bytes=VMEM_LIMIT, collective_id=0, has_side_effects=True
+        ),
+        name="enter",
+    )(owner, slot, x, pos, vec, turned)
 
 
 def project_kernel(
@@ -192,7 +410,8 @@
 ):
     tokens = q_ref.shape[1]
     blocks = tokens // BLOCK
-    size = q_ref.shape[0] // HEADS
+    heads = log_ref.shape[0] // 8
+    size = q_ref.shape[0] // heads
     half = size // 2
     group = 2
     gk_ref[...] = jnp.zeros_like(gk_ref)
@@ -231,7 +450,7 @@
                     one(block, part, base, n)
                     return c
 
-                lax.fori_loop(0, HEADS // group, inner, 0)
+                lax.fori_loop(0, heads // group, inner, 0)
 
         return carry
 
@@ -261,27 +480,30 @@
         dv_ref[both, :] = gv_ref[both, :].astype(BF)
         return carry
 
-    lax.fori_loop(0, HEADS, unturn, 0)
+    lax.fori_loop(0, heads, unturn, 0)
     freq_ref[...] = dot(pos_ref[...], turn_ref[...], 1, 1, lax.Precision.HIGHEST)
     ones = jnp.ones((8, tokens), BF)
     for index, ref in enumerate((dq_ref, dk_ref, dv_ref)):
         bias_ref[8 * index : 8 * index + 8, :] = dot(ones, ref[...], 1, 1)
 
 
-def attend_back(heights, widths, q, k, v, qmark, kmark, log_totals, do, pos, cosine, sine):
+def attend_back(heights, widths, q, k, v, qmark, kmark, log_totals, do, pos, cosine, sine, part):
     smem = pl.BlockSpec(memory_space=pltpu.SMEM)
-    vmem = pl.BlockSpec(memory_space=pltpu.VMEM)
     width, tokens = q.shape
+    half = width // PARTS
+    cut = lambda a: pl.BlockSpec((a.shape[0] // PARTS, tokens), lambda i: (part, 0))
+    whole = lambda a: pl.BlockSpec(a.shape, lambda i: (0, 0))
+    out = lambda n, cols, dtype: jax.ShapeDtypeStruct((n, cols), dtype)
+    outs = [out(half, tokens, BF)] * 3 + [out(8, half // 2, F32), out(24, half, F32)]
     return pl.pallas_call(
         attend_back_kernel,
-        in_specs=[smem, smem] + [vmem] * 10,
-        out_specs=[vmem] * 5,
-        out_shape=[jax.ShapeDtypeStruct(q.shape, BF)] * 3
-        + [
-            jax.ShapeDtypeStruct((8, width // 2), F32),
-            jax.ShapeDtypeStruct((24, width), F32),
-        ],
-        scratch_shapes=[pltpu.VMEM(q.shape, F32)] * 3 + [pltpu.VMEM((width // 2, tokens), F32)],
+        grid=(1,),
+        in_specs=[smem, smem, cut(q), cut(k), cut(v), whole(qmark), whole(kmark), cut(log_totals)]
+        + [cut(do), whole(pos), cut(cosine), cut(sine)],
+        out_specs=[whole(a) for a in outs],
+        out_shape=outs,
+        scratch_shapes=[pltpu.VMEM((half, tokens), F32)] * 3
+        + [pltpu.VMEM((half // 2, tokens), F32)],
         compiler_params=pltpu.CompilerParams(vmem_limit_bytes=VMEM_LIMIT),
         name="attend_back",
     )(heights, widths, q, k, v, qmark, kmark, log_totals, do, pos, cosine, sine)
@@ -416,10 +638,11 @@
 
 
 def final_kernel(
-    x_ref, dh_ref, n1_ref, dq_ref, dk_ref, dv_ref, vec_ref, weight_ref,
+    x_ref, dh_ref, n1_ref, dq_ref, dk_ref, dv_ref, vec_ref, weight_ref, dwo_ref,
     dx_ref, dw_ref, rows_ref,
 ):
     tokens, width = x_ref.shape
+    dw_ref[3] = dwo_ref[...]
     for index, ref in enumerate((dq_ref, dk_ref, dv_ref)):
         dw_ref[index] = dot(n1_ref[...], ref[...], 1, 1).astype(BF)
     rows_ref[...] = jnp.zeros_like(rows_ref)
@@ -438,21 +661,481 @@
     lax.fori_loop(0, tokens // TILE, loop, 0)
 
 
-def final_part(x, dh, n1, dq, dk, dv, vec, weights):
+def final_part(x, dh, n1, dq, dk, dv, vec, weights, dwo):
     tokens, width = x.shape
     vmem = pl.BlockSpec(memory_space=pltpu.VMEM)
     return pl.pallas_call(
         final_kernel,
-        in_specs=[vmem] * 8,
+        in_specs=[vmem] * 9,
         out_specs=[vmem] * 3,
         out_shape=[
             jax.ShapeDtypeStruct((tokens, width), F32),
-            jax.ShapeDtypeStruct((3, width, width), BF),
+            jax.ShapeDtypeStruct((4, width, width), BF),
             jax.ShapeDtypeStruct((16, width), F32),
         ],
         compiler_params=pltpu.CompilerParams(vmem_limit_bytes=VMEM_LIMIT),
         name="final",
-    )(x, dh, n1, dq, dk, dv, vec, weights)
+    )(x, dh, n1, dq, dk, dv, vec, weights, dwo)
+
+
+def center_kernel(
+    x_ref, g_ref, o_ref, vec_ref, weight_ref, zone_ref, xzone_ref, yzone_ref,
+    y_ref, dh_ref, do_ref, dwo_ref, rows_ref, dc_ref, upgo_ref, upstay_ref, downgo_ref, downstay_ref,
+    h_ref, n2_ref, n2t_ref, acc_ref, dn_ref, a_ref, dz_ref, wo_ref, w_ref, near_ref,
+    land_sem, near_sem, send_sem, local_sem, out_sem,
+):
+    z, x, y, c = place()
+    m = 2 * y + c
+    m_y = 2 * (1 - y) + c
+    right_x, right_y, partner = at(z, 1 - x, y, c), at(z, x, 1 - y, c), at(z, x, y, 1 - c)
+    tokens, width = x_ref.shape
+    tiles = tokens // TILE
+    n_dp = w_ref.shape[2]
+    fetch = pltpu.make_async_copy(weight_ref.at[3], wo_ref, local_sem.at[24])
+    fetch.start()
+    greet([right_x, right_y, partner])
+    mail = Mail(send_sem)
+    piece = w_ref.at[0, 0, 0]
+    column_like = near_ref.at[0, 0]
+    kept = []
+    for kind in range(2):
+        to = w_ref.at[kind]
+        sem = land_sem.at[kind]
+        for part in range(4):
+            own, from_x = 2 * part + x, 2 * part + 1 - x
+            if part < 2:
+                mail.send(xzone_ref.at[kind, part], to.at[m, from_x], sem.at[m, from_x], right_y, piece)
+            else:
+                mail.send(yzone_ref.at[kind, part], to.at[m_y, own], sem.at[m_y, own], right_x, piece)
+    for ref, column, shift in ((zone_ref, m, 0), (xzone_ref, m, 1), (yzone_ref, m_y, 0)):
+        for kind in range(2):
+            to = w_ref.at[kind]
+            sem = land_sem.at[kind]
+            for part in range(4):
+                e = 2 * part + (x + shift) % 2
+                mail.send(ref.at[kind, part], to.at[column, e], sem.at[column, e], partner, piece)
+                copy = pltpu.make_async_copy(
+                    ref.at[kind, part], to.at[column, e], local_sem.at[len(kept)]
+                )
+                copy.start()
+                kept.append(copy)
+
+    def tile(i):
+        return pl.ds(pl.multiple_of(i * TILE, TILE), TILE)
+
+    fetch.wait()
+    wo = wo_ref.reshape(width, width)
+
+    def first(i, carry):
+        t = tile(i)
+        branch = dot(o_ref[:, t], wo[...], 0, 0) + vec_ref[5:6, :]
+        h = x_ref[t, :].astype(F32) + branch
+        h_ref[t, :] = h
+        unit, _ = normed(h)
+        n2 = (unit * vec_ref[6:7, :] + vec_ref[7:8, :]).astype(BF)
+        n2_ref[t, :] = n2
+        n2t_ref[:, t] = n2.T
+        acc_ref[t, :] = h + vec_ref[12:13, :]
+        dn_ref[t, :] = jnp.zeros((TILE, width), F32)
+        return carry
+
+    lax.fori_loop(0, tiles, first, 0)
+    for copy in kept:
+        copy.wait()
+    forwards = []
+
+    def work(step, carry):
+        column = 2 * ((y + step // 2) % 2) + (c + (step + 1) // 2) % 2
+
+        @pl.when(step == 1)
+        def _():
+            for kind in range(2):
+                sem = land_sem.at[kind]
+                for part in range(4):
+                    e = 2 * part + 1 - x
+                    arrived(w_ref.at[kind, m_y, e], sem.at[m_y, e])
+                    forwards.append(
+                        mail.send(
+                            w_ref.at[kind, m_y, e], w_ref.at[kind, m_y, e], sem.at[m_y, e], partner, piece
+                        )
+                    )
+                for e in range(n_dp):
+                    arrived(w_ref.at[kind, 2 * y + 1 - c, e], sem.at[2 * y + 1 - c, e])
+
+        @pl.when(step == 2)
+        def _():
+            for kind in range(2):
+                for e in range(n_dp):
+                    other = 2 * (1 - y) + 1 - c
+                    arrived(w_ref.at[kind, other, e], land_sem.at[kind, other, e])
+            for slot in forwards:
+                arrived(w_ref.at[0, 0, 0], send_sem.at[slot])
+                mail.like[slot] = None
+
+        up = w_ref.at[0, column].reshape(width, width)
+        down = w_ref.at[1, column].reshape(width, width)
+        up_bias = vec_ref[pl.ds(8 + column, 1), :]
+
+        def second(i, c):
+            t = tile(i)
+            zed = dot(n2_ref[t, :], up[...], 1, 0) + up_bias
+            cdf = 0.5 * (1.0 + lax.erf(zed * math.sqrt(0.5)))
+            a = (zed * cdf).astype(BF)
+            a_ref[t, :] = a
+            acc_ref[t, :] += dot(a, down[...], 1, 0)
+            da = dot(g_ref[t, :], down[...], 1, 1)
+            slope = cdf + zed * (jnp.exp(-0.5 * zed * zed) * (1.0 / math.sqrt(2.0 * math.pi)))
+            dz = (da * slope).astype(BF)
+            dz_ref[t, :] = dz
+            dn_ref[t, :] += dot(dz, up[...], 1, 1)
+            return c
+
+        lax.fori_loop(0, tiles, second, 0)
+        dc_ref[column] = dot(jnp.ones((8, tokens), BF), dz_ref[...], 1, 0)
+        up[...] = dot(n2t_ref[...], dz_ref[...], 1, 0).astype(BF)
+        down[...] = dot(a_ref[...], g_ref[...], 0, 0).astype(BF)
+        for s, row in ((1, y), (2, 1 - y)):
+
+            @pl.when(step == s)
+            def _():
+                for kind in range(2):
+                    mail.send(
+                        w_ref.at[kind, 2 * row + 1 - c], near_ref.at[kind, row],
+                        near_sem.at[kind, row], partner, column_like,
+                    )
+
+        return carry
+
+    lax.fori_loop(0, 4, work, 0)
+
+    outs = []
+
+    def emit(source, target):
+        copy = pltpu.make_async_copy(source, target, out_sem.at[len(outs)])
+        copy.start()
+        outs.append(copy)
+
+    for row in (y, 1 - y):
+        for kind in range(2):
+            arrived(near_ref.at[kind, row], near_sem.at[kind, row])
+
+            def summed(e, carry):
+                total = w_ref[kind, 2 * row + c, e].astype(F32) + near_ref[kind, row, e].astype(F32)
+                near_ref[kind, row, e] = total.astype(BF)
+                return carry
+
+            lax.fori_loop(0, n_dp, summed, 0)
+    for row in range(2):
+        for part in range(4):
+            emit(near_ref.at[0, row, 2 * part + 1 - x], upgo_ref.at[row, part])
+            emit(near_ref.at[0, row, 2 * part + x], upstay_ref.at[row, part])
+    emit(near_ref.at[1, 1 - y], downgo_ref)
+    emit(near_ref.at[1, y], downstay_ref)
+
+    rows_ref[...] = jnp.zeros_like(rows_ref)
+
+    def third(i, carry):
+        t = tile(i)
+        y_ref[t, :] = acc_ref[t, :].astype(BF)
+        g = g_ref[t, :].astype(F32)
+        unit, scale = normed(h_ref[t, :])
+        dn = dn_ref[t, :]
+        dh = g + norm_back(dn, unit, scale, vec_ref[6:7, :])
+        dh_ref[t, :] = dh
+        dr = dh.astype(BF)
+        a_ref[t, :] = dr
+        do_ref[:, t] = dot(wo[...], dr, 1, 1).astype(BF)
+        rows_ref[0:8, :] += fold_rows(dr.astype(F32))
+        rows_ref[8:16, :] += fold_rows(dn * unit)
+        rows_ref[16:24, :] += fold_rows(dn)
+        rows_ref[24:32, :] += fold_rows(g)
+        return carry
+
+    lax.fori_loop(0, tiles, third, 0)
+    dwo_ref[...] = dot(o_ref[...], a_ref[...], 1, 0).astype(BF)
+    for copy in outs:
+        copy.wait()
+    mail.finish()
+
+
+def center(x, g, o, vec, weights, zone, xzone, yzone):
+    tokens, width = x.shape
+    n_mlp, n_dp, share, _ = weights.shape
+    vmem = pl.BlockSpec(memory_space=pltpu.VMEM)
+    hbm = pl.BlockSpec(memory_space=pl.ANY)
+    shape = jax.ShapeDtypeStruct
+    dma = pltpu.SemaphoreType.DMA
+    return pl.pallas_call(
+        center_kernel,
+        in_specs=[vmem] * 4 + [hbm] * 4,
+        out_specs=[vmem] * 6 + [hbm] * 4,
+        out_shape=[
+            shape((tokens, width), BF),
+            shape((tokens, width), F32),
+            shape((width, tokens), BF),
+            shape((width, width), BF),
+            shape((32, width), F32),
+            shape((n_mlp, 8, width), F32),
+        ]
+        + [shape((2, 4, share, width), BF)] * 2
+        + [shape((n_dp, share, width), BF)] * 2,
+        scratch_shapes=[
+            pltpu.VMEM((tokens, width), F32),
+            pltpu.VMEM((tokens, width), BF),
+            pltpu.VMEM((width, tokens), BF),
+            pltpu.VMEM((tokens, width), F32),
+            pltpu.VMEM((tokens, width), F32),
+            pltpu.VMEM((tokens, width), BF),
+            pltpu.VMEM((tokens, width), BF),
+            pltpu.VMEM((n_dp, share, width), BF),
+            pltpu.VMEM((2, n_mlp, n_dp, share, width), BF),
+            pltpu.VMEM((2, 2, n_dp, share, width), BF),
+            dma((2, n_mlp, n_dp)), dma((2, 2)), dma((48,)), dma((25,)), dma((18,)),
+        ],
+        compiler_params=pltpu.CompilerParams(
+            vmem_limit_bytes=VMEM_LIMIT, collective_id=1, has_side_effects=True
+        ),
+        name="center",
+    )(x, g, o, vec, weights, zone, xzone, yzone)
+
+
+def added(*values):
+    total = values[0].astype(F32)
+    for value in values[1:]:
+        total = total + value.astype(F32)
+    return total.astype(BF)
+
+
+def merge_kernel(
+    upstay_ref, upgot_ref, downstay_ref, downgot_ref, upgo_out, upstay_out, downgo_out, downstay_out
+):
+    _, x, y, _ = place()
+    for part in range(4):
+        upgo_out[part] = added(upstay_ref[1 - y, part], upgot_ref[1 - y, part])
+        upstay_out[part] = added(upstay_ref[y, part], upgot_ref[y, part])
+        e = 2 * part + 1 - x
+        downgo_out[part] = added(downstay_ref[e], downgot_ref[e])
+        f = 2 * part + x
+        downstay_out[part] = added(downstay_ref[f], downgot_ref[f])
+
+
+def merge(upstay, upgot, downstay, downgot):
+    vmem = pl.BlockSpec(memory_space=pltpu.VMEM)
+    return pl.pallas_call(
+        merge_kernel,
+        in_specs=[vmem] * 4,
+        out_specs=[vmem] * 4,
+        out_shape=[jax.ShapeDtypeStruct((4,) + upstay.shape[2:], BF)] * 4,
+        compiler_params=pltpu.CompilerParams(vmem_limit_bytes=VMEM_LIMIT),
+        name="merge",
+    )(upstay, upgot, downstay, downgot)
+
+
+def leave_kernel(
+    owner_ref, n1_ref, dq0_ref, dq1_ref, dk0_ref, dk1_ref, dv0_ref, dv1_ref, vec_ref, small_ref,
+    upstay_ref, upgot_ref, downstay_ref, downgot_ref, x_hbm, dh_hbm, weight_hbm, dwo_hbm,
+    dx_ref, grad_ref, total_ref,
+    x_ref, dh_ref, weight_ref, rows_ref,
+    dw_ref, near_ref, fromx_ref, fromy_ref, diagx_ref, diagy_ref, third_ref, zone_ref, done_ref,
+    pack_ref, side_ref, sums_ref,
+    near_sem, x_sem, y_sem, dx_sem, dy_sem, z_sem, grad_sem, side_sem, send_sem, local_sem,
+):
+    z, x, y, c = place()
+    m = 2 * y + c
+    d = 2 * z + x
+    n_dp = grad_ref.shape[0]
+    right_x, right_y, partner = at(z, 1 - x, y, c), at(z, x, 1 - y, c), at(z, x, y, 1 - c)
+    dp_peers = [((d + off) % n_dp, m) for off in range(1, n_dp)]
+    tokens, width = x_ref.shape
+    loads = []
+    for source, target in (
+        (dwo_hbm, dw_ref.at[3]), (x_hbm, x_ref), (dh_hbm, dh_ref), (weight_hbm, weight_ref)
+    ):
+        load = pltpu.make_async_copy(source, target, local_sem.at[len(loads)])
+        load.start()
+        loads.append(load)
+    greet(dp_peers + [right_y, partner])
+    mail = Mail(send_sem)
+    piece = pack_ref.at[0]
+    for kind, (stay_ref, got_ref) in enumerate(
+        ((upstay_ref, upgot_ref), (downstay_ref, downgot_ref))
+    ):
+        for off in (2, 1, 3, 0):
+            to = (z + off) % 4
+            third_ref[1 + kind, to] = added(stay_ref[to], got_ref[to])
+            if off:
+                mail.send(
+                    third_ref.at[1 + kind, to], zone_ref.at[1 + kind, z], z_sem.at[1 + kind, z],
+                    at(to, x, y, c), piece,
+                )
+
+    pairs = ((dq0_ref, dq1_ref), (dk0_ref, dk1_ref), (dv0_ref, dv1_ref))
+    half = width // PARTS
+    for index, pair in enumerate(pairs):
+        out = dw_ref.at[index].reshape(width, width)
+        for part, ref in enumerate(pair):
+            out[:, part * half : (part + 1) * half] = dot(n1_ref[...], ref[...], 1, 1).astype(BF)
+    loads[0].wait()
+    for step in range(2):
+        mail.send(
+            dw_ref.at[2 * step + 1 - c], near_ref.at[step], near_sem.at[step], partner,
+            near_ref.at[0],
+        )
+    for load in loads[1:]:
+        load.wait()
+    rows_ref[...] = jnp.zeros_like(rows_ref)
+    flat = [weight_ref.at[index].reshape(width, width) for index in range(3)]
+
+    def back(i, carry):
+        t = pl.ds(pl.multiple_of(i * TILE, TILE), TILE)
+        dn = jnp.zeros((TILE, width), F32)
+        for index, pair in enumerate(pairs):
+            for part, ref in enumerate(pair):
+                dn += dot(ref[:, t], flat[index][:, part * half : (part + 1) * half], 0, 1)
+        unit, scale = normed(x_ref[t, :].astype(F32))
+        dx_ref[t, :] = dh_ref[t, :] + norm_back(dn, unit, scale, vec_ref[0:1, :])
+        rows_ref[0:8, :] += fold_rows(dn * unit)
+        rows_ref[8:16, :] += fold_rows(dn)
+        return carry
+
+    lax.fori_loop(0, 1, back, 0)
+    for row in (0, 1):
+        arrived(near_ref.at[row], near_sem.at[row])
+
+        def summed(e, carry):
+            near_ref[row, e] = added(near_ref[row, e], dw_ref[2 * row + c, e])
+            return carry
+
+        lax.fori_loop(0, n_dp, summed, 0)
+    for part in range(2):
+        mail.send(
+            near_ref.at[1 - y, 2 * part + 1 - x], diagy_ref.at[part], dy_sem.at[part], right_y, piece
+        )
+        mail.send(
+            near_ref.at[1 - y, 2 * (2 + part) + 1 - x], diagx_ref.at[part], dx_sem.at[part],
+            right_x, piece,
+        )
+    for part in range(2):
+        mail.send(
+            near_ref.at[y, 2 * (2 + part) + 1 - x], fromx_ref.at[2 + part], x_sem.at[2 + part],
+            right_x, piece,
+        )
+        mail.send(near_ref.at[1 - y, 2 * part + x], fromy_ref.at[part], y_sem.at[part], right_y, piece)
+    lax.fori_loop(1, 3, back, 0)
+    for part in range(2):
+        arrived(diagy_ref.at[part], dy_sem.at[part])
+        e = 2 * part + 1 - x
+        diagy_ref[part] = added(near_ref[y, e], diagy_ref[part])
+        mail.send(diagy_ref.at[part], fromx_ref.at[part], x_sem.at[part], right_x, piece)
+        arrived(diagx_ref.at[part], dx_sem.at[part])
+        f = 2 * (2 + part) + x
+        diagx_ref[part] = added(near_ref[1 - y, f], diagx_ref[part])
+        mail.send(diagx_ref.at[part], fromy_ref.at[2 + part], y_sem.at[2 + part], right_y, piece)
+    lax.fori_loop(3, tokens // TILE, back, 0)
+
+    sums_ref[0] = small_ref[...]
+    sums_ref[0, 0:1, :] = jnp.sum(rows_ref[0:8, :], axis=0, keepdims=True)
+    sums_ref[0, 1:2, :] = jnp.sum(rows_ref[8:16, :], axis=0, keepdims=True)
+
+    def hop(index, peer):
+        mail.send(
+            sums_ref.at[index], side_ref.at[index], side_sem.at[index], peer, sums_ref.at[0]
+        )
+
+    def landed(index):
+        arrived(side_ref.at[index], side_sem.at[index])
+        sums_ref[index + 1] = sums_ref[index] + side_ref[index]
+
+    hop(0, partner)
+    for kind in (1, 2):
+        total = third_ref[kind, z].astype(F32)
+        for off in range(1, 4):
+            e = (z + off) % 4
+            arrived(zone_ref.at[kind, e], z_sem.at[kind, e])
+            total = total + zone_ref[kind, e].astype(F32)
+        done_ref[kind] = total.astype(BF)
+    landed(0)
+    hop(1, right_x)
+    for part in (2, 3, 0, 1):
+        arrived(fromx_ref.at[part], x_sem.at[part])
+        arrived(fromy_ref.at[part], y_sem.at[part])
+    for off in (2, 1, 3, 0):
+        to = (z + off) % 4
+        third_ref[0, to] = added(near_ref[y, 2 * to + x], fromx_ref[to], fromy_ref[to])
+        if off:
+            mail.send(
+                third_ref.at[0, to], zone_ref.at[0, z], z_sem.at[0, z], at(to, x, y, c), piece
+            )
+    landed(1)
+    hop(2, right_y)
+    landed(2)
+    for off in range(1, 4):
+        mail.send(
+            sums_ref.at[3], side_ref.at[3 + z], side_sem.at[3 + z], at((z + off) % 4, x, y, c),
+            sums_ref.at[0],
+        )
+    side_ref[3 + z] = sums_ref[3]
+    total = third_ref[0, z].astype(F32)
+    for off in range(1, 4):
+        e = (z + off) % 4
+        arrived(zone_ref.at[0, e], z_sem.at[0, e])
+        total = total + zone_ref[0, e].astype(F32)
+    done_ref[0] = total.astype(BF)
+    for off in (3, 4, 5, 2, 6, 1, 7):
+        e = (d + off) % n_dp
+        kind = jnp.where(owner_ref[m, 1] == e, 1, jnp.where(owner_ref[m, 2] == e, 2, 0))
+        pack_ref[e] = done_ref[kind]
+        mail.send(pack_ref.at[e], grad_ref.at[d], grad_sem.at[d], (e, m), piece)
+    kind = jnp.where(owner_ref[m, 1] == d, 1, jnp.where(owner_ref[m, 2] == d, 2, 0))
+    grad_ref[d] = done_ref[kind]
+    for off in range(1, 4):
+        e = (z + off) % 4
+        arrived(side_ref.at[3 + e], side_sem.at[3 + e])
+    total_ref[...] = (side_ref[3] + side_ref[4]) + (side_ref[5] + side_ref[6])
+    for off in range(1, n_dp):
+        e = (d + off) % n_dp
+        arrived(grad_ref.at[e], grad_sem.at[e])
+    mail.finish()
+
+
+def leave(owner, x, dh, n1, flows, vec, weights, dwo, small, rest):
+    tokens, width = x.shape
+    n_mlp, n_dp, share, _ = weights.shape
+    smem = pl.BlockSpec(memory_space=pltpu.SMEM)
+    vmem = pl.BlockSpec(memory_space=pltpu.VMEM)
+    hbm = pl.BlockSpec(memory_space=pl.ANY)
+    dma = pltpu.SemaphoreType.DMA
+    part = lambda *lead: pltpu.VMEM(lead + (share, width), BF)
+    flat = [ref for pair in flows for ref in pair]
+    return pl.pallas_call(
+        leave_kernel,
+        in_specs=[smem] + [vmem] * 13 + [hbm] * 4,
+        out_specs=[vmem] * 3,
+        out_shape=[
+            jax.ShapeDtypeStruct((tokens, width), F32),
+            jax.ShapeDtypeStruct((n_dp, share, width), BF),
+            jax.ShapeDtypeStruct(small.shape, F32),
+        ],
+        scratch_shapes=[
+            pltpu.VMEM((tokens, width), BF),
+            pltpu.VMEM((tokens, width), F32),
+            part(n_mlp, n_dp),
+            pltpu.VMEM((16, width), F32),
+            part(n_mlp, n_dp), part(2, n_dp), part(4), part(4), part(2), part(2), part(3, 4),
+            part(3, 4), part(3), part(n_dp),
+            pltpu.VMEM((7,) + small.shape, F32),
+            pltpu.VMEM((4,) + small.shape, F32),
+            dma((2,)), dma((4,)), dma((4,)), dma((2,)), dma((2,)), dma((3, 4)),
+            dma((n_dp,)), dma((7,)), dma((48,)), dma((4,)),
+        ],
+        compiler_params=pltpu.CompilerParams(
+            vmem_limit_bytes=VMEM_LIMIT, collective_id=2, has_side_effects=True
+        ),
+        name="leave",
+    )(
+        owner, n1, *flat, vec, small, *rest, x, dh, weights,
+        dwo.reshape(n_dp, share, width),
+    )
 
 
 def halves(values):
@@ -534,55 +1217,79 @@
     share = width // n_dp
     owner_row = jnp.take(owner, mlp_index, axis=0)
     holds = owner_row == dp_index
+    owns = jnp.any(holds).astype(jnp.int32).reshape(1)
     master = master_slots[0, 0]
-    pieces = lax.all_to_all(master.astype(BF).reshape(n_dp, share, width), "dp", 0, 0, tiled=True)
-    mine = jnp.take(pieces, owner_row, axis=0)
-    every = lax.all_gather(mine[None], ("dp", "mlp"), axis=0, tiled=True)
-    blocks = every.reshape(n_dp, n_mlp, 3, share, width).transpose(2, 1, 0, 3, 4)
-    blocks = blocks.reshape(3, n_mlp, width, width)
-    attention = blocks[0]
+    slot = master.astype(BF).reshape(n_dp, share, width)
     turned = vectors.T
     pos = positions(segment, grid_height, grid_width, patch_rows, patch_cols)
-    n1t, q, k, v, cosine, sine, qmark, kmark = project(tokens, pos, vectors, turned, attention)
+    direct = n_dp == 8 and n_mlp == 4
+    if direct:
+        n1t, q, k, v, cosine, sine, qmark, kmark, attention, zone = enter(
+            owner, slot, tokens, pos, vectors, turned
+        )
+        over_x = [(i, i ^ 1) for i in range(n_dp)]
+        over_y = [(i, i ^ 2) for i in range(n_mlp)]
+        xzone = lax.ppermute(zone, "dp", over_x)
+        yzone = lax.ppermute(zone, "mlp", over_y)
+    else:
+        pieces = lax.all_to_all(slot, "dp", 0, 0, tiled=True)
+        mine = jnp.take(pieces, owner_row, axis=0)
+        every = lax.all_gather(mine[None], ("dp", "mlp"), axis=0, tiled=True)
+        blocks = every.reshape(n_dp, n_mlp, 3, share, width).transpose(2, 1, 0, 3, 4)
+        attention, up, down = blocks.reshape(3, n_mlp, width, width)
+        n1t, q, k, v, cosine, sine, qmark, kmark = project(tokens, pos, vectors, turned, attention)
     o, log_totals = attend(grid_height, grid_width, q, k, v, qmark, kmark)
-    output, dh, do, dwo, dup, ddown, mid_rows, dc = middle_part(
-        tokens, cotangent, o, vectors, attention[3], blocks[1], blocks[2]
-    )
-    dq, dk, dv, freq, bias = attend_back(
-        grid_height, grid_width, q, k, v, qmark, kmark, log_totals, do, pos, cosine, sine
-    )
-    input_grad, dwqkv, fin_rows = final_part(tokens, dh, n1t, dq, dk, dv, vectors, attention)
-
-    attention_grads = jnp.concatenate([dwqkv, dwo[None]], axis=0)
-    grads = jnp.stack([attention_grads, dup, ddown], axis=1)
-    grads = grads.reshape(n_mlp, 3, n_dp, share, width).transpose(2, 0, 1, 3, 4)
-    grads = grads.reshape(n_dp * n_mlp * 3, share, width)
-    reduced = lax.psum_scatter(grads, ("dp", "mlp"), scatter_dimension=0, tiled=True)
-    takers = owner_row[None, :] == jnp.arange(n_dp, dtype=jnp.int32)[:, None]
-    kind_of = jnp.sum(jnp.where(takers, jnp.arange(3, dtype=jnp.int32)[None, :], 0), axis=1)
-    gradient = lax.all_to_all(jnp.take(reduced, kind_of, axis=0), "dp", 0, 0, tiled=True)
+    fine = (n_mlp, n_dp, share, width)
+    back = functools.partial(attend_back, grid_height, grid_width)
+    if direct:
+        output, dh, do, dwo, mid_rows, dc, upgo, upstay, downgo, downstay = center(
+            tokens, cotangent, o, vectors, attention, zone, xzone, yzone
+        )
+        upgot = lax.ppermute(upgo, "dp", over_x)
+        downgot = lax.ppermute(downgo, "mlp", over_y)
+        first = back(q, k, v, qmark, kmark, log_totals, do, pos, cosine, sine, 0)
+        first, upgot, downgot = lax.optimization_barrier((first, upgot, downgot))
+        upgo, upstay, downgo, downstay = merge(upstay, upgot, downstay, downgot)
+        upgot = lax.ppermute(upgo, "mlp", over_y)
+        downgot = lax.ppermute(downgo, "dp", over_x)
+        do, upstay, downstay = lax.optimization_barrier((do, upstay, downstay))
+    else:
+        output, dh, do, dwo, dup, ddown, mid_rows, dc = middle_part(
+            tokens, cotangent, o, vectors, attention[3], up, down
+        )
+        first = back(q, k, v, qmark, kmark, log_totals, do, pos, cosine, sine, 0)
+    second = back(q, k, v, qmark, kmark, log_totals, do, pos, cosine, sine, 1)
+    both = list(zip(first, second))
+    freq = jnp.concatenate(both[3], axis=1)[0:2].reshape(1, width)
+    bias = jnp.concatenate(both[4], axis=1)[0::8]
+    eights = lambda rows: jnp.sum(rows.reshape(-1, 8, width), axis=1)
+    mid = eights(mid_rows)
+    tail = [bias, mid[0:3], dc[:, 0, :], mid[3:4], freq]
+    if direct:
+        small = jnp.concatenate([jnp.zeros((2, width), F32)] + tail, axis=0)
+        input_grad, gradient, total = leave(
+            owner, tokens, dh, n1t, both[0:3], vectors, attention.reshape(fine), dwo, small,
+            (upstay, upgot, downstay, downgot),
+        )
+    else:
+        dq, dk, dv = (jnp.concatenate(pair, axis=0) for pair in both[0:3])
+        input_grad, datt, fin_rows = final_part(
+            tokens, dh, n1t, dq, dk, dv, vectors, attention, dwo
+        )
+        grads = jnp.stack([datt, dup, ddown], axis=1)
+        grads = grads.reshape(n_mlp, 3, n_dp, share, width).transpose(2, 0, 1, 3, 4)
+        grads = grads.reshape(n_dp * n_mlp * 3, share, width)
+        reduced = lax.psum_scatter(grads, ("dp", "mlp"), scatter_dimension=0, tiled=True)
+        takers = owner_row[None, :] == jnp.arange(n_dp, dtype=jnp.int32)[:, None]
+        kind_of = jnp.sum(jnp.where(takers, jnp.arange(3, dtype=jnp.int32)[None, :], 0), axis=1)
+        gradient = lax.all_to_all(jnp.take(reduced, kind_of, axis=0), "dp", 0, 0, tiled=True)
+        total = lax.psum(jnp.concatenate([eights(fin_rows)] + tail, axis=0), ("dp", "mlp"))
     gradient = gradient.reshape(width, width)
-    owns = jnp.any(holds).astype(jnp.int32).reshape(1)
     slot_grad, left_out, right_out, master_out = update(
         owns, decays, gradient, left_slots[0, 0], right_slots[0, 0], left_roots[0, 0],
         right_roots[0, 0], master,
     )
 
-    eights = lambda rows: jnp.sum(rows.reshape(-1, 8, width), axis=1)
-    fin = eights(fin_rows)
-    mid = eights(mid_rows)
-    local_vectors = jnp.concatenate(
-        [
-            fin,
-            bias[0::8],
-            mid[0:3],
-            dc[:, 0, :],
-            mid[3:4],
-            freq[0:2].reshape(1, width),
-        ],
-        axis=0,
-    )
-    total = lax.psum(local_vectors, ("dp", "mlp"))
     cut = width // n_mlp
     own = lambda table: lax.dynamic_slice_in_dim(table, mlp_index * cut, cut, 1)
     grad_share = own(total)

time: 602 us -> 377 us (0.63)
  the two profiles are of different devices: /device:TPU:0 before, /device:TPU:20 now
where the time goes in v2:
time: 377 us; the launch traced here: 374 us
  Pallas kernels  343 us (91%)
  local copies, waits for them, and re-layouts  11.1 us (3%)
  other arithmetic  8.61 us (2%)
  starting transfers between devices  6.73 us (2%)
    pallas_call x1, Pallas kernels, leave(): pl.pallas_call(leave_kernel, in_specs=[smem] + [vmem] * 13 + [hbm] * 4, o...  85.5 us
    pallas_call x1, Pallas kernels, enter(): pl.pallas_call(enter_kernel, in_specs=[smem, hbm, vmem, vmem, vmem, vmem]...  79.1 us
    pallas_call x1, Pallas kernels, center(): pl.pallas_call(center_kernel, in_specs=[vmem] * 4 + [hbm] * 4, out_specs=...  73.2 us
    pallas_call x2, Pallas kernels, attend_back(): pl.pallas_call(attend_back_kernel, grid=(1,), in_specs=[smem, smem, cut(q...  50.3 us
    pallas_call x1, Pallas kernels, attend(): pl.pallas_call(attend_kernel, in_specs=[smem, smem] + [vmem] * 5, out_spe...  28.8 us
    pallas_call x1, Pallas kernels, update(): pl.pallas_call(update_kernel, in_specs=[smem, smem] + [vmem] * 6, out_spe...  21.9 us
    unnamed x42, local copies, waits for them, and re-layouts  8.5 us
  transfers between devices with their start and end apart: 6, of which 2 were waited for; matrix products, arithmetic and copies ran while one was open for 1% of the time, Pallas kernels for 21%

profile of v2, /device:TPU:20, one launch (start us, length us, event | category | flops | bytes accessed | tf_op | source)
XLA Modules:
  0.0 374.0 jit_solution(17765055415247393338)
XLA Ops:
  0.6 0.7 convert_element_type.29
  1.3 0.0 copy-start.16
  1.4 0.0 copy-start.17
  1.4 2.9 convert_element_type.23
  4.2 0.9 copy.27
  5.2 0.0 copy-done.12
  5.2 0.0 copy-done.15
  5.2 0.1 select_reduce_fusion
  5.3 0.6 stack.19.pos_ref
  6.0 79.1 %enter.1 = (bf16[768,1024]{1,0:T(8,128)(2,1)}, bf16[768,1024]{1,0:T(8,128)(2,1)}, bf16[768,1024]{1,0:T(8,128)(2,1)}, bf16[768,1024]{1,0:T(8,128)(2,1)}, f32[384,...) custom-call(s32[4,3]{1,0:T(4,128)} %owner_ref.3, ...), custom_call_target="tpu_custom_call" | custom-call | tf_op jit(solution)/shard_map/enter/pallas_call | solution.py:244
  85.1 1.6 collective-permute-start
  86.6 0.5 collective-permute-start.1
  87.2 28.8 %attend.1 = (bf16[768,1024]{1,0:T(8,128)(2,1)}, f32[96,1024]{1,0:T(8,128)}) custom-call(s32[4]{0:T(128)} %height_ref.5, s32[4]{0:T(128)} %width_ref.5, bf16[768,1024]{1,0:T(8,128)(2,1)} %get-tuple-element.62.q_ref, bf16[768,1024]{1,0:T(8,128)(2,1)} %get-tuple-element.63.k_ref, bf16[768,1024]{1,0:T(8,128)(2,1)} %get-tuple-element.64.v_ref, ...), custom_call_target="tpu_custom_call" | custom-call | tf_op jit(solution)/shard_map/attend/pallas_call | solution.py:392
  116.0 0.0 collective-permute-done.xzone_ref
  116.0 0.0 collective-permute-done.1.yzone_ref
  116.0 0.0 copy-start.3
  116.0 1.0 copy-done.2
  117.0 0.4 copy-done.3
  117.4 73.2 %center.1 = (bf16[1024,768]{1,0:T(8,128)(2,1)}, f32[1024,768]{1,0:T(8,128)}, bf16[768,1024]{1,0:T(8,128)(2,1)}, bf16[768,768]{1,0:T(8,128)(2,1)}, f32[32,768]{1,...) custom-call(bf16[1024,768]{1,0:T(8,128)(2,1)} %x_hbm.1, ...), custom_call_target="tpu_custom_call" | custom-call | tf_op jit(solution)/shard_map/center/pallas_call | solution.py:868
  190.6 1.2 collective-permute-start.2
  191.8 0.9 collective-permute-start.3
  192.7 24.9 %attend_back.2 = (bf16[384,1024]{1,0:T(8,128)(2,1)}, bf16[384,1024]{1,0:T(8,128)(2,1)}, bf16[384,1024]{1,0:T(8,128)(2,1)}, f32[8,192]{1,0:T(8,128)}, f32[24,384]{1,0:T(8,128)}) custom-call(s32[4]{0:T(128)} %height_ref.5, s32[4]{0:T(128)} %width_ref.5, bf16[768,1024]{1,0:T(8,128)(2,1)} %get-tuple-element.62.q_ref, bf16[768,1024]{1,0:T(8,128)(2,1)} %get-tuple-element.63.k_ref, ...), custom_call_target="tpu_custom_call" | custom-call | tf_op jit(solution)/shard_map/attend_back/pallas_call | solution.py:498
  217.6 1.8 collective-permute-done.2.upgot_ref
  219.4 0.5 collective-permute-done.3.downgot_ref
  219.9 0.5 copy-done.4
  220.4 0.5 copy-done.5
  220.9 4.3 %merge.1 = (bf16[4,96,768]{2,1,0:T(8,128)(2,1)}, bf16[4,96,768]{2,1,0:T(8,128)(2,1)}, bf16[4,96,768]{2,1,0:T(8,128)(2,1)}, bf16[4,96,768]{2,1,0:T(8,128)(2,1)}) custom-call(bf16[2,4,96,768]{3,2,1,0:T(8,128)(2,1)} %get-tuple-element.84.upstay_ref, bf16[2,4,96,768]{3,2,1,0:T(8,128)(2,1)} %copy-done.4, bf16[8,96,768]{2,1,0:T(8,128)(2,1)} %get-tuple-element.86.downstay_ref, ...), custom_call_target="tpu_custom_call" | custom-call | tf_op jit(solution)/shard_map/merge/pallas_call | solution.py:924
  225.2 1.4 collective-permute-start.4
  226.6 1.1 collective-permute-start.5
  227.7 1.3 compare_reduce_fusion
  229.7 0.0 copy-done.18
  229.7 0.6 slice.23
  231.0 0.0 copy-start.13
  231.0 25.4 %attend_back.3 = (bf16[384,1024]{1,0:T(8,128)(2,1)}, bf16[384,1024]{1,0:T(8,128)(2,1)}, bf16[384,1024]{1,0:T(8,128)(2,1)}, f32[8,192]{1,0:T(8,128)}, f32[24,384]{1,0:T(8,128)}) custom-call(s32[4]{0:T(128)} %height_ref.5, s32[4]{0:T(128)} %width_ref.5, bf16[768,1024]{1,0:T(8,128)(2,1)} %get-tuple-element.62.q_ref, bf16[768,1024]{1,0:T(8,128)(2,1)} %get-tuple-element.63.k_ref, ...), custom_call_target="tpu_custom_call" | custom-call | tf_op jit(solution)/shard_map/attend_back/pallas_call | solution.py:498
  256.4 0.8 fusion.1
  257.2 0.8 pad_maximum_fusion
  258.0 1.3 concatenate.11.small_ref
  259.2 0.0 collective-permute-done.4.upgot_ref
  259.2 0.0 collective-permute-done.5.downgot_ref
  259.2 0.8 copy-done.7
  260.1 0.2 copy-done.8
  260.2 85.5 %leave.1 = (f32[1024,768]{1,0:T(8,128)}, bf16[8,96,768]{2,1,0:T(8,128)(2,1)}, f32[14,768]{1,0:T(8,128)}) custom-call(s32[4,3]{1,0:T(4,128)} %owner_ref.3, bf16[768,1024]{1,0:T(8,128)(2,1)} %get-tuple-element.71.n1_ref, bf16[384,1024]{1,0:T(8,128)(2,1)} %get-tuple-element.83.dq0_ref, bf16[384,1024]{1,0:T(8,128)(2,1)} %get-tuple-element.91.dq1_ref, ...), custom_call_target="tpu_custom_call" | custom-call | tf_op jit(solution)/shard_map/leave/pallas_call | solution.py:1110
  345.7 2.1 divide_subtract_fusion
  347.8 21.9 %update.1 = (f32[768,768]{1,0:T(8,128)}, f32[768,768]{1,0:T(8,128)}, f32[768,768]{1,0:T(8,128)}, f32[768,768]{1,0:T(8,128)}) custom-call(s32[1]{0:T(128)} %bitcast.8.keep_ref, f32[2]{0:T(128)} %decay_ref.1, bf16[768,768]{1,0:T(8,128)(2,1)} %bitcast.35, f32[768,768]{1,0:T(8,128)} %bitcast.29, f32[768,768]{1,0:T(8,128)} %bitcast.30, f32[768,768]{1,0:T(8,128)} %bitcast.31, ...), custom_call_target="tpu_custom_call" | custom-call | tf_op jit(solution)/shard_map/update/pallas_call | solution.py:1187
  369.7 0.0 copy-done.1
  369.7 1.1 copy.32
  370.8 1.3 copy-done
  372.1 1.7 copy.33
  (33 shorter events, 0.2 us)
Async XLA Ops:
  1.3 2.9 copy-start.6
  1.3 3.8 %copy-start.12 = (s32[1024]{0:T(1024)S(1)}, s32[1024]{0:T(1024)}, u32[]{:S(2)}) copy-start(s32[1024]{0:T(1024)} %param.31) | copy-start | bytes 12292
  1.3 3.8 %copy-start.14 = (s32[4]{0:T(128)S(1)}, s32[4]{0:T(128)}, u32[]{:S(2)}) copy-start(s32[4]{0:T(128)} %height_ref.5) | copy-start | bytes 52
  1.3 3.8 %copy-start.15 = (s32[4]{0:T(128)S(1)}, s32[4]{0:T(128)}, u32[]{:S(2)}) copy-start(s32[4]{0:T(128)} %width_ref.5) | copy-start | bytes 52
  1.3 3.9 %copy-start.16 = (s32[1024]{0:T(1024)S(1)}, s32[1024]{0:T(1024)}, u32[]{:S(2)}) copy-start(s32[1024]{0:T(1024)} %param.29) | copy-start | bytes 12292
  1.4 3.9 %copy-start.17 = (s32[1024]{0:T(1024)S(1)}, s32[1024]{0:T(1024)}, u32[]{:S(2)}) copy-start(s32[1024]{0:T(1024)} %param.30) | copy-start | bytes 12292
  85.1 30.9 %collective-permute-start = (bf16[2,4,96,768]{3,2,1,0:T(8,128)(2,1)}, bf16[2,4,96,768]{3,2,1,0:T(8,128)(2,1)S(1)}, u32[]{:S(2)}, u32[]{:S(2)}) collective-permute-start(bf16[2,4,96,768]{3,2,1,0:T(8,128)(2,1)} %get-tuple-element.69.zone_ref), channel_id=1, source_target_pairs={{0,4},{4,0},{8,12},{12,8},{16,20},{20,16},{24,28},{28,24},{1,5},{5... | collective-permute-start | bytes 3538952 | tf_op jit(solution)/shard_map/ppermute | solution.py:1232
  86.6 29.4 %collective-permute-start.1 = (bf16[2,4,96,768]{3,2,1,0:T(8,128)(2,1)}, bf16[2,4,96,768]{3,2,1,0:T(8,128)(2,1)S(1)}, u32[]{:S(2)}, u32[]{:S(2)}) collective-permute-start(bf16[2,4,96,768]{3,2,1,0:T(8,128)(2,1)} %get-tuple-element.69.zone_ref), channel_id=1, source_target_pairs={{0,2},{1,3},{2,0},{3,1},{4,6},{5,7},{6,4},{7,5},{8,10},{9,11},{10,... | collective-permute-start | bytes 3538952 | tf_op jit(solution)/shard_map/ppermute | solution.py:1233
  116.0 1.0 copy-start.2
  116.0 1.4 copy-start.3
  190.6 28.8 %collective-permute-start.2 = (bf16[2,4,96,768]{3,2,1,0:T(8,128)(2,1)}, bf16[2,4,96,768]{3,2,1,0:T(8,128)(2,1)S(1)}, u32[]{:S(2)}, u32[]{:S(2)}) collective-permute-start(bf16[2,4,96,768]{3,2,1,0:T(8,128)(2,1)} %get-tuple-element.81), channel_id=1, source_target_pairs={{0,4},{4,0},{8,12},{12,8},{16,20},{20,16},{24,28},{28,24},{1,5},{5... | collective-permute-start | bytes 3538952 | tf_op jit(solution)/shard_map/ppermute | solution.py:1248
  191.8 28.1 %collective-permute-start.3 = (bf16[8,96,768]{2,1,0:T(8,128)(2,1)}, bf16[8,96,768]{2,1,0:T(8,128)(2,1)S(1)}, u32[]{:S(2)}, u32[]{:S(2)}) collective-permute-start(bf16[8,96,768]{2,1,0:T(8,128)(2,1)} %get-tuple-element.82), channel_id=1, source_target_pairs={{0,2},{1,3},{2,0},{3,1},{4,6},{5,7},{6,4},{7,5},{8,10},{9,11},{10,... | collective-permute-start | bytes 3538952 | tf_op jit(solution)/shard_map/ppermute | solution.py:1249
  219.4 1.0 copy-start.4
  219.9 1.0 copy-start.5
  220.9 8.8 %copy-start.18 = (f32[2]{0:T(128)S(1)}, f32[2]{0:T(128)}, u32[]{:S(2)}) copy-start(f32[2]{0:T(128)} %decay_ref.1) | copy-start | bytes 28
  220.9 10.0 %copy-start.10 = (f32[4,8,768]{2,1,0:T(8,128)S(1)}, f32[4,8,768]{2,1,0:T(8,128)}, u32[]{:S(2)}) copy-start(f32[4,8,768]{2,1,0:T(8,128)} %get-tuple-element.99) | copy-start | bytes 294916
  220.9 10.0 %copy-start.9 = (f32[32,768]{1,0:T(8,128)S(1)}, f32[32,768]{1,0:T(8,128)}, u32[]{:S(2)}) copy-start(f32[32,768]{1,0:T(8,128)} %get-tuple-element.98) | copy-start | bytes 294916
  225.2 34.0 %collective-permute-start.4 = (bf16[4,96,768]{2,1,0:T(8,128)(2,1)}, bf16[4,96,768]{2,1,0:T(8,128)(2,1)S(1)}, u32[]{:S(2)}, u32[]{:S(2)}) collective-permute-start(bf16[4,96,768]{2,1,0:T(8,128)(2,1)} %get-tuple-element.103), channel_id=1, source_target_pairs={{0,2},{1,3},{2,0},{3,1},{4,6},{5,7},{6,4},{7,5},{8,10},{9,11},{10,... | collective-permute-start | bytes 1769480 | tf_op jit(solution)/shard_map/ppermute | solution.py:1253
  226.6 32.6 %collective-permute-start.5 = (bf16[4,96,768]{2,1,0:T(8,128)(2,1)}, bf16[4,96,768]{2,1,0:T(8,128)(2,1)S(1)}, u32[]{:S(2)}, u32[]{:S(2)}) collective-permute-start(bf16[4,96,768]{2,1,0:T(8,128)(2,1)} %get-tuple-element.105), channel_id=1, source_target_pairs={{0,4},{4,0},{8,12},{12,8},{16,20},{20,16},{24,28},{28,24},{1,5},{5... | collective-permute-start | bytes 1769480 | tf_op jit(solution)/shard_map/ppermute | solution.py:1254
  231.0 25.4 %copy-start.13 = (f32[8,192]{1,0:T(8,128)S(1)}, f32[8,192]{1,0:T(8,128)}, u32[]{:S(2)}) copy-start(f32[8,192]{1,0:T(8,128)} %get-tuple-element.100) | copy-start | bytes 18436
  231.0 26.2 %copy-start.11 = (f32[24,384]{1,0:T(8,128)S(1)}, f32[24,384]{1,0:T(8,128)}, u32[]{:S(2)}) copy-start(f32[24,384]{1,0:T(8,128)} %get-tuple-element.96) | copy-start | bytes 110596
  259.2 0.8 copy-start.7
  259.2 1.0 copy-start.8
  347.8 21.9 %copy-start.1 = (bf16[1024,768]{1,0:T(8,128)(2,1)S(1)}, bf16[1024,768]{1,0:T(8,128)(2,1)}, u32[]{:S(2)}) copy-start(bf16[1024,768]{1,0:T(8,128)(2,1)} %get-tuple-element.142) | copy-start | bytes 4718596
  369.7 2.5 copy-start

commit v3 on v2

--- a/solution.py
+++ b/solution.py
@@ -19,6 +19,7 @@
 BLOCK = 128
 TILE = 256
 PARTS = 2
+WINDOW = 6
 F32 = jnp.float32
 BF = jnp.bfloat16
 VMEM_LIMIT = 60 * 1024 * 1024
@@ -103,24 +104,28 @@
 
 
 def enter_kernel(
-    owner_ref, slot_ref, x_ref, pos_ref, vec_ref, turned_ref,
+    owner_ref, slot_hbm, x_ref, pos_ref, vec_ref, turned_ref,
     n1_ref, q_ref, k_ref, v_ref, cos_ref, sin_ref, qmark_ref, kmark_ref, weight_ref, zone_ref,
-    land_ref, mine_ref, att_ref, zland_ref,
-    land_sem, zone_sem, att_sem, send_sem, local_sem,
+    raw_ref, slot_ref, cross_ref, chain_ref, att_ref, zland_ref,
+    cross_sem, chain_sem, relay_sem, att_sem, send_sem, local_sem,
 ):
     z, x, y, c = place()
     m = 2 * y + c
-    d = 2 * z + x
-    n_dp = land_ref.shape[0]
+    n_dp = slot_ref.shape[0]
     right_x, right_y, partner = at(z, 1 - x, y, c), at(z, x, 1 - y, c), at(z, x, y, 1 - c)
-    dp_peers = [((d + off) % n_dp, m) for off in range(1, n_dp)]
-    greet(dp_peers + [right_y, partner])
+    own = pltpu.make_async_copy(slot_hbm, raw_ref, local_sem.at[0])
+    own.start()
+    greet([right_x, right_y, partner, at((z + 1) % 4, x, y, c), at((z + 3) % 4, x, y, c)])
     mail = Mail(send_sem)
-    piece = mine_ref.at[0]
-    own = pltpu.make_async_copy(slot_ref.at[d], land_ref.at[d], local_sem.at[0])
-    own.start()
-    for peer in dp_peers:
-        mail.send(slot_ref.at[peer[0]], land_ref.at[d], land_sem.at[d], peer, piece)
+    piece = slot_ref.at[0]
+    own.wait()
+    for part in range(4):
+        e = 2 * part + 1 - x
+        slot_ref[e] = raw_ref[e].astype(BF)
+        mail.send(slot_ref.at[e], cross_ref.at[part], cross_sem.at[part], right_x, piece)
+    for part in range(4):
+        e = 2 * part + x
+        slot_ref[e] = raw_ref[e].astype(BF)
 
     tokens = x_ref.shape[0]
     half = cos_ref.shape[0]
@@ -140,37 +145,98 @@
         kmark_ref[:, t] = jnp.where(row == seg, 0.0, MASK_SHIFT).astype(BF)
         return carry
 
-    lax.fori_loop(0, tiles, prepare, 0)
-
-    own.wait()
-    for off in range(1, n_dp):
-        source = (d + off) % n_dp
-        arrived(land_ref.at[source], land_sem.at[source])
-    for kind in range(3):
-        mine_ref[kind] = land_ref[owner_ref[m, kind]]
-
-    def spread_z(source, target, sem):
-        for off in range(1, 4):
-            mail.send(source, target, sem, at((z + off) % 4, x, y, c), piece)
-
-    spread_z(mine_ref.at[0], att_ref.at[m, d], att_sem.at[m, d])
-    for peer in (right_x, right_y, partner):
-        mail.send(mine_ref.at[0], att_ref.at[m, d], att_sem.at[m, d], peer, piece)
-    keep = pltpu.make_async_copy(mine_ref.at[0], att_ref.at[m, d], local_sem.at[1])
-    keep.start()
-    for off in (1, 3, 2):
-        e = 2 * ((z + off) % 4) + x
-        arrived(att_ref.at[m, e], att_sem.at[m, e])
+    lax.fori_loop(0, tiles // 2, prepare, 0)
+
+    edge = z % 3 == 0
+    inner = z % 3 != 0
+    far = z // 2
+    near = 1 - far
+
+    def relay(direction, kind, part):
+        ref = chain_ref.at[direction, kind, part]
+        return pltpu.make_async_remote_copy(
+            src_ref=ref,
+            dst_ref=ref,
+            send_sem=relay_sem.at[direction, kind, part],
+            recv_sem=chain_sem.at[direction, kind, part],
+            device_id=at(z + 1 - 2 * direction, x, y, c),
+            device_id_type=pl.DeviceIdType.MESH,
+        )
+
+    def merged(direction, kind, part, opening):
+        ref = chain_ref.at[direction, kind, part]
+        home = owner_ref[m, kind]
+        value = lax.select(home % 2 == x, slot_ref[2 * part + x], cross_ref[part])
+        if not opening:
+            arrived(ref, chain_sem.at[direction, kind, part])
+            value = lax.select(home // 2 == z, value, ref[...])
+        ref[...] = value
+
+    def crossed(part):
+        arrived(cross_ref.at[part], cross_sem.at[part])
+
+    def outward(kind, part):
+        merged(far, kind, part, False)
+        relay(far, kind, part).start()
+
+    def inward(kind, part):
+        merged(near, kind, part, False)
+
+        @pl.when(inner)
+        def _():
+            relay(near, kind, part).start()
+
+        return lax.select(
+            owner_ref[m, kind] // 2 <= z, chain_ref[0, kind, part], chain_ref[1, kind, part]
+        )
+
+    def bring(part):
+        e = 2 * part + x
+        att_ref[m, e] = inward(0, part)
         for peer in (right_x, right_y, partner):
             mail.send(att_ref.at[m, e], att_ref.at[m, e], att_sem.at[m, e], peer, piece)
-    keeps = []
-    for kind in range(2):
-        spread_z(mine_ref.at[1 + kind], zland_ref.at[kind, z], zone_sem.at[kind, z])
-        copy = pltpu.make_async_copy(
-            mine_ref.at[1 + kind], zland_ref.at[kind, z], local_sem.at[2 + kind]
-        )
-        copy.start()
-        keeps.append(copy)
+
+    @pl.when(edge)
+    def _():
+        def opening(part, carry):
+            crossed(part)
+            merged(far, 0, part, True)
+            relay(far, 0, part).start()
+            return carry
+
+        lax.fori_loop(0, 4, opening, 0)
+
+        def rest(s, carry):
+            merged(far, 1 + s // 4, s % 4, True)
+            relay(far, 1 + s // 4, s % 4).start()
+            return carry
+
+        lax.fori_loop(0, 8, rest, 0)
+
+    def early(part):
+        @pl.when(inner)
+        def _():
+            crossed(part)
+            outward(0, part)
+
+    early(0)
+    early(1)
+    bring(0)
+    early(2)
+    bring(1)
+    early(3)
+    bring(2)
+    bring(3)
+    lax.fori_loop(tiles // 2, tiles, prepare, 0)
+
+    def ahead(s):
+        @pl.when(inner)
+        def _():
+            outward(1 + s // 4, s % 4)
+
+    def keep(s):
+        zland_ref[s // 4, s % 4] = inward(1 + s // 4, s % 4)
+
     m_y = 2 * (1 - y) + c
     for part in range(4):
         e = 2 * part + 1 - x
@@ -183,6 +249,9 @@
         if part >= 2:
             mail.send(att_ref.at[m_y, f], att_ref.at[m_y, f], att_sem.at[m_y, f], right_x, piece)
         mail.send(att_ref.at[m_y, f], att_ref.at[m_y, f], att_sem.at[m_y, f], partner, piece)
+        ahead(part)
+        if part:
+            keep(part - 1)
     for part in range(4):
         e = 2 * part + 1 - x
         arrived(att_ref.at[m_y, e], att_sem.at[m_y, e])
@@ -191,8 +260,7 @@
         other = 2 * step + 1 - c
         for e in range(n_dp):
             arrived(att_ref.at[other, e], att_sem.at[other, e])
-    keep.wait()
-    out = pltpu.make_async_copy(att_ref, weight_ref, local_sem.at[4])
+    out = pltpu.make_async_copy(att_ref, weight_ref, local_sem.at[1])
     out.start()
 
     part = half // HEADS
@@ -202,6 +270,8 @@
         return att_ref[index].reshape(width, width)
 
     def rotate(i, carry):
+        ahead(4 + i)
+        keep(3 + i)
         t = pl.ds(pl.multiple_of(i * TILE, TILE), TILE)
         n1t = n1_ref[:, t]
         cosine = cos_ref[:, t]
@@ -220,16 +290,20 @@
         return carry
 
     lax.fori_loop(0, tiles, rotate, 0)
-    for kind in range(2):
-        keeps[kind].wait()
-        for off in range(1, 4):
-            e = (z + off) % 4
-            arrived(zland_ref.at[kind, e], zone_sem.at[kind, e])
-    last_out = pltpu.make_async_copy(zland_ref, zone_ref, local_sem.at[5])
+    keep(7)
+    last_out = pltpu.make_async_copy(zland_ref, zone_ref, local_sem.at[2])
     last_out.start()
+    mail.finish()
+    for kind in range(3):
+        for step in range(4):
+            arrived(piece, relay_sem.at[far, kind, step])
+
+            @pl.when(inner)
+            def _():
+                arrived(piece, relay_sem.at[near, kind, step])
+
     out.wait()
     last_out.wait()
-    mail.finish()
 
 
 def enter(owner, slot, x, pos, vec, turned):
@@ -253,15 +327,18 @@
             jax.ShapeDtypeStruct((2, 4, share, width), BF),
         ],
         scratch_shapes=[
+            pltpu.VMEM((n_dp, share, width), F32),
             pltpu.VMEM((n_dp, share, width), BF),
-            pltpu.VMEM((3, share, width), BF),
+            pltpu.VMEM((4, share, width), BF),
+            pltpu.VMEM((2, 3, 4, share, width), BF),
             pltpu.VMEM((n_mlp, n_dp, share, width), BF),
             pltpu.VMEM((2, 4, share, width), BF),
-            pltpu.SemaphoreType.DMA((n_dp,)),
-            pltpu.SemaphoreType.DMA((2, 4)),
+            pltpu.SemaphoreType.DMA((4,)),
+            pltpu.SemaphoreType.DMA((2, 3, 4)),
+            pltpu.SemaphoreType.DMA((2, 3, 4)),
             pltpu.SemaphoreType.DMA((n_mlp, n_dp)),
-            pltpu.SemaphoreType.DMA((64,)),
-            pltpu.SemaphoreType.DMA((6,)),
+            pltpu.SemaphoreType.DMA((48,)),
+            pltpu.SemaphoreType.DMA((3,)),
         ],
         compiler_params=pltpu.CompilerParams(
             vmem_limit_bytes=VMEM_LIMIT, collective_id=0, has_side_effects=True
@@ -371,7 +448,7 @@
 
     def step(block, carry):
         base, count = key_window(height_ref, width_ref, block)
-        for n in range(1, blocks + 1):
+        for n in range(1, min(blocks, WINDOW) + 1):
 
             @pl.when(count == n)
             def _():
@@ -442,7 +519,7 @@
 
     def step(block, carry):
         base, count = key_window(height_ref, width_ref, block)
-        for n in range(1, blocks + 1):
+        for n in range(1, min(blocks, WINDOW) + 1):
 
             @pl.when(count == n)
             def _():
@@ -936,16 +1013,15 @@
     upstay_ref, upgot_ref, downstay_ref, downgot_ref, x_hbm, dh_hbm, weight_hbm, dwo_hbm,
     dx_ref, grad_ref, total_ref,
     x_ref, dh_ref, weight_ref, rows_ref,
-    dw_ref, near_ref, fromx_ref, fromy_ref, diagx_ref, diagy_ref, third_ref, zone_ref, done_ref,
+    dw_ref, near_ref, fromx_ref, fromy_ref, diagx_ref, diagy_ref, third_ref, chain_ref, done_ref,
     pack_ref, side_ref, sums_ref,
-    near_sem, x_sem, y_sem, dx_sem, dy_sem, z_sem, grad_sem, side_sem, send_sem, local_sem,
+    near_sem, x_sem, y_sem, dx_sem, dy_sem, chain_sem, relay_sem, grad_sem, side_sem, send_sem, local_sem,
 ):
     z, x, y, c = place()
     m = 2 * y + c
     d = 2 * z + x
     n_dp = grad_ref.shape[0]
     right_x, right_y, partner = at(z, 1 - x, y, c), at(z, x, 1 - y, c), at(z, x, y, 1 - c)
-    dp_peers = [((d + off) % n_dp, m) for off in range(1, n_dp)]
     tokens, width = x_ref.shape
     loads = []
     for source, target in (
@@ -954,20 +1030,69 @@
         load = pltpu.make_async_copy(source, target, local_sem.at[len(loads)])
         load.start()
         loads.append(load)
-    greet(dp_peers + [right_y, partner])
+    greet([right_x, right_y, partner] + [at((z + off) % 4, x, y, c) for off in range(1, 4)])
     mail = Mail(send_sem)
     piece = pack_ref.at[0]
+
+    edge = z % 3 == 0
+    inner = z % 3 != 0
+    far = z // 2
+    near = 1 - far
+
+    def relay(direction, kind, part):
+        ref = chain_ref.at[direction, kind, part]
+        return pltpu.make_async_remote_copy(
+            src_ref=ref,
+            dst_ref=ref,
+            send_sem=relay_sem.at[direction, kind, part],
+            recv_sem=chain_sem.at[direction, kind, part],
+            device_id=at(z + 1 - 2 * direction, x, y, c),
+            device_id_type=pl.DeviceIdType.MESH,
+        )
+
+    def opening(kind, part):
+        chain_ref[far, kind, part] = third_ref[kind, part]
+        relay(far, kind, part).start()
+
+    def outward(kind, part):
+        ref = chain_ref.at[far, kind, part]
+        arrived(ref, chain_sem.at[far, kind, part])
+        ref[...] = added(third_ref[kind, part], ref[...])
+        relay(far, kind, part).start()
+
+    def inward(kind, part):
+        ref = chain_ref.at[near, kind, part]
+        arrived(ref, chain_sem.at[near, kind, part])
+        total = added(chain_ref[far, kind, part], ref[...])
+
+        @pl.when(inner)
+        def _():
+            ref[...] = added(third_ref[kind, part], ref[...])
+            relay(near, kind, part).start()
+
+        return total
+
+    def ahead(s):
+        @pl.when(inner)
+        def _():
+            outward(1 + s // 4, s % 4)
+
+    def keep(s):
+        done_ref[s // 4, s % 4] = inward(1 + s // 4, s % 4)
+
     for kind, (stay_ref, got_ref) in enumerate(
         ((upstay_ref, upgot_ref), (downstay_ref, downgot_ref))
     ):
-        for off in (2, 1, 3, 0):
-            to = (z + off) % 4
-            third_ref[1 + kind, to] = added(stay_ref[to], got_ref[to])
-            if off:
-                mail.send(
-                    third_ref.at[1 + kind, to], zone_ref.at[1 + kind, z], z_sem.at[1 + kind, z],
-                    at(to, x, y, c), piece,
-                )
+        for part in range(4):
+            third_ref[1 + kind, part] = added(stay_ref[part], got_ref[part])
+
+    @pl.when(edge)
+    def _():
+        def rest(s, carry):
+            opening(1 + s // 4, s % 4)
+            return carry
+
+        lax.fori_loop(0, 8, rest, 0)
 
     pairs = ((dq0_ref, dq1_ref), (dk0_ref, dk1_ref), (dv0_ref, dv1_ref))
     half = width // PARTS
@@ -987,6 +1112,7 @@
     flat = [weight_ref.at[index].reshape(width, width) for index in range(3)]
 
     def back(i, carry):
+        ahead(2 + i)
         t = pl.ds(pl.multiple_of(i * TILE, TILE), TILE)
         dn = jnp.zeros((TILE, width), F32)
         for index, pair in enumerate(pairs):
@@ -996,8 +1122,11 @@
         dx_ref[t, :] = dh_ref[t, :] + norm_back(dn, unit, scale, vec_ref[0:1, :])
         rows_ref[0:8, :] += fold_rows(dn * unit)
         rows_ref[8:16, :] += fold_rows(dn)
+        keep(i)
         return carry
 
+    ahead(0)
+    ahead(1)
     lax.fori_loop(0, 1, back, 0)
     for row in (0, 1):
         arrived(near_ref.at[row], near_sem.at[row])
@@ -1047,27 +1176,15 @@
         sums_ref[index + 1] = sums_ref[index] + side_ref[index]
 
     hop(0, partner)
-    for kind in (1, 2):
-        total = third_ref[kind, z].astype(F32)
-        for off in range(1, 4):
-            e = (z + off) % 4
-            arrived(zone_ref.at[kind, e], z_sem.at[kind, e])
-            total = total + zone_ref[kind, e].astype(F32)
-        done_ref[kind] = total.astype(BF)
+    ahead(6)
+    keep(4)
     landed(0)
     hop(1, right_x)
-    for part in (2, 3, 0, 1):
-        arrived(fromx_ref.at[part], x_sem.at[part])
-        arrived(fromy_ref.at[part], y_sem.at[part])
-    for off in (2, 1, 3, 0):
-        to = (z + off) % 4
-        third_ref[0, to] = added(near_ref[y, 2 * to + x], fromx_ref[to], fromy_ref[to])
-        if off:
-            mail.send(
-                third_ref.at[0, to], zone_ref.at[0, z], z_sem.at[0, z], at(to, x, y, c), piece
-            )
+    ahead(7)
+    keep(5)
     landed(1)
     hop(2, right_y)
+    keep(6)
     landed(2)
     for off in range(1, 4):
         mail.send(
@@ -1075,27 +1192,58 @@
             sums_ref.at[0],
         )
     side_ref[3 + z] = sums_ref[3]
-    total = third_ref[0, z].astype(F32)
-    for off in range(1, 4):
-        e = (z + off) % 4
-        arrived(zone_ref.at[0, e], z_sem.at[0, e])
-        total = total + zone_ref[0, e].astype(F32)
-    done_ref[0] = total.astype(BF)
-    for off in (3, 4, 5, 2, 6, 1, 7):
-        e = (d + off) % n_dp
-        kind = jnp.where(owner_ref[m, 1] == e, 1, jnp.where(owner_ref[m, 2] == e, 2, 0))
-        pack_ref[e] = done_ref[kind]
-        mail.send(pack_ref.at[e], grad_ref.at[d], grad_sem.at[d], (e, m), piece)
-    kind = jnp.where(owner_ref[m, 1] == d, 1, jnp.where(owner_ref[m, 2] == d, 2, 0))
-    grad_ref[d] = done_ref[kind]
+    keep(7)
+
+    def gathered(part):
+        arrived(fromx_ref.at[part], x_sem.at[part])
+        arrived(fromy_ref.at[part], y_sem.at[part])
+        third_ref[0, part] = added(near_ref[y, 2 * part + x], fromx_ref[part], fromy_ref[part])
+
+    def wanted(e, part, first):
+        second = lax.select(owner_ref[m, 2] == e, done_ref[1, part], first)
+        return lax.select(owner_ref[m, 1] == e, done_ref[0, part], second)
+
+    def close(part):
+        first = inward(0, part)
+        e = 2 * part + x
+        pack_ref[part] = wanted(2 * z + 1 - x, part, first)
+        mail.send(pack_ref.at[part], grad_ref.at[e], grad_sem.at[part], right_x, piece)
+        grad_ref[e] = wanted(d, part, first)
+
+    @pl.when(edge)
+    def _():
+        for part in (2, 3, 0, 1):
+            gathered(part)
+            opening(0, part)
+
+    def early(part):
+        @pl.when(inner)
+        def _():
+            gathered(part)
+            outward(0, part)
+
+    early(2)
+    early(3)
+    close(2)
+    early(0)
+    close(3)
+    early(1)
+    close(0)
+    close(1)
     for off in range(1, 4):
         e = (z + off) % 4
         arrived(side_ref.at[3 + e], side_sem.at[3 + e])
     total_ref[...] = (side_ref[3] + side_ref[4]) + (side_ref[5] + side_ref[6])
-    for off in range(1, n_dp):
-        e = (d + off) % n_dp
-        arrived(grad_ref.at[e], grad_sem.at[e])
+    for part in (2, 3, 0, 1):
+        arrived(grad_ref.at[2 * part + 1 - x], grad_sem.at[part])
     mail.finish()
+    for kind in range(3):
+        for part in range(4):
+            arrived(piece, relay_sem.at[far, kind, part])
+
+            @pl.when(inner)
+            def _():
+                arrived(piece, relay_sem.at[near, kind, part])
 
 
 def leave(owner, x, dh, n1, flows, vec, weights, dwo, small, rest):
@@ -1122,11 +1270,11 @@
             part(n_mlp, n_dp),
             pltpu.VMEM((16, width), F32),
             part(n_mlp, n_dp), part(2, n_dp), part(4), part(4), part(2), part(2), part(3, 4),
-            part(3, 4), part(3), part(n_dp),
+            part(2, 3, 4), part(2, 4), part(4),
             pltpu.VMEM((7,) + small.shape, F32),
             pltpu.VMEM((4,) + small.shape, F32),
-            dma((2,)), dma((4,)), dma((4,)), dma((2,)), dma((2,)), dma((3, 4)),
-            dma((n_dp,)), dma((7,)), dma((48,)), dma((4,)),
+            dma((2,)), dma((4,)), dma((4,)), dma((2,)), dma((2,)), dma((2, 3, 4)), dma((2, 3, 4)),
+            dma((4,)), dma((7,)), dma((32,)), dma((4,)),
         ],
         compiler_params=pltpu.CompilerParams(
             vmem_limit_bytes=VMEM_LIMIT, collective_id=2, has_side_effects=True
@@ -1138,60 +1286,112 @@
     )
 
 
-def halves(values):
-    high = values.astype(BF)
-    return high, (values - high.astype(F32)).astype(BF)
-
-
-def dot_fine(left, right):
-    left_high, left_low = halves(left)
-    right_high, right_low = halves(right)
-    return (
-        dot(left_high, right_low, 1, 0)
-        + dot(left_low, right_high, 1, 0)
-        + dot(left_high, right_high, 1, 0)
-    )
-
-
 def update_kernel(
-    keep_ref, decay_ref, grad_ref, left_ref, right_ref, lroot_ref, rroot_ref, master_ref,
-    slot_ref, newleft_ref, newright_ref, newmaster_ref,
+    keep_ref, decay_ref, grad_ref, left_hbm, right_hbm, lroot_hbm, rroot_hbm, master_hbm, y_hbm, dx_hbm,
+    slot_out, left_out, right_out, master_out, y_out, dx_out,
+    left_ref, right_ref, lroot_ref, rroot_ref, master_ref, y_ref, dx_ref, slot_ref, turn_ref,
+    in_sem, out_sem,
 ):
-    @pl.when(keep_ref[0] == 0)
+    loads = []
+    for source, target in (
+        (left_hbm, left_ref), (right_hbm, right_ref), (lroot_hbm, lroot_ref), (rroot_hbm, rroot_ref),
+        (master_hbm, master_ref), (y_hbm, y_ref), (dx_hbm, dx_ref),
+    ):
+        loads.append(pltpu.make_async_copy(source, target, in_sem.at[len(loads)]))
+        loads[-1].start()
+    outs = []
+
+    def emit(source, target):
+        outs.append(pltpu.make_async_copy(source, target, out_sem.at[len(outs)]))
+        outs[-1].start()
+
+    held = keep_ref[0] != 0
+    decay = decay_ref[0]
+    width = grad_ref.shape[0]
+    tall = width // 3
+
+    def strip(i):
+        return pl.ds(pl.multiple_of(i * tall, tall), tall)
+
+    @pl.when(held)
+    def _():
+        slot_ref[...] = grad_ref[...].astype(F32)
+
+    @pl.when(jnp.logical_not(held))
     def _():
         slot_ref[...] = jnp.zeros_like(slot_ref)
-        newleft_ref[...] = left_ref[...]
-        newright_ref[...] = right_ref[...]
-        newmaster_ref[...] = master_ref[...]
-
-    @pl.when(keep_ref[0] != 0)
+
+    emit(slot_ref, slot_out)
+    loads[0].wait()
+
+    @pl.when(held)
     def _():
-        decay = decay_ref[0]
-        grad = grad_ref[...].astype(F32)
-        slot_ref[...] = grad
-        low = grad.astype(BF)
-        newleft_ref[...] = decay * left_ref[...] + (1.0 - decay) * dot(low, low, 1, 1)
-        newright_ref[...] = decay * right_ref[...] + (1.0 - decay) * dot(low, low, 0, 0)
-        inner = dot_fine(lroot_ref[...], grad)
-        direction = dot_fine(inner, rroot_ref[...])
-        size = direction.shape[0] * direction.shape[1]
-        mean = jnp.sum(direction * direction, keepdims=True) * (1.0 / size)
-        newmaster_ref[...] = master_ref[...] - RATE_MATRIX * direction * lax.rsqrt(
-            mean + GRAFT_EPSILON
-        )
-
-
-def update(owns, decays, grad, left, right, lroot, rroot, master):
+        def rows(i, carry):
+            r = strip(i)
+            gram = dot(grad_ref[r, :], grad_ref[...], 1, 1)
+            left_ref[r, :] = decay * left_ref[r, :] + (1.0 - decay) * gram
+            return carry
+
+        lax.fori_loop(0, 3, rows, 0)
+
+    emit(left_ref, left_out)
+    loads[1].wait()
+
+    @pl.when(held)
+    def _():
+        turn_ref[...] = grad_ref[...].T
+
+        def rows(i, carry):
+            r = strip(i)
+            gram = dot(turn_ref[r, :], grad_ref[...], 1, 0)
+            right_ref[r, :] = decay * right_ref[r, :] + (1.0 - decay) * gram
+            return carry
+
+        lax.fori_loop(0, 3, rows, 0)
+
+    emit(right_ref, right_out)
+    for index, source, target in ((5, y_ref, y_out), (6, dx_ref, dx_out)):
+        loads[index].wait()
+        emit(source, target)
+    for load in loads[2:5]:
+        load.wait()
+
+    @pl.when(held)
+    def _():
+        turn_ref[...] = rroot_ref[...].astype(BF)
+
+        def rows(i, total):
+            r = strip(i)
+            inner = dot(lroot_ref[r, :].astype(BF), grad_ref[...], 1, 0).astype(BF)
+            direction = dot(inner, turn_ref[...], 1, 0)
+            lroot_ref[r, :] = direction
+            return total + jnp.sum(direction * direction, axis=0, keepdims=True)
+
+        total = jnp.sum(lax.fori_loop(0, 3, rows, jnp.zeros((1, width), F32)), keepdims=True)
+        mean = total * (1.0 / (width * width))
+        master_ref[...] -= lroot_ref[...] * (RATE_MATRIX * lax.rsqrt(mean + GRAFT_EPSILON))
+
+    emit(master_ref, master_out)
+    for copy in outs:
+        copy.wait()
+
+
+def update(owns, decays, grad, left, right, lroot, rroot, master, output, input_grad):
     smem = pl.BlockSpec(memory_space=pltpu.SMEM)
     vmem = pl.BlockSpec(memory_space=pltpu.VMEM)
+    hbm = pl.BlockSpec(memory_space=pl.ANY)
+    shape = lambda a: jax.ShapeDtypeStruct(a.shape, a.dtype)
+    room = lambda a: pltpu.VMEM(a.shape, a.dtype)
     return pl.pallas_call(
         update_kernel,
-        in_specs=[smem, smem] + [vmem] * 6,
-        out_specs=[vmem] * 4,
-        out_shape=[jax.ShapeDtypeStruct(left.shape, F32)] * 4,
+        in_specs=[smem, smem, vmem] + [hbm] * 7,
+        out_specs=[hbm] * 6,
+        out_shape=[shape(a) for a in (left, left, right, master, output, input_grad)],
+        scratch_shapes=[room(a) for a in (left, right, lroot, rroot, master, output, input_grad, left, grad)]
+        + [pltpu.SemaphoreType.DMA((7,)), pltpu.SemaphoreType.DMA((6,))],
         compiler_params=pltpu.CompilerParams(vmem_limit_bytes=VMEM_LIMIT),
         name="update",
-    )(owns, decays, grad, left, right, lroot, rroot, master)
+    )(owns, decays, grad, left, right, lroot, rroot, master, output, input_grad)
 
 
 def positions(segment, heights, widths, patch_rows, patch_cols):
@@ -1219,19 +1419,19 @@
     holds = owner_row == dp_index
     owns = jnp.any(holds).astype(jnp.int32).reshape(1)
     master = master_slots[0, 0]
-    slot = master.astype(BF).reshape(n_dp, share, width)
     turned = vectors.T
     pos = positions(segment, grid_height, grid_width, patch_rows, patch_cols)
     direct = n_dp == 8 and n_mlp == 4
     if direct:
         n1t, q, k, v, cosine, sine, qmark, kmark, attention, zone = enter(
-            owner, slot, tokens, pos, vectors, turned
+            owner, master.reshape(n_dp, share, width), tokens, pos, vectors, turned
         )
         over_x = [(i, i ^ 1) for i in range(n_dp)]
         over_y = [(i, i ^ 2) for i in range(n_mlp)]
         xzone = lax.ppermute(zone, "dp", over_x)
         yzone = lax.ppermute(zone, "mlp", over_y)
     else:
+        slot = master.astype(BF).reshape(n_dp, share, width)
         pieces = lax.all_to_all(slot, "dp", 0, 0, tiled=True)
         mine = jnp.take(pieces, owner_row, axis=0)
         every = lax.all_gather(mine[None], ("dp", "mlp"), axis=0, tiled=True)
@@ -1285,9 +1485,9 @@
         gradient = lax.all_to_all(jnp.take(reduced, kind_of, axis=0), "dp", 0, 0, tiled=True)
         total = lax.psum(jnp.concatenate([eights(fin_rows)] + tail, axis=0), ("dp", "mlp"))
     gradient = gradient.reshape(width, width)
-    slot_grad, left_out, right_out, master_out = update(
+    slot_grad, left_out, right_out, master_out, output, input_grad = update(
         owns, decays, gradient, left_slots[0, 0], right_slots[0, 0], left_roots[0, 0],
-        right_roots[0, 0], master,
+        right_roots[0, 0], master, output, input_grad,
     )
 
     cut = width // n_mlp

time: 377 us -> 346 us (0.918)
  the two profiles are of different devices: /device:TPU:20 before, /device:TPU:0 now
where the time goes in v3:
time: 346 us; the launch traced here: 341 us
  Pallas kernels  313 us (90%)
  local copies, waits for them, and re-layouts  7.8 us (2%)
  starting transfers between devices  7.61 us (2%)
  other arithmetic  7.27 us (2%)
    pallas_call x1, Pallas kernels, leave(): pl.pallas_call(leave_kernel, in_specs=[smem] + [vmem] * 13 + [hbm] * 4, o...  85 us
    pallas_call x1, Pallas kernels, enter(): pl.pallas_call(enter_kernel, in_specs=[smem, hbm, vmem, vmem, vmem, vmem]...  74.7 us
    pallas_call x1, Pallas kernels, center(): pl.pallas_call(center_kernel, in_specs=[vmem] * 4 + [hbm] * 4, out_specs=...  58.1 us
    pallas_call x2, Pallas kernels, attend_back(): pl.pallas_call(attend_back_kernel, grid=(1,), in_specs=[smem, smem, cut(q...  50.1 us
    pallas_call x1, Pallas kernels, attend(): pl.pallas_call(attend_kernel, in_specs=[smem, smem] + [vmem] * 5, out_spe...  28.8 us
    pallas_call x1, Pallas kernels, update(): pl.pallas_call(update_kernel, in_specs=[smem, smem, vmem] + [hbm] * 7, ou...  12.2 us
  transfers between devices with their start and end apart: 6, of which 2 were waited for; matrix products, arithmetic and copies ran while one was open for 1% of the time, Pallas kernels for 23%

profile of v3, /device:TPU:0, one launch (start us, length us, event | category | flops | bytes accessed | tf_op | source)
XLA Modules:
  0.0 341.1 jit_solution(7104387055965901107)
XLA Ops:
  0.6 0.7 convert_element_type.20
  1.3 1.7 copy.27
  3.1 0.8 select_reduce_fusion
  3.8 0.7 convert_divide_fusion
  4.6 0.6 stack.19.pos_ref
  5.2 74.7 %enter.1 = (bf16[768,1024]{1,0:T(8,128)(2,1)}, bf16[768,1024]{1,0:T(8,128)(2,1)}, bf16[768,1024]{1,0:T(8,128)(2,1)}, bf16[768,1024]{1,0:T(8,128)(2,1)}, f32[384,...) custom-call(s32[4,3]{1,0:T(4,128)} %owner_ref.3, ...), custom_call_target="tpu_custom_call" | custom-call | tf_op jit(solution)/shard_map/enter/pallas_call | solution.py:318
  79.9 1.5 collective-permute-start
  81.4 1.5 collective-permute-start.1
  82.9 28.8 %attend.1 = (bf16[768,1024]{1,0:T(8,128)(2,1)}, f32[96,1024]{1,0:T(8,128)}) custom-call(s32[4]{0:T(128)} %height_ref.5, s32[4]{0:T(128)} %width_ref.5, bf16[768,1024]{1,0:T(8,128)(2,1)} %get-tuple-element.65.q_ref, bf16[768,1024]{1,0:T(8,128)(2,1)} %get-tuple-element.66.k_ref, bf16[768,1024]{1,0:T(8,128)(2,1)} %get-tuple-element.67.v_ref, ...), custom_call_target="tpu_custom_call" | custom-call | tf_op jit(solution)/shard_map/attend/pallas_call | solution.py:469
  111.6 0.0 collective-permute-done.xzone_ref
  111.6 0.0 copy-start
  111.7 0.0 collective-permute-done.1.yzone_ref
  111.7 0.0 copy-start.1
  111.7 1.0 copy-done
  112.7 0.4 copy-done.1
  113.0 58.1 %center.1 = (bf16[1024,768]{1,0:T(8,128)(2,1)}, f32[1024,768]{1,0:T(8,128)}, bf16[768,1024]{1,0:T(8,128)(2,1)}, bf16[768,768]{1,0:T(8,128)(2,1)}, f32[32,768]{1,...) custom-call(bf16[1024,768]{1,0:T(8,128)(2,1)} %x_hbm.1, ...), custom_call_target="tpu_custom_call" | custom-call | tf_op jit(solution)/shard_map/center/pallas_call | solution.py:945
  171.2 2.6 collective-permute-start.2
  173.7 0.0 collective-permute-start.3
  173.8 24.8 %attend_back.2 = (bf16[384,1024]{1,0:T(8,128)(2,1)}, bf16[384,1024]{1,0:T(8,128)(2,1)}, bf16[384,1024]{1,0:T(8,128)(2,1)}, f32[8,192]{1,0:T(8,128)}, f32[24,384]{1,0:T(8,128)}) custom-call(s32[4]{0:T(128)} %height_ref.5, s32[4]{0:T(128)} %width_ref.5, bf16[768,1024]{1,0:T(8,128)(2,1)} %get-tuple-element.65.q_ref, bf16[768,1024]{1,0:T(8,128)(2,1)} %get-tuple-element.66.k_ref, ...), custom_call_target="tpu_custom_call" | custom-call | tf_op jit(solution)/shard_map/attend_back/pallas_call | solution.py:575
  198.6 1.4 collective-permute-done.2.upgot_ref
  200.0 0.0 copy-start.2
  200.0 1.5 collective-permute-done.3.downgot_ref
  201.5 0.0 copy-done.2
  201.5 1.0 copy-done.3
  202.5 4.3 %merge.1 = (bf16[4,96,768]{2,1,0:T(8,128)(2,1)}, bf16[4,96,768]{2,1,0:T(8,128)(2,1)}, bf16[4,96,768]{2,1,0:T(8,128)(2,1)}, bf16[4,96,768]{2,1,0:T(8,128)(2,1)}) custom-call(bf16[2,4,96,768]{3,2,1,0:T(8,128)(2,1)} %get-tuple-element.85.upstay_ref, bf16[2,4,96,768]{3,2,1,0:T(8,128)(2,1)} %copy-done.2, bf16[8,96,768]{2,1,0:T(8,128)(2,1)} %get-tuple-element.87.downstay_ref, ...), custom_call_target="tpu_custom_call" | custom-call | tf_op jit(solution)/shard_map/merge/pallas_call | solution.py:1001
  206.8 0.6 collective-permute-start.4
  207.4 1.4 collective-permute-start.5
  208.8 1.3 compare_reduce_fusion
  210.8 0.0 copy-done.10
  210.8 0.7 slice.23
  212.1 0.0 copy-done.7
  212.2 0.0 copy-done.6
  212.3 0.0 copy-start.9
  212.3 0.0 copy-start.8
  212.3 25.3 %attend_back.3 = (bf16[384,1024]{1,0:T(8,128)(2,1)}, bf16[384,1024]{1,0:T(8,128)(2,1)}, bf16[384,1024]{1,0:T(8,128)(2,1)}, f32[8,192]{1,0:T(8,128)}, f32[24,384]{1,0:T(8,128)}) custom-call(s32[4]{0:T(128)} %height_ref.5, s32[4]{0:T(128)} %width_ref.5, bf16[768,1024]{1,0:T(8,128)(2,1)} %get-tuple-element.65.q_ref, bf16[768,1024]{1,0:T(8,128)(2,1)} %get-tuple-element.66.k_ref, ...), custom_call_target="tpu_custom_call" | custom-call | tf_op jit(solution)/shard_map/attend_back/pallas_call | solution.py:575
  237.6 0.0 copy-done.9
  237.6 0.8 fusion.1
  238.3 0.0 copy-done.8
  238.4 0.8 pad_maximum_fusion
  239.2 1.3 concatenate.11.small_ref
  240.4 0.0 collective-permute-done.4.upgot_ref
  240.4 0.0 collective-permute-done.5.downgot_ref
  240.4 0.0 copy-start.5
  240.4 0.8 copy-done.4
  241.2 0.2 copy-done.5
  241.5 85.0 %leave.1 = (f32[1024,768]{1,0:T(8,128)}, bf16[8,96,768]{2,1,0:T(8,128)(2,1)}, f32[14,768]{1,0:T(8,128)}) custom-call(s32[4,3]{1,0:T(4,128)} %owner_ref.3, bf16[768,1024]{1,0:T(8,128)(2,1)} %get-tuple-element.64.n1_ref, bf16[384,1024]{1,0:T(8,128)(2,1)} %get-tuple-element.84.dq0_ref, bf16[384,1024]{1,0:T(8,128)(2,1)} %get-tuple-element.92.dq1_ref, ...), custom_call_target="tpu_custom_call" | custom-call | tf_op jit(solution)/shard_map/leave/pallas_call | solution.py:1258
  326.5 2.2 divide_subtract_fusion
  328.7 12.2 %update.1 = (f32[768,768]{1,0:T(8,128)}, f32[768,768]{1,0:T(8,128)}, f32[768,768]{1,0:T(8,128)}, f32[768,768]{1,0:T(8,128)}, bf16[1024,768]{1,0:T(8,128)(2,1)}, /*index=5*/f32[1024,768]{1,0:T(8,128)}) custom-call(s32[1]{0:T(128)} %bitcast.keep_ref, f32[2]{0:T(128)} %decay_ref.1, bf16[768,768]{1,0:T(8,128)(2,1)} %bitcast.35, f32[768,768]{1,0:T(8,128)} %bitcast.29, ...), custom_call_target="tpu_custom_call" | custom-call | tf_op jit(solution)/shard_map/update/pallas_call | solution.py:1385
  (14 shorter events, 0.1 us)
Async XLA Ops:
  79.9 31.8 %collective-permute-start = (bf16[2,4,96,768]{3,2,1,0:T(8,128)(2,1)}, bf16[2,4,96,768]{3,2,1,0:T(8,128)(2,1)S(1)}, u32[]{:S(2)}, u32[]{:S(2)}) collective-permute-start(bf16[2,4,96,768]{3,2,1,0:T(8,128)(2,1)} %get-tuple-element.73.zone_ref), channel_id=1, source_target_pairs={{0,4},{4,0},{8,12},{12,8},{16,20},{20,16},{24,28},{28,24},{1,5},{5... | collective-permute-start | bytes 3538952 | tf_op jit(solution)/shard_map/ppermute | solution.py:1431
  81.4 30.2 %collective-permute-start.1 = (bf16[2,4,96,768]{3,2,1,0:T(8,128)(2,1)}, bf16[2,4,96,768]{3,2,1,0:T(8,128)(2,1)S(1)}, u32[]{:S(2)}, u32[]{:S(2)}) collective-permute-start(bf16[2,4,96,768]{3,2,1,0:T(8,128)(2,1)} %get-tuple-element.73.zone_ref), channel_id=1, source_target_pairs={{0,2},{1,3},{2,0},{3,1},{4,6},{5,7},{6,4},{7,5},{8,10},{9,11},{10,... | collective-permute-start | bytes 3538952 | tf_op jit(solution)/shard_map/ppermute | solution.py:1432
  111.6 1.0 copy-start
  111.7 1.4 copy-start.1
  171.2 28.8 %collective-permute-start.2 = (bf16[2,4,96,768]{3,2,1,0:T(8,128)(2,1)}, bf16[2,4,96,768]{3,2,1,0:T(8,128)(2,1)S(1)}, u32[]{:S(2)}, u32[]{:S(2)}) collective-permute-start(bf16[2,4,96,768]{3,2,1,0:T(8,128)(2,1)} %get-tuple-element.82), channel_id=1, source_target_pairs={{0,4},{4,0},{8,12},{12,8},{16,20},{20,16},{24,28},{28,24},{1,5},{5... | collective-permute-start | bytes 3538952 | tf_op jit(solution)/shard_map/ppermute | solution.py:1448
  173.7 27.7 %collective-permute-start.3 = (bf16[8,96,768]{2,1,0:T(8,128)(2,1)}, bf16[8,96,768]{2,1,0:T(8,128)(2,1)S(1)}, u32[]{:S(2)}, u32[]{:S(2)}) collective-permute-start(bf16[8,96,768]{2,1,0:T(8,128)(2,1)} %get-tuple-element.83), channel_id=1, source_target_pairs={{0,2},{1,3},{2,0},{3,1},{4,6},{5,7},{6,4},{7,5},{8,10},{9,11},{10,... | collective-permute-start | bytes 3538952 | tf_op jit(solution)/shard_map/ppermute | solution.py:1449
  200.0 1.5 copy-start.2
  201.5 1.0 copy-start.3
  202.5 8.3 %copy-start.10 = (f32[2]{0:T(128)S(1)}, f32[2]{0:T(128)}, u32[]{:S(2)}) copy-start(f32[2]{0:T(128)} %decay_ref.1) | copy-start | bytes 28
  202.5 9.7 %copy-start.7 = (f32[4,8,768]{2,1,0:T(8,128)S(1)}, f32[4,8,768]{2,1,0:T(8,128)}, u32[]{:S(2)}) copy-start(f32[4,8,768]{2,1,0:T(8,128)} %get-tuple-element.100) | copy-start | bytes 294916
  202.5 9.7 %copy-start.6 = (f32[32,768]{1,0:T(8,128)S(1)}, f32[32,768]{1,0:T(8,128)}, u32[]{:S(2)}) copy-start(f32[32,768]{1,0:T(8,128)} %get-tuple-element.99) | copy-start | bytes 294916
  206.8 33.6 %collective-permute-start.4 = (bf16[4,96,768]{2,1,0:T(8,128)(2,1)}, bf16[4,96,768]{2,1,0:T(8,128)(2,1)S(1)}, u32[]{:S(2)}, u32[]{:S(2)}) collective-permute-start(bf16[4,96,768]{2,1,0:T(8,128)(2,1)} %get-tuple-element.104), channel_id=1, source_target_pairs={{0,2},{1,3},{2,0},{3,1},{4,6},{5,7},{6,4},{7,5},{8,10},{9,11},{10,... | collective-permute-start | bytes 1769480 | tf_op jit(solution)/shard_map/ppermute | solution.py:1453
  207.4 33.0 %collective-permute-start.5 = (bf16[4,96,768]{2,1,0:T(8,128)(2,1)}, bf16[4,96,768]{2,1,0:T(8,128)(2,1)S(1)}, u32[]{:S(2)}, u32[]{:S(2)}) collective-permute-start(bf16[4,96,768]{2,1,0:T(8,128)(2,1)} %get-tuple-element.106), channel_id=1, source_target_pairs={{0,4},{4,0},{8,12},{12,8},{16,20},{20,16},{24,28},{28,24},{1,5},{5... | collective-permute-start | bytes 1769480 | tf_op jit(solution)/shard_map/ppermute | solution.py:1454
  212.3 25.3 %copy-start.9 = (f32[8,192]{1,0:T(8,128)S(1)}, f32[8,192]{1,0:T(8,128)}, u32[]{:S(2)}) copy-start(f32[8,192]{1,0:T(8,128)} %get-tuple-element.101) | copy-start | bytes 18436
  212.3 26.1 %copy-start.8 = (f32[24,384]{1,0:T(8,128)S(1)}, f32[24,384]{1,0:T(8,128)}, u32[]{:S(2)}) copy-start(f32[24,384]{1,0:T(8,128)} %get-tuple-element.97) | copy-start | bytes 110596
  240.4 0.8 copy-start.4
  240.4 1.0 copy-start.5

commit v4 on v3

--- a/solution.py
+++ b/solution.py
@@ -219,16 +219,6 @@
             crossed(part)
             outward(0, part)
 
-    early(0)
-    early(1)
-    bring(0)
-    early(2)
-    bring(1)
-    early(3)
-    bring(2)
-    bring(3)
-    lax.fori_loop(tiles // 2, tiles, prepare, 0)
-
     def ahead(s):
         @pl.when(inner)
         def _():
@@ -238,7 +228,8 @@
         zland_ref[s // 4, s % 4] = inward(1 + s // 4, s % 4)
 
     m_y = 2 * (1 - y) + c
-    for part in range(4):
+
+    def spread(part):
         e = 2 * part + 1 - x
         arrived(att_ref.at[m, e], att_sem.at[m, e])
         if part < 2:
@@ -249,9 +240,28 @@
         if part >= 2:
             mail.send(att_ref.at[m_y, f], att_ref.at[m_y, f], att_sem.at[m_y, f], right_x, piece)
         mail.send(att_ref.at[m_y, f], att_ref.at[m_y, f], att_sem.at[m_y, f], partner, piece)
-        ahead(part)
-        if part:
-            keep(part - 1)
+
+    early(0)
+    early(1)
+    bring(0)
+    early(2)
+    bring(1)
+    early(3)
+    bring(2)
+    ahead(0)
+    spread(0)
+    bring(3)
+    ahead(1)
+    spread(1)
+    ahead(2)
+    keep(0)
+    lax.fori_loop(tiles // 2, tiles, prepare, 0)
+    spread(2)
+    ahead(3)
+    keep(1)
+    spread(3)
+    ahead(4)
+    keep(2)
     for part in range(4):
         e = 2 * part + 1 - x
         arrived(att_ref.at[m_y, e], att_sem.at[m_y, e])
@@ -270,7 +280,10 @@
         return att_ref[index].reshape(width, width)
 
     def rotate(i, carry):
-        ahead(4 + i)
+        @pl.when(i < 3)
+        def _():
+            ahead(5 + i)
+
         keep(3 + i)
         t = pl.ds(pl.multiple_of(i * TILE, TILE), TILE)
         n1t = n1_ref[:, t]
@@ -1096,23 +1109,75 @@
 
     pairs = ((dq0_ref, dq1_ref), (dk0_ref, dk1_ref), (dv0_ref, dv1_ref))
     half = width // PARTS
-    for index, pair in enumerate(pairs):
-        out = dw_ref.at[index].reshape(width, width)
-        for part, ref in enumerate(pair):
-            out[:, part * half : (part + 1) * half] = dot(n1_ref[...], ref[...], 1, 1).astype(BF)
+    groups = ((0, 2), (1, 3))
+    share = near_ref.shape[2]
+    twin = near_ref.at[0, pl.ds(0, 2)]
+
+    def products(group):
+        rows = [slice(2 * share * part, 2 * share * (part + 1)) for part in group]
+        left = jnp.concatenate([n1_ref[r, :] for r in rows], axis=0)
+        for index, pair in enumerate(pairs):
+            out = dw_ref.at[index].reshape(width, width)
+            for side, ref in enumerate(pair):
+                value = dot(left, ref[...], 1, 1).astype(BF)
+                for place_in, r in enumerate(rows):
+                    out[r, side * half : (side + 1) * half] = value[
+                        2 * share * place_in : 2 * share * (place_in + 1)
+                    ]
+
+    def pass_over(group):
+        for part in group:
+            for row in range(2):
+                mail.send(
+                    dw_ref.at[2 * row + 1 - c, pl.ds(2 * part, 2)], near_ref.at[row, pl.ds(2 * part, 2)],
+                    near_sem.at[row, part], partner, twin,
+                )
+
+    def summed(group):
+        for part in group:
+            for row in range(2):
+                arrived(twin, near_sem.at[row, part])
+
+            def one(i, carry):
+                row, e = i // 2, 2 * part + i % 2
+                near_ref[row, e] = added(near_ref[row, e], dw_ref[2 * row + c, e])
+                return carry
+
+            lax.fori_loop(0, 4, one, 0)
+
+    def issue(group):
+        low, high = group
+        mail.send(
+            near_ref.at[1 - y, 2 * low + 1 - x], diagy_ref.at[low], dy_sem.at[low], right_y, piece
+        )
+        mail.send(
+            near_ref.at[1 - y, 2 * high + 1 - x], diagx_ref.at[high - 2], dx_sem.at[high - 2],
+            right_x, piece,
+        )
+        mail.send(near_ref.at[1 - y, 2 * low + x], fromy_ref.at[low], y_sem.at[low], right_y, piece)
+        mail.send(near_ref.at[y, 2 * high + 1 - x], fromx_ref.at[high], x_sem.at[high], right_x, piece)
+
+    def forward(group):
+        low, high = group
+        turn = high - 2
+        arrived(diagy_ref.at[low], dy_sem.at[low])
+        diagy_ref[low] = added(near_ref[y, 2 * low + 1 - x], diagy_ref[low])
+        mail.send(diagy_ref.at[low], fromx_ref.at[low], x_sem.at[low], right_x, piece)
+        arrived(diagx_ref.at[turn], dx_sem.at[turn])
+        diagx_ref[turn] = added(near_ref[1 - y, 2 * high + x], diagx_ref[turn])
+        mail.send(diagx_ref.at[turn], fromy_ref.at[high], y_sem.at[high], right_y, piece)
+
+    products(groups[0])
     loads[0].wait()
-    for step in range(2):
-        mail.send(
-            dw_ref.at[2 * step + 1 - c], near_ref.at[step], near_sem.at[step], partner,
-            near_ref.at[0],
-        )
+    pass_over(groups[0])
+    products(groups[1])
+    pass_over(groups[1])
     for load in loads[1:]:
         load.wait()
     rows_ref[...] = jnp.zeros_like(rows_ref)
     flat = [weight_ref.at[index].reshape(width, width) for index in range(3)]
 
     def back(i, carry):
-        ahead(2 + i)
         t = pl.ds(pl.multiple_of(i * TILE, TILE), TILE)
         dn = jnp.zeros((TILE, width), F32)
         for index, pair in enumerate(pairs):
@@ -1122,49 +1187,36 @@
         dx_ref[t, :] = dh_ref[t, :] + norm_back(dn, unit, scale, vec_ref[0:1, :])
         rows_ref[0:8, :] += fold_rows(dn * unit)
         rows_ref[8:16, :] += fold_rows(dn)
-        keep(i)
         return carry
 
-    ahead(0)
-    ahead(1)
-    lax.fori_loop(0, 1, back, 0)
-    for row in (0, 1):
-        arrived(near_ref.at[row], near_sem.at[row])
-
-        def summed(e, carry):
-            near_ref[row, e] = added(near_ref[row, e], dw_ref[2 * row + c, e])
-            return carry
-
-        lax.fori_loop(0, n_dp, summed, 0)
-    for part in range(2):
-        mail.send(
-            near_ref.at[1 - y, 2 * part + 1 - x], diagy_ref.at[part], dy_sem.at[part], right_y, piece
-        )
-        mail.send(
-            near_ref.at[1 - y, 2 * (2 + part) + 1 - x], diagx_ref.at[part], dx_sem.at[part],
-            right_x, piece,
-        )
-    for part in range(2):
-        mail.send(
-            near_ref.at[y, 2 * (2 + part) + 1 - x], fromx_ref.at[2 + part], x_sem.at[2 + part],
-            right_x, piece,
-        )
-        mail.send(near_ref.at[1 - y, 2 * part + x], fromy_ref.at[part], y_sem.at[part], right_y, piece)
-    lax.fori_loop(1, 3, back, 0)
-    for part in range(2):
-        arrived(diagy_ref.at[part], dy_sem.at[part])
-        e = 2 * part + 1 - x
-        diagy_ref[part] = added(near_ref[y, e], diagy_ref[part])
-        mail.send(diagy_ref.at[part], fromx_ref.at[part], x_sem.at[part], right_x, piece)
-        arrived(diagx_ref.at[part], dx_sem.at[part])
-        f = 2 * (2 + part) + x
-        diagx_ref[part] = added(near_ref[1 - y, f], diagx_ref[part])
-        mail.send(diagx_ref.at[part], fromy_ref.at[2 + part], y_sem.at[2 + part], right_y, piece)
-    lax.fori_loop(3, tokens // TILE, back, 0)
-
-    sums_ref[0] = small_ref[...]
-    sums_ref[0, 0:1, :] = jnp.sum(rows_ref[0:8, :], axis=0, keepdims=True)
-    sums_ref[0, 1:2, :] = jnp.sum(rows_ref[8:16, :], axis=0, keepdims=True)
+    def gathered(part):
+        arrived(fromx_ref.at[part], x_sem.at[part])
+        arrived(fromy_ref.at[part], y_sem.at[part])
+        third_ref[0, part] = added(near_ref[y, 2 * part + x], fromx_ref[part], fromy_ref[part])
+
+    def wanted(e, part, first):
+        second = lax.select(owner_ref[m, 2] == e, done_ref[1, part], first)
+        return lax.select(owner_ref[m, 1] == e, done_ref[0, part], second)
+
+    def close(part):
+        first = inward(0, part)
+        e = 2 * part + x
+        pack_ref[part] = wanted(2 * z + 1 - x, part, first)
+        mail.send(pack_ref.at[part], grad_ref.at[e], grad_sem.at[part], right_x, piece)
+        grad_ref[e] = wanted(d, part, first)
+
+    def begin(group):
+        @pl.when(edge)
+        def _():
+            for part in group[::-1]:
+                gathered(part)
+                opening(0, part)
+
+    def early(part):
+        @pl.when(inner)
+        def _():
+            gathered(part)
+            outward(0, part)
 
     def hop(index, peer):
         mail.send(
@@ -1175,7 +1227,31 @@
         arrived(side_ref.at[index], side_sem.at[index])
         sums_ref[index + 1] = sums_ref[index] + side_ref[index]
 
+    ahead(0)
+    summed(groups[0])
+    issue(groups[0])
+    ahead(1)
+    lax.fori_loop(0, 1, back, 0)
+    summed(groups[1])
+    ahead(2)
+    keep(0)
+    forward(groups[0])
+    issue(groups[1])
+
+    def middle(i, carry):
+        ahead(2 + i)
+        keep(i)
+        return back(i, carry)
+
+    lax.fori_loop(1, 3, middle, 0)
+    begin(groups[0])
+    lax.fori_loop(3, tokens // TILE, middle, 0)
+
+    sums_ref[0] = small_ref[...]
+    sums_ref[0, 0:1, :] = jnp.sum(rows_ref[0:8, :], axis=0, keepdims=True)
+    sums_ref[0, 1:2, :] = jnp.sum(rows_ref[8:16, :], axis=0, keepdims=True)
     hop(0, partner)
+    forward(groups[1])
     ahead(6)
     keep(4)
     landed(0)
@@ -1184,6 +1260,7 @@
     keep(5)
     landed(1)
     hop(2, right_y)
+    begin(groups[1])
     keep(6)
     landed(2)
     for off in range(1, 4):
@@ -1192,43 +1269,14 @@
             sums_ref.at[0],
         )
     side_ref[3 + z] = sums_ref[3]
+    early(2)
     keep(7)
-
-    def gathered(part):
-        arrived(fromx_ref.at[part], x_sem.at[part])
-        arrived(fromy_ref.at[part], y_sem.at[part])
-        third_ref[0, part] = added(near_ref[y, 2 * part + x], fromx_ref[part], fromy_ref[part])
-
-    def wanted(e, part, first):
-        second = lax.select(owner_ref[m, 2] == e, done_ref[1, part], first)
-        return lax.select(owner_ref[m, 1] == e, done_ref[0, part], second)
-
-    def close(part):
-        first = inward(0, part)
-        e = 2 * part + x
-        pack_ref[part] = wanted(2 * z + 1 - x, part, first)
-        mail.send(pack_ref.at[part], grad_ref.at[e], grad_sem.at[part], right_x, piece)
-        grad_ref[e] = wanted(d, part, first)
-
-    @pl.when(edge)
-    def _():
-        for part in (2, 3, 0, 1):
-            gathered(part)
-            opening(0, part)
-
-    def early(part):
-        @pl.when(inner)
-        def _():
-            gathered(part)
-            outward(0, part)
-
-    early(2)
+    early(0)
+    close(2)
     early(3)
-    close(2)
-    early(0)
+    close(0)
+    early(1)
     close(3)
-    early(1)
-    close(0)
     close(1)
     for off in range(1, 4):
         e = (z + off) % 4
@@ -1273,7 +1321,7 @@
             part(2, 3, 4), part(2, 4), part(4),
             pltpu.VMEM((7,) + small.shape, F32),
             pltpu.VMEM((4,) + small.shape, F32),
-            dma((2,)), dma((4,)), dma((4,)), dma((2,)), dma((2,)), dma((2, 3, 4)), dma((2, 3, 4)),
+            dma((2, 4)), dma((4,)), dma((4,)), dma((2,)), dma((2,)), dma((2, 3, 4)), dma((2, 3, 4)),
             dma((4,)), dma((7,)), dma((32,)), dma((4,)),
         ],
         compiler_params=pltpu.CompilerParams(

time: 346 us -> 327 us (0.945)
  Pallas kernels: 313 us -> 298 us
    pallas_call x1, Pallas kernels: 85 us -> 68.1 us  [leave(): pl.pallas_call(leave_kernel, in_specs=[smem] + [vmem] * 13 + [hbm] * 4, o...]
    pallas_call x1, Pallas kernels: 74.7 us -> 70.9 us  [enter(): pl.pallas_call(enter_kernel, in_specs=[smem, hbm, vmem, vmem, vmem, vmem]...]
  transfers between devices with their start and end apart: 6 -> 6, of which waited for: 2 -> 0; matrix products, arithmetic and copies ran while one was open for 1% -> 2% of each run, Pallas kernels for 23% -> 26%
where the time goes in v4:
time: 327 us; the launch traced here: 322 us
  Pallas kernels  298 us (91%)
  local copies, waits for them, and re-layouts  8.16 us (2%)
  other arithmetic  7.27 us (2%)
  starting transfers between devices  5.84 us (2%)
    pallas_call x1, Pallas kernels, enter(): pl.pallas_call(enter_kernel, in_specs=[smem, hbm, vmem, vmem, vmem, vmem]...  70.9 us
    pallas_call x1, Pallas kernels, leave(): pl.pallas_call(leave_kernel, in_specs=[smem] + [vmem] * 13 + [hbm] * 4, o...  68.1 us
    pallas_call x1, Pallas kernels, center(): pl.pallas_call(center_kernel, in_specs=[vmem] * 4 + [hbm] * 4, out_specs=...  59 us
    pallas_call x2, Pallas kernels, attend_back(): pl.pallas_call(attend_back_kernel, grid=(1,), in_specs=[smem, smem, cut(q...  53.2 us
    pallas_call x1, Pallas kernels, attend(): pl.pallas_call(attend_kernel, in_specs=[smem, smem] + [vmem] * 5, out_spe...  30.7 us
    pallas_call x1, Pallas kernels, update(): pl.pallas_call(update_kernel, in_specs=[smem, smem, vmem] + [hbm] * 7, ou...  12.2 us
  transfers between devices with their start and end apart: 6, of which 0 were waited for; matrix products, arithmetic and copies ran while one was open for 2% of the time, Pallas kernels for 26%

profile of v4, /device:TPU:0, one launch (start us, length us, event | category | flops | bytes accessed | tf_op | source)
XLA Modules:
  0.0 322.1 jit_solution(17996226390379196648)
XLA Ops:
  0.6 0.7 convert_element_type.20
  1.3 1.7 copy.27
  3.1 0.8 select_reduce_fusion
  3.8 0.7 convert_divide_fusion
  4.6 0.6 stack.19.pos_ref
  5.2 70.9 %enter.1 = (bf16[768,1024]{1,0:T(8,128)(2,1)}, bf16[768,1024]{1,0:T(8,128)(2,1)}, bf16[768,1024]{1,0:T(8,128)(2,1)}, bf16[768,1024]{1,0:T(8,128)(2,1)}, f32[384,...) custom-call(s32[4,3]{1,0:T(4,128)} %owner_ref.3, ...), custom_call_target="tpu_custom_call" | custom-call | tf_op jit(solution)/shard_map/enter/pallas_call | solution.py:331
  76.1 0.6 collective-permute-start
  76.8 1.5 collective-permute-start.1
  78.3 30.7 %attend.1 = (bf16[768,1024]{1,0:T(8,128)(2,1)}, f32[96,1024]{1,0:T(8,128)}) custom-call(s32[4]{0:T(128)} %height_ref.5, s32[4]{0:T(128)} %width_ref.5, bf16[768,1024]{1,0:T(8,128)(2,1)} %get-tuple-element.65.q_ref, bf16[768,1024]{1,0:T(8,128)(2,1)} %get-tuple-element.66.k_ref, bf16[768,1024]{1,0:T(8,128)(2,1)} %get-tuple-element.67.v_ref, ...), custom_call_target="tpu_custom_call" | custom-call | tf_op jit(solution)/shard_map/attend/pallas_call | solution.py:482
  109.0 0.0 collective-permute-done.xzone_ref
  109.0 0.0 collective-permute-done.1.yzone_ref
  109.0 0.0 copy-start.1
  109.0 1.0 copy-done
  110.0 0.4 copy-done.1
  110.4 59.0 %center.1 = (bf16[1024,768]{1,0:T(8,128)(2,1)}, f32[1024,768]{1,0:T(8,128)}, bf16[768,1024]{1,0:T(8,128)(2,1)}, bf16[768,768]{1,0:T(8,128)(2,1)}, f32[32,768]{1,...) custom-call(bf16[1024,768]{1,0:T(8,128)(2,1)} %x_hbm.1, ...), custom_call_target="tpu_custom_call" | custom-call | tf_op jit(solution)/shard_map/center/pallas_call | solution.py:958
  169.4 0.9 collective-permute-start.2
  170.3 1.2 collective-permute-start.3
  171.5 26.4 %attend_back.2 = (bf16[384,1024]{1,0:T(8,128)(2,1)}, bf16[384,1024]{1,0:T(8,128)(2,1)}, bf16[384,1024]{1,0:T(8,128)(2,1)}, f32[8,192]{1,0:T(8,128)}, f32[24,384]{1,0:T(8,128)}) custom-call(s32[4]{0:T(128)} %height_ref.5, s32[4]{0:T(128)} %width_ref.5, bf16[768,1024]{1,0:T(8,128)(2,1)} %get-tuple-element.65.q_ref, bf16[768,1024]{1,0:T(8,128)(2,1)} %get-tuple-element.66.k_ref, ...), custom_call_target="tpu_custom_call" | custom-call | tf_op jit(solution)/shard_map/attend_back/pallas_call | solution.py:588
  197.9 0.0 collective-permute-done.2.upgot_ref
  197.9 0.0 copy-start.2
  197.9 0.0 collective-permute-done.3.downgot_ref
  197.9 0.0 copy-start.3
  197.9 1.0 copy-done.2
  198.9 0.4 copy-done.3
  199.3 4.3 %merge.1 = (bf16[4,96,768]{2,1,0:T(8,128)(2,1)}, bf16[4,96,768]{2,1,0:T(8,128)(2,1)}, bf16[4,96,768]{2,1,0:T(8,128)(2,1)}, bf16[4,96,768]{2,1,0:T(8,128)(2,1)}) custom-call(bf16[2,4,96,768]{3,2,1,0:T(8,128)(2,1)} %get-tuple-element.85.upstay_ref, bf16[2,4,96,768]{3,2,1,0:T(8,128)(2,1)} %copy-done.2, bf16[8,96,768]{2,1,0:T(8,128)(2,1)} %get-tuple-element.87.downstay_ref, ...), custom_call_target="tpu_custom_call" | custom-call | tf_op jit(solution)/shard_map/merge/pallas_call | solution.py:1014
  203.6 0.9 collective-permute-start.4
  204.6 0.7 collective-permute-start.5
  205.2 1.3 compare_reduce_fusion
  207.2 0.0 copy-done.10
  207.2 0.7 slice.23
  208.6 0.0 copy-done.7
  208.6 0.0 copy-done.6
  208.7 0.0 copy-start.9
  208.7 0.0 copy-start.8
  208.7 26.8 %attend_back.3 = (bf16[384,1024]{1,0:T(8,128)(2,1)}, bf16[384,1024]{1,0:T(8,128)(2,1)}, bf16[384,1024]{1,0:T(8,128)(2,1)}, f32[8,192]{1,0:T(8,128)}, f32[24,384]{1,0:T(8,128)}) custom-call(s32[4]{0:T(128)} %height_ref.5, s32[4]{0:T(128)} %width_ref.5, bf16[768,1024]{1,0:T(8,128)(2,1)} %get-tuple-element.65.q_ref, bf16[768,1024]{1,0:T(8,128)(2,1)} %get-tuple-element.66.k_ref, ...), custom_call_target="tpu_custom_call" | custom-call | tf_op jit(solution)/shard_map/attend_back/pallas_call | solution.py:588
  235.6 0.0 copy-done.9
  235.6 0.8 fusion.1
  236.3 0.0 copy-done.8
  236.3 0.8 pad_maximum_fusion
  237.2 1.3 concatenate.11.small_ref
  238.4 0.0 collective-permute-done.4.upgot_ref
  238.4 0.0 collective-permute-done.5.downgot_ref
  238.4 0.0 copy-start.5
  238.4 0.8 copy-done.4
  239.2 0.2 copy-done.5
  239.4 68.1 %leave.1 = (f32[1024,768]{1,0:T(8,128)}, bf16[8,96,768]{2,1,0:T(8,128)(2,1)}, f32[14,768]{1,0:T(8,128)}) custom-call(s32[4,3]{1,0:T(4,128)} %owner_ref.3, bf16[768,1024]{1,0:T(8,128)(2,1)} %get-tuple-element.64.n1_ref, bf16[384,1024]{1,0:T(8,128)(2,1)} %get-tuple-element.84.dq0_ref, bf16[384,1024]{1,0:T(8,128)(2,1)} %get-tuple-element.92.dq1_ref, ...), custom_call_target="tpu_custom_call" | custom-call | tf_op jit(solution)/shard_map/leave/pallas_call | solution.py:1306
  307.6 2.2 divide_subtract_fusion
  309.7 12.2 %update.1 = (f32[768,768]{1,0:T(8,128)}, f32[768,768]{1,0:T(8,128)}, f32[768,768]{1,0:T(8,128)}, f32[768,768]{1,0:T(8,128)}, bf16[1024,768]{1,0:T(8,128)(2,1)}, /*index=5*/f32[1024,768]{1,0:T(8,128)}) custom-call(s32[1]{0:T(128)} %bitcast.keep_ref, f32[2]{0:T(128)} %decay_ref.1, bf16[768,768]{1,0:T(8,128)(2,1)} %bitcast.35, f32[768,768]{1,0:T(8,128)} %bitcast.29, ...), custom_call_target="tpu_custom_call" | custom-call | tf_op jit(solution)/shard_map/update/pallas_call | solution.py:1433
  (14 shorter events, 0.1 us)
Async XLA Ops:
  76.1 32.8 %collective-permute-start = (bf16[2,4,96,768]{3,2,1,0:T(8,128)(2,1)}, bf16[2,4,96,768]{3,2,1,0:T(8,128)(2,1)S(1)}, u32[]{:S(2)}, u32[]{:S(2)}) collective-permute-start(bf16[2,4,96,768]{3,2,1,0:T(8,128)(2,1)} %get-tuple-element.73.zone_ref), channel_id=1, source_target_pairs={{0,4},{4,0},{8,12},{12,8},{16,20},{20,16},{24,28},{28,24},{1,5},{5... | collective-permute-start | bytes 3538952 | tf_op jit(solution)/shard_map/ppermute | solution.py:1479
  76.8 32.2 %collective-permute-start.1 = (bf16[2,4,96,768]{3,2,1,0:T(8,128)(2,1)}, bf16[2,4,96,768]{3,2,1,0:T(8,128)(2,1)S(1)}, u32[]{:S(2)}, u32[]{:S(2)}) collective-permute-start(bf16[2,4,96,768]{3,2,1,0:T(8,128)(2,1)} %get-tuple-element.73.zone_ref), channel_id=1, source_target_pairs={{0,2},{1,3},{2,0},{3,1},{4,6},{5,7},{6,4},{7,5},{8,10},{9,11},{10,... | collective-permute-start | bytes 3538952 | tf_op jit(solution)/shard_map/ppermute | solution.py:1480
  109.0 1.0 copy-start
  109.0 1.4 copy-start.1
  169.4 28.5 %collective-permute-start.2 = (bf16[2,4,96,768]{3,2,1,0:T(8,128)(2,1)}, bf16[2,4,96,768]{3,2,1,0:T(8,128)(2,1)S(1)}, u32[]{:S(2)}, u32[]{:S(2)}) collective-permute-start(bf16[2,4,96,768]{3,2,1,0:T(8,128)(2,1)} %get-tuple-element.82), channel_id=1, source_target_pairs={{0,4},{4,0},{8,12},{12,8},{16,20},{20,16},{24,28},{28,24},{1,5},{5... | collective-permute-start | bytes 3538952 | tf_op jit(solution)/shard_map/ppermute | solution.py:1496
  170.3 27.7 %collective-permute-start.3 = (bf16[8,96,768]{2,1,0:T(8,128)(2,1)}, bf16[8,96,768]{2,1,0:T(8,128)(2,1)S(1)}, u32[]{:S(2)}, u32[]{:S(2)}) collective-permute-start(bf16[8,96,768]{2,1,0:T(8,128)(2,1)} %get-tuple-element.83), channel_id=1, source_target_pairs={{0,2},{1,3},{2,0},{3,1},{4,6},{5,7},{6,4},{7,5},{8,10},{9,11},{10,... | collective-permute-start | bytes 3538952 | tf_op jit(solution)/shard_map/ppermute | solution.py:1497
  197.9 1.0 copy-start.2
  197.9 1.4 copy-start.3
  199.3 7.9 %copy-start.10 = (f32[2]{0:T(128)S(1)}, f32[2]{0:T(128)}, u32[]{:S(2)}) copy-start(f32[2]{0:T(128)} %decay_ref.1) | copy-start | bytes 28
  199.3 9.3 %copy-start.7 = (f32[4,8,768]{2,1,0:T(8,128)S(1)}, f32[4,8,768]{2,1,0:T(8,128)}, u32[]{:S(2)}) copy-start(f32[4,8,768]{2,1,0:T(8,128)} %get-tuple-element.100) | copy-start | bytes 294916
  199.3 9.3 %copy-start.6 = (f32[32,768]{1,0:T(8,128)S(1)}, f32[32,768]{1,0:T(8,128)}, u32[]{:S(2)}) copy-start(f32[32,768]{1,0:T(8,128)} %get-tuple-element.99) | copy-start | bytes 294916
  203.6 34.8 %collective-permute-start.4 = (bf16[4,96,768]{2,1,0:T(8,128)(2,1)}, bf16[4,96,768]{2,1,0:T(8,128)(2,1)S(1)}, u32[]{:S(2)}, u32[]{:S(2)}) collective-permute-start(bf16[4,96,768]{2,1,0:T(8,128)(2,1)} %get-tuple-element.104), channel_id=1, source_target_pairs={{0,2},{1,3},{2,0},{3,1},{4,6},{5,7},{6,4},{7,5},{8,10},{9,11},{10,... | collective-permute-start | bytes 1769480 | tf_op jit(solution)/shard_map/ppermute | solution.py:1501
  204.6 33.8 %collective-permute-start.5 = (bf16[4,96,768]{2,1,0:T(8,128)(2,1)}, bf16[4,96,768]{2,1,0:T(8,128)(2,1)S(1)}, u32[]{:S(2)}, u32[]{:S(2)}) collective-permute-start(bf16[4,96,768]{2,1,0:T(8,128)(2,1)} %get-tuple-element.106), channel_id=1, source_target_pairs={{0,4},{4,0},{8,12},{12,8},{16,20},{20,16},{24,28},{28,24},{1,5},{5... | collective-permute-start | bytes 1769480 | tf_op jit(solution)/shard_map/ppermute | solution.py:1502
  208.7 26.8 %copy-start.9 = (f32[8,192]{1,0:T(8,128)S(1)}, f32[8,192]{1,0:T(8,128)}, u32[]{:S(2)}) copy-start(f32[8,192]{1,0:T(8,128)} %get-tuple-element.101) | copy-start | bytes 18436
  208.7 27.6 %copy-start.8 = (f32[24,384]{1,0:T(8,128)S(1)}, f32[24,384]{1,0:T(8,128)}, u32[]{:S(2)}) copy-start(f32[24,384]{1,0:T(8,128)} %get-tuple-element.97) | copy-start | bytes 110596
  238.4 0.8 copy-start.4
  238.4 1.0 copy-start.5

commit v5 on v4

--- a/solution.py
+++ b/solution.py
@@ -104,9 +104,9 @@
 
 
 def enter_kernel(
-    owner_ref, slot_hbm, x_ref, pos_ref, vec_ref, turned_ref,
-    n1_ref, q_ref, k_ref, v_ref, cos_ref, sin_ref, qmark_ref, kmark_ref, weight_ref, zone_ref,
-    raw_ref, slot_ref, cross_ref, chain_ref, att_ref, zland_ref,
+    owner_ref, height_ref, width_ref, slot_hbm, x_ref, seg_ref, patch_rows_ref, patch_cols_ref, vec_ref,
+    n1_ref, q_ref, k_ref, v_ref, cos_ref, sin_ref, qmark_ref, kmark_ref, pos_ref, weight_ref, zone_ref,
+    wide_ref, turned_ref, raw_ref, slot_ref, cross_ref, chain_ref, att_ref, zland_ref,
     cross_sem, chain_sem, relay_sem, att_sem, send_sem, local_sem,
 ):
     z, x, y, c = place()
@@ -129,14 +129,27 @@
 
     tokens = x_ref.shape[0]
     half = cos_ref.shape[0]
-    last = turned_ref.shape[1] - 1
+    last = vec_ref.shape[0] - 1
     tiles = tokens // TILE
+    wide_ref[...] = jnp.zeros_like(wide_ref)
+    wide_ref[0 : last + 1, :] = vec_ref[...]
+    turned_ref[...] = wide_ref[...].T
+    tall = jnp.zeros(seg_ref.shape, F32)
+    broad = jnp.zeros(seg_ref.shape, F32)
+    for image in range(height_ref.shape[0]):
+        match = seg_ref[...] == image
+        tall = jnp.where(match, height_ref[image].astype(F32), tall)
+        broad = jnp.where(match, width_ref[image].astype(F32), broad)
+    pos_ref[...] = jnp.zeros_like(pos_ref)
+    pos_ref[0:1, :] = patch_cols_ref[...].astype(F32) * GRID_BASE / broad
+    pos_ref[1:2, :] = patch_rows_ref[...].astype(F32) * GRID_BASE / tall
+    pos_ref[2:3, :] = seg_ref[...].astype(F32)
 
     def prepare(i, carry):
         t = pl.ds(pl.multiple_of(i * TILE, TILE), TILE)
         unit, _ = normed(x_ref[t, :].astype(F32))
         n1_ref[:, t] = (unit * vec_ref[0:1, :] + vec_ref[1:2, :]).astype(BF).T
-        angle = turned_ref[half:, last:] * pos_ref[1:2, t] + turned_ref[:half, last:] * pos_ref[0:1, t]
+        angle = turned_ref[half:, last : last + 1] * pos_ref[1:2, t] + turned_ref[:half, last : last + 1] * pos_ref[0:1, t]
         cos_ref[:, t] = jnp.cos(angle)
         sin_ref[:, t] = jnp.sin(angle)
         seg = pos_ref[2:3, t].astype(jnp.int32)
@@ -319,7 +332,7 @@
     last_out.wait()
 
 
-def enter(owner, slot, x, pos, vec, turned):
+def enter(owner, heights, widths, slot, x, segment, patch_rows, patch_cols, vec):
     rows, width = x.shape
     half = width // 2
     n_dp, share, _ = slot.shape
@@ -330,16 +343,19 @@
     out = lambda n, dtype: jax.ShapeDtypeStruct((n, rows), dtype)
     return pl.pallas_call(
         enter_kernel,
-        in_specs=[smem, hbm, vmem, vmem, vmem, vmem],
-        out_specs=[vmem] * 8 + [hbm] * 2,
+        in_specs=[smem, smem, smem, hbm] + [vmem] * 5,
+        out_specs=[vmem] * 9 + [hbm] * 2,
         out_shape=[out(width, BF)] * 4
         + [out(half, F32)] * 2
         + [out(16, BF)] * 2
+        + [out(8, F32)]
         + [
             jax.ShapeDtypeStruct((n_mlp, n_dp, share, width), BF),
             jax.ShapeDtypeStruct((2, 4, share, width), BF),
         ],
         scratch_shapes=[
+            pltpu.VMEM((16, width), F32),
+            pltpu.VMEM((width, 16), F32),
             pltpu.VMEM((n_dp, share, width), F32),
             pltpu.VMEM((n_dp, share, width), BF),
             pltpu.VMEM((4, share, width), BF),
@@ -354,10 +370,13 @@
             pltpu.SemaphoreType.DMA((3,)),
         ],
         compiler_params=pltpu.CompilerParams(
-            vmem_limit_bytes=VMEM_LIMIT, collective_id=0, has_side_effects=True
+            vmem_limit_bytes=31 * 1024 * 1024, collective_id=0, has_side_effects=True
         ),
         name="enter",
-    )(owner, slot, x, pos, vec, turned)
+    )(
+        owner, heights, widths, slot, x,
+        *(a.reshape(1, rows) for a in (segment, patch_rows, patch_cols)), vec,
+    )
 
 
 def project_kernel(
@@ -487,7 +506,7 @@
             jax.ShapeDtypeStruct(q.shape, BF),
             jax.ShapeDtypeStruct((8 * HEADS, q.shape[1]), F32),
         ],
-        compiler_params=pltpu.CompilerParams(vmem_limit_bytes=VMEM_LIMIT),
+        compiler_params=pltpu.CompilerParams(vmem_limit_bytes=9 * 1024 * 1024),
         name="attend",
     )(heights, widths, q, k, v, qmark, kmark)
 
@@ -594,7 +613,7 @@
         out_shape=outs,
         scratch_shapes=[pltpu.VMEM((half, tokens), F32)] * 3
         + [pltpu.VMEM((half // 2, tokens), F32)],
-        compiler_params=pltpu.CompilerParams(vmem_limit_bytes=VMEM_LIMIT),
+        compiler_params=pltpu.CompilerParams(vmem_limit_bytes=18 * 1024 * 1024),
         name="attend_back",
     )(heights, widths, q, k, v, qmark, kmark, log_totals, do, pos, cosine, sine)
 
@@ -983,7 +1002,7 @@
             dma((2, n_mlp, n_dp)), dma((2, 2)), dma((48,)), dma((25,)), dma((18,)),
         ],
         compiler_params=pltpu.CompilerParams(
-            vmem_limit_bytes=VMEM_LIMIT, collective_id=1, has_side_effects=True
+            vmem_limit_bytes=48 * 1024 * 1024, collective_id=1, has_side_effects=True
         ),
         name="center",
     )(x, g, o, vec, weights, zone, xzone, yzone)
@@ -1016,13 +1035,14 @@
         in_specs=[vmem] * 4,
         out_specs=[vmem] * 4,
         out_shape=[jax.ShapeDtypeStruct((4,) + upstay.shape[2:], BF)] * 4,
-        compiler_params=pltpu.CompilerParams(vmem_limit_bytes=VMEM_LIMIT),
+        compiler_params=pltpu.CompilerParams(vmem_limit_bytes=6 * 1024 * 1024),
         name="merge",
     )(upstay, upgot, downstay, downgot)
 
 
 def leave_kernel(
-    owner_ref, n1_ref, dq0_ref, dq1_ref, dk0_ref, dk1_ref, dv0_ref, dv1_ref, vec_ref, small_ref,
+    owner_ref, n1_ref, dq0_ref, dq1_ref, dk0_ref, dk1_ref, dv0_ref, dv1_ref, vec_ref,
+    freq0_ref, freq1_ref, bias0_ref, bias1_ref, mid_ref, dc_ref,
     upstay_ref, upgot_ref, downstay_ref, downgot_ref, x_hbm, dh_hbm, weight_hbm, dwo_hbm,
     dx_ref, grad_ref, total_ref,
     x_ref, dh_ref, weight_ref, rows_ref,
@@ -1247,9 +1267,22 @@
     begin(groups[0])
     lax.fori_loop(3, tokens // TILE, middle, 0)
 
-    sums_ref[0] = small_ref[...]
-    sums_ref[0, 0:1, :] = jnp.sum(rows_ref[0:8, :], axis=0, keepdims=True)
-    sums_ref[0, 1:2, :] = jnp.sum(rows_ref[8:16, :], axis=0, keepdims=True)
+    def eight(ref, index):
+        return jnp.sum(ref[8 * index : 8 * index + 8, :], axis=0, keepdims=True)
+
+    ups = dc_ref.shape[0]
+    sums_ref[0, 0:1, :] = eight(rows_ref, 0)
+    sums_ref[0, 1:2, :] = eight(rows_ref, 1)
+    for index in range(3):
+        sums_ref[0, 2 + index : 3 + index, 0:half] = bias0_ref[8 * index : 8 * index + 1, :]
+        sums_ref[0, 2 + index : 3 + index, half:width] = bias1_ref[8 * index : 8 * index + 1, :]
+        sums_ref[0, 5 + index : 6 + index, :] = eight(mid_ref, index)
+    for index in range(ups):
+        sums_ref[0, 8 + index : 9 + index, :] = dc_ref[index, 0:1, :]
+    sums_ref[0, 8 + ups : 9 + ups, :] = eight(mid_ref, 3)
+    sums_ref[0, 9 + ups : 10 + ups, :] = jnp.concatenate(
+        [freq0_ref[0:1, :], freq1_ref[0:1, :], freq0_ref[1:2, :], freq1_ref[1:2, :]], axis=1
+    )
     hop(0, partner)
     forward(groups[1])
     ahead(6)
@@ -1294,7 +1327,7 @@
                 arrived(piece, relay_sem.at[near, kind, part])
 
 
-def leave(owner, x, dh, n1, flows, vec, weights, dwo, small, rest):
+def leave(owner, x, dh, n1, flows, vec, weights, dwo, smalls, rest):
     tokens, width = x.shape
     n_mlp, n_dp, share, _ = weights.shape
     smem = pl.BlockSpec(memory_space=pltpu.SMEM)
@@ -1305,12 +1338,12 @@
     flat = [ref for pair in flows for ref in pair]
     return pl.pallas_call(
         leave_kernel,
-        in_specs=[smem] + [vmem] * 13 + [hbm] * 4,
+        in_specs=[smem] + [vmem] * 18 + [hbm] * 4,
         out_specs=[vmem] * 3,
         out_shape=[
             jax.ShapeDtypeStruct((tokens, width), F32),
             jax.ShapeDtypeStruct((n_dp, share, width), BF),
-            jax.ShapeDtypeStruct(small.shape, F32),
+            jax.ShapeDtypeStruct(vec.shape, F32),
         ],
         scratch_shapes=[
             pltpu.VMEM((tokens, width), BF),
@@ -1319,24 +1352,25 @@
             pltpu.VMEM((16, width), F32),
             part(n_mlp, n_dp), part(2, n_dp), part(4), part(4), part(2), part(2), part(3, 4),
             part(2, 3, 4), part(2, 4), part(4),
-            pltpu.VMEM((7,) + small.shape, F32),
-            pltpu.VMEM((4,) + small.shape, F32),
+            pltpu.VMEM((7,) + vec.shape, F32),
+            pltpu.VMEM((4,) + vec.shape, F32),
             dma((2, 4)), dma((4,)), dma((4,)), dma((2,)), dma((2,)), dma((2, 3, 4)), dma((2, 3, 4)),
             dma((4,)), dma((7,)), dma((32,)), dma((4,)),
         ],
         compiler_params=pltpu.CompilerParams(
-            vmem_limit_bytes=VMEM_LIMIT, collective_id=2, has_side_effects=True
+            vmem_limit_bytes=38 * 1024 * 1024, collective_id=2, has_side_effects=True
         ),
         name="leave",
     )(
-        owner, n1, *flat, vec, small, *rest, x, dh, weights,
+        owner, n1, *flat, vec, *smalls, *rest, x, dh, weights,
         dwo.reshape(n_dp, share, width),
     )
 
 
 def update_kernel(
-    keep_ref, decay_ref, grad_ref, left_hbm, right_hbm, lroot_hbm, rroot_hbm, master_hbm, y_hbm, dx_hbm,
-    slot_out, left_out, right_out, master_out, y_out, dx_out,
+    owner_ref, decay_ref, grad_ref, total_ref, moment_ref, vec_ref,
+    left_hbm, right_hbm, lroot_hbm, rroot_hbm, master_hbm, y_hbm, dx_hbm,
+    small_out, moment_out, vec_out, slot_out, left_out, right_out, master_out, y_out, dx_out,
     left_ref, right_ref, lroot_ref, rroot_ref, master_ref, y_ref, dx_ref, slot_ref, turn_ref,
     in_sem, out_sem,
 ):
@@ -1353,7 +1387,9 @@
         outs.append(pltpu.make_async_copy(source, target, out_sem.at[len(outs)]))
         outs[-1].start()
 
-    held = keep_ref[0] != 0
+    d = lax.axis_index("dp")
+    m = lax.axis_index("mlp")
+    held = (owner_ref[m, 0] == d) | (owner_ref[m, 1] == d) | (owner_ref[m, 2] == d)
     decay = decay_ref[0]
     width = grad_ref.shape[0]
     tall = width // 3
@@ -1370,6 +1406,20 @@
         slot_ref[...] = jnp.zeros_like(slot_ref)
 
     emit(slot_ref, slot_out)
+
+    def own(ref):
+        cut = small_out.shape[1]
+        value = ref[:, 0:cut]
+        for index in range(1, owner_ref.shape[0]):
+            value = lax.select(m == index, ref[:, index * cut : (index + 1) * cut], value)
+        return value
+
+    slow = decay_ref[1]
+    small = own(total_ref)
+    moment = slow * own(moment_ref) + (1.0 - slow) * small * small
+    small_out[...] = small
+    moment_out[...] = moment
+    vec_out[...] = own(vec_ref) - RATE_VECTOR * small / (jnp.sqrt(moment) + STEP_EPSILON)
     loads[0].wait()
 
     @pl.when(held)
@@ -1424,7 +1474,9 @@
         copy.wait()
 
 
-def update(owns, decays, grad, left, right, lroot, rroot, master, output, input_grad):
+def update(
+    owner, decays, grad, total, moments, vectors, left, right, lroot, rroot, master, output, input_grad
+):
     smem = pl.BlockSpec(memory_space=pltpu.SMEM)
     vmem = pl.BlockSpec(memory_space=pltpu.VMEM)
     hbm = pl.BlockSpec(memory_space=pl.ANY)
@@ -1432,14 +1484,17 @@
     room = lambda a: pltpu.VMEM(a.shape, a.dtype)
     return pl.pallas_call(
         update_kernel,
-        in_specs=[smem, smem, vmem] + [hbm] * 7,
-        out_specs=[hbm] * 6,
-        out_shape=[shape(a) for a in (left, left, right, master, output, input_grad)],
+        in_specs=[smem, smem] + [vmem] * 4 + [hbm] * 7,
+        out_specs=[vmem] * 3 + [hbm] * 6,
+        out_shape=[jax.ShapeDtypeStruct((total.shape[0], total.shape[1] // owner.shape[0]), F32)] * 3
+        + [shape(a) for a in (left, left, right, master, output, input_grad)],
         scratch_shapes=[room(a) for a in (left, right, lroot, rroot, master, output, input_grad, left, grad)]
         + [pltpu.SemaphoreType.DMA((7,)), pltpu.SemaphoreType.DMA((6,))],
-        compiler_params=pltpu.CompilerParams(vmem_limit_bytes=VMEM_LIMIT),
+        compiler_params=pltpu.CompilerParams(vmem_limit_bytes=26 * 1024 * 1024),
         name="update",
-    )(owns, decays, grad, left, right, lroot, rroot, master, output, input_grad)
+    )(
+        owner, decays, grad, total, moments, vectors, left, right, lroot, rroot, master, output, input_grad
+    )
 
 
 def positions(segment, heights, widths, patch_rows, patch_cols):
@@ -1457,28 +1512,26 @@
     tokens, cotangent, vectors, vector_moments, decays, owner, master_slots, left_slots,
     right_slots, left_roots, right_roots, grid_height, grid_width, patch_rows, patch_cols, segment,
 ):
-    dp_index = lax.axis_index("dp")
     mlp_index = lax.axis_index("mlp")
     n_dp = lax.axis_size("dp")
     n_mlp = lax.axis_size("mlp")
     width = tokens.shape[1]
     share = width // n_dp
     owner_row = jnp.take(owner, mlp_index, axis=0)
-    holds = owner_row == dp_index
-    owns = jnp.any(holds).astype(jnp.int32).reshape(1)
     master = master_slots[0, 0]
-    turned = vectors.T
-    pos = positions(segment, grid_height, grid_width, patch_rows, patch_cols)
     direct = n_dp == 8 and n_mlp == 4
     if direct:
-        n1t, q, k, v, cosine, sine, qmark, kmark, attention, zone = enter(
-            owner, master.reshape(n_dp, share, width), tokens, pos, vectors, turned
+        n1t, q, k, v, cosine, sine, qmark, kmark, pos, attention, zone = enter(
+            owner, grid_height, grid_width, master.reshape(n_dp, share, width), tokens, segment,
+            patch_rows, patch_cols, vectors,
         )
         over_x = [(i, i ^ 1) for i in range(n_dp)]
         over_y = [(i, i ^ 2) for i in range(n_mlp)]
         xzone = lax.ppermute(zone, "dp", over_x)
         yzone = lax.ppermute(zone, "mlp", over_y)
     else:
+        turned = vectors.T
+        pos = positions(segment, grid_height, grid_width, patch_rows, patch_cols)
         slot = master.astype(BF).reshape(n_dp, share, width)
         pieces = lax.all_to_all(slot, "dp", 0, 0, tiled=True)
         mine = jnp.take(pieces, owner_row, axis=0)
@@ -1508,18 +1561,18 @@
         first = back(q, k, v, qmark, kmark, log_totals, do, pos, cosine, sine, 0)
     second = back(q, k, v, qmark, kmark, log_totals, do, pos, cosine, sine, 1)
     both = list(zip(first, second))
-    freq = jnp.concatenate(both[3], axis=1)[0:2].reshape(1, width)
-    bias = jnp.concatenate(both[4], axis=1)[0::8]
-    eights = lambda rows: jnp.sum(rows.reshape(-1, 8, width), axis=1)
-    mid = eights(mid_rows)
-    tail = [bias, mid[0:3], dc[:, 0, :], mid[3:4], freq]
     if direct:
-        small = jnp.concatenate([jnp.zeros((2, width), F32)] + tail, axis=0)
         input_grad, gradient, total = leave(
-            owner, tokens, dh, n1t, both[0:3], vectors, attention.reshape(fine), dwo, small,
+            owner, tokens, dh, n1t, both[0:3], vectors, attention.reshape(fine), dwo,
+            (*both[3], *both[4], mid_rows, dc),
             (upstay, upgot, downstay, downgot),
         )
     else:
+        freq = jnp.concatenate(both[3], axis=1)[0:2].reshape(1, width)
+        bias = jnp.concatenate(both[4], axis=1)[0::8]
+        eights = lambda rows: jnp.sum(rows.reshape(-1, 8, width), axis=1)
+        mid = eights(mid_rows)
+        tail = [bias, mid[0:3], dc[:, 0, :], mid[3:4], freq]
         dq, dk, dv = (jnp.concatenate(pair, axis=0) for pair in both[0:3])
         input_grad, datt, fin_rows = final_part(
             tokens, dh, n1t, dq, dk, dv, vectors, attention, dwo
@@ -1533,17 +1586,12 @@
         gradient = lax.all_to_all(jnp.take(reduced, kind_of, axis=0), "dp", 0, 0, tiled=True)
         total = lax.psum(jnp.concatenate([eights(fin_rows)] + tail, axis=0), ("dp", "mlp"))
     gradient = gradient.reshape(width, width)
-    slot_grad, left_out, right_out, master_out, output, input_grad = update(
-        owns, decays, gradient, left_slots[0, 0], right_slots[0, 0], left_roots[0, 0],
-        right_roots[0, 0], master, output, input_grad,
+    grad_share, moment_next, vector_next, slot_grad, left_out, right_out, master_out, output, input_grad = (
+        update(
+            owner, decays, gradient, total, vector_moments, vectors, left_slots[0, 0], right_slots[0, 0],
+            left_roots[0, 0], right_roots[0, 0], master, output, input_grad,
+        )
     )
-
-    cut = width // n_mlp
-    own = lambda table: lax.dynamic_slice_in_dim(table, mlp_index * cut, cut, 1)
-    grad_share = own(total)
-    decay = decays[1]
-    moment_next = decay * own(vector_moments) + (1.0 - decay) * grad_share * grad_share
-    vector_next = own(vectors) - RATE_VECTOR * grad_share / (jnp.sqrt(moment_next) + STEP_EPSILON)
     lift = lambda a: a[None, None]
     return (
         output, input_grad, lift(slot_grad), lift(left_out), lift(right_out), lift(master_out),

time: 327 us -> 309 us (0.945)
  Pallas kernels: 298 us -> 270 us
  local copies, waits for them, and re-layouts: 8.16 us -> 20.4 us
  other arithmetic: 7.27 us -> 0 us
  waiting for transfers between devices: 0.02 us -> 4.87 us
    unnamed x24 -> x82, local copies, waits for them, and re-layouts: 5.52 us -> 20.4 us
    pallas_call x3, Pallas kernels: 151 us -> 141 us  [the longest x1 66.8 us: leave(): pl.pallas_call(leave_kernel, in_specs=[smem] + [vmem] * 18 + [hbm] * 4, o...]
    pallas_call x2, Pallas kernels: 53.2 us -> 44.1 us  [attend_back(): pl.pallas_call(attend_back_kernel, grid=(1,), in_specs=[smem, smem, cut(q...]
    pallas_call x1, Pallas kernels: 30.7 us -> 23.6 us  [attend(): pl.pallas_call(attend_kernel, in_specs=[smem, smem] + [vmem] * 5, out_spe...]
    pallas_call x1, Pallas kernels: 4.31 us -> 0.53 us  [merge(): pl.pallas_call(merge_kernel, in_specs=[vmem] * 4, out_specs=[vmem] * 4, o...]
  transfers between devices with their start and end apart: 6 -> 6, of which waited for: 0 -> 3; matrix products, arithmetic and copies ran while one was open for 2% -> 0% of each run, Pallas kernels for 26% -> 22%
where the time goes in v5:
time: 309 us; the launch traced here: 303 us
  Pallas kernels  270 us (87%)
  local copies, waits for them, and re-layouts  20.4 us (7%)
  starting transfers between devices  6.5 us (2%)
  waiting for transfers between devices  4.87 us (2%)
    pallas_call x1, Pallas kernels, leave(): pl.pallas_call(leave_kernel, in_specs=[smem] + [vmem] * 18 + [hbm] * 4, o...  66.8 us
    pallas_call x1, Pallas kernels, enter(): pl.pallas_call(enter_kernel, in_specs=[smem, smem, smem, hbm] + [vmem] *...  65.9 us
    pallas_call x1, Pallas kernels, center(): pl.pallas_call(center_kernel, in_specs=[vmem] * 4 + [hbm] * 4, out_specs=...  61.2 us
    pallas_call x2, Pallas kernels, attend_back(): pl.pallas_call(attend_back_kernel, grid=(1,), in_specs=[smem, smem, cut(q...  44.1 us
    pallas_call x1, Pallas kernels, attend(): pl.pallas_call(attend_kernel, in_specs=[smem, smem] + [vmem] * 5, out_spe...  23.6 us
    unnamed x82, local copies, waits for them, and re-layouts  20.4 us
    pallas_call x1, Pallas kernels, update(): pl.pallas_call(update_kernel, in_specs=[smem, smem] + [vmem] * 4 + [hbm]...  7.87 us
  transfers between devices with their start and end apart: 6, of which 3 were waited for; matrix products, arithmetic and copies ran while one was open for 0% of the time, Pallas kernels for 22%

profile of v5, /device:TPU:0, one launch (start us, length us, event | category | flops | bytes accessed | tf_op | source)
XLA Modules:
  0.0 302.9 jit_solution(17522616726539414402)
XLA Ops:
  0.6 0.0 copy-start.1
  0.7 1.4 copy-done.1
  2.1 1.7 copy-done.3
  3.7 0.8 copy-done.17
  4.5 0.7 copy-done.28
  5.2 0.7 copy-done.30
  5.9 0.7 copy-done.32
  6.5 0.7 copy-done.34
  7.2 0.7 copy-done.35
  7.9 0.7 copy-done.36
  8.6 65.9 %enter.1 = (bf16[768,1024]{1,0:T(8,128)(2,1)S(1)}, bf16[768,1024]{1,0:T(8,128)(2,1)S(1)}, bf16[768,1024]{1,0:T(8,128)(2,1)S(1)}, bf16[768,1024]{1,0:T(8,128)(2,1...) custom-call(s32[4,3]{1,0:T(4,128)S(1)} %copy-done.28, ...), custom_call_target="tpu_custom_call" | custom-call | tf_op jit(solution)/shard_map/enter/pallas_call | solution.py:344
  74.5 0.0 copy-start.11
  74.5 1.1 copy-done.11
  75.6 1.5 collective-permute-start.1
  77.2 0.8 collective-permute-start
  78.0 23.6 %attend.1 = (bf16[768,1024]{1,0:T(8,128)(2,1)S(1)}, f32[96,1024]{1,0:T(8,128)S(1)}) custom-call(s32[4]{0:T(128)S(1)} %copy-done.30, s32[4]{0:T(128)S(1)} %copy-done.32, bf16[768,1024]{1,0:T(8,128)(2,1)S(1)} %get-tuple-element.69.q_ref, bf16[768,1024]{1,0:T(8,128)(2,1)S(1)} %get-tuple-element.70.k_ref, bf16[768,1024]{1,0:T(8,128)(2,1)S(1)} %get-tuple-element.71.v_ref, ...), custom_call_target="tpu_custom_call" | custom-call | tf_op jit(solution)/shard_map/attend/pallas_call | solution.py:501
  101.6 0.0 copy-start.13
  101.6 1.1 copy-done.13
  102.7 0.9 collective-permute-done.1.yzone_ref
  103.6 1.2 collective-permute-done.xzone_ref
  104.9 1.0 copy-done.40
  105.9 61.2 %center.1 = (bf16[1024,768]{1,0:T(8,128)(2,1)}, f32[1024,768]{1,0:T(8,128)}, bf16[768,1024]{1,0:T(8,128)(2,1)}, bf16[768,768]{1,0:T(8,128)(2,1)S(1)}, f32[32,768...) custom-call(bf16[1024,768]{1,0:T(8,128)(2,1)} %x_hbm.1, ...), custom_call_target="tpu_custom_call" | custom-call | tf_op jit(solution)/shard_map/center/pallas_call | solution.py:977
  167.1 0.0 copy-start.23
  167.2 0.6 copy-done.23
  167.8 0.6 copy-done.25
  168.4 1.0 copy-done.38
  169.4 2.1 collective-permute-start.3
  171.5 1.4 copy-done.5
  172.9 21.8 %attend_back.2 = (bf16[384,1024]{1,0:T(8,128)(2,1)S(1)}, bf16[384,1024]{1,0:T(8,128)(2,1)S(1)}, bf16[384,1024]{1,0:T(8,128)(2,1)S(1)}, f32[8,192]{1,0:T(8,128)S(1)}, f32[24,384]{1,0:T(8,128)S(1)}) custom-call(s32[4]{0:T(128)S(1)} %copy-done.31, s32[4]{0:T(128)S(1)} %copy-done.33, bf16[768,1024]{1,0:T(8,128)(2,1)S(1)} %get-tuple-element.69.q_ref, ...), custom_call_target="tpu_custom_call" | custom-call | tf_op jit(solution)/shard_map/attend_back/pallas_call | solution.py:607
  194.8 2.7 collective-permute-done.2.upgot_ref
  197.5 0.0 collective-permute-done.3.downgot_ref
  197.5 0.5 merge.1
  198.0 1.8 collective-permute-start.4
  199.8 0.3 collective-permute-start.5
  200.1 0.0 copy-start.26
  200.1 0.0 copy-start.29
  200.2 22.3 %attend_back.3 = (bf16[384,1024]{1,0:T(8,128)(2,1)S(1)}, bf16[384,1024]{1,0:T(8,128)(2,1)S(1)}, bf16[384,1024]{1,0:T(8,128)(2,1)S(1)}, f32[8,192]{1,0:T(8,128)S(1)}, f32[24,384]{1,0:T(8,128)S(1)}) custom-call(s32[4]{0:T(128)S(1)} %copy-done.31, s32[4]{0:T(128)S(1)} %copy-done.33, bf16[768,1024]{1,0:T(8,128)(2,1)S(1)} %get-tuple-element.69.q_ref, ...), custom_call_target="tpu_custom_call" | custom-call | tf_op jit(solution)/shard_map/attend_back/pallas_call | solution.py:607
  222.4 0.0 copy-start.19
  222.4 0.8 copy-done.19
  223.3 0.8 copy-done.21
  224.1 0.0 copy-start.20
  224.1 1.1 copy-done.20
  225.2 1.1 copy-done.22
  226.3 0.0 copy-start.27
  226.3 0.0 copy-start.37
  226.3 66.8 %leave.1 = (f32[1024,768]{1,0:T(8,128)S(1)}, bf16[8,96,768]{2,1,0:T(8,128)(2,1)S(1)}, f32[14,768]{1,0:T(8,128)S(1)}) custom-call(s32[4,3]{1,0:T(4,128)S(1)} %copy-done.29, bf16[768,1024]{1,0:T(8,128)(2,1)S(1)} %copy-done.12, bf16[384,1024]{1,0:T(8,128)(2,1)S(1)} %get-tuple-element.89.dq0_ref, bf16[384,1024]{1,0:T(8,128)(2,1)S(1)} %get-tuple-element.97.dq1_ref, ...), custom_call_target="tpu_custom_call" | custom-call | tf_op jit(solution)/shard_map/leave/pallas_call | solution.py:1339
  293.2 1.7 copy-done.9
  294.8 7.9 %update.1 = (f32[14,192]{1,0:T(8,128)}, f32[14,192]{1,0:T(8,128)}, f32[14,192]{1,0:T(8,128)}, f32[768,768]{1,0:T(8,128)}, f32[768,768]{1,0:T(8,128)}, /*index=5*...) custom-call(s32[4,3]{1,0:T(4,128)S(1)} %copy-done.29, f32[2]{0:T(128)S(1)} %copy-done.37, ...), custom_call_target="tpu_custom_call" | custom-call | tf_op jit(solution)/shard_map/update/pallas_call | solution.py:1485
  (54 shorter events, 0.1 us)
Async XLA Ops:
  0.6 1.4 copy-start.1
  2.1 1.7 copy-start.3
  3.7 0.8 copy-start.17
  4.5 0.7 copy-start.28
  5.2 0.7 copy-start.30
  5.9 0.7 copy-start.32
  6.5 0.7 copy-start.34
  7.2 0.7 copy-start.35
  7.9 0.7 copy-start.36
  74.5 1.1 copy-start.11
  75.6 25.9 %copy-start = (bf16[4,8,96,768]{3,2,1,0:T(8,128)(2,1)}, bf16[4,8,96,768]{3,2,1,0:T(8,128)(2,1)S(1)}, u32[]{:S(2)}) copy-start(bf16[4,8,96,768]{3,2,1,0:T(8,128)(2,1)S(1)} %get-tuple-element.76.weight_ref.weight_hbm) | copy-start | bytes 14155780
  75.6 30.2 %copy-start.16 = (bf16[2,4,96,768]{3,2,1,0:T(8,128)(2,1)}, bf16[2,4,96,768]{3,2,1,0:T(8,128)(2,1)S(1)}, u32[]{:S(2)}) copy-start(bf16[2,4,96,768]{3,2,1,0:T(8,128)(2,1)S(1)} %get-tuple-element.77.zone_ref) | copy-start | bytes 3538948
  75.6 28.0 %collective-permute-start.1 = (bf16[2,4,96,768]{3,2,1,0:T(8,128)(2,1)S(1)}, bf16[2,4,96,768]{3,2,1,0:T(8,128)(2,1)S(1)}, u32[]{:S(2)}, u32[]{:S(2)}) collective-permute-start(bf16[2,4,96,768]{3,2,1,0:T(8,128)(2,1)S(1)} %get-tuple-element.77.zone_ref), channel_id=1, source_target_pairs={{0,2},{1,3},{2,0},{3,1},{4,6},{5,7},{6,4},{7,5},{8,10},{9,11},{10,... | collective-permute-start | bytes 3538952 | tf_op jit(solution)/shard_map/ppermute | solution.py:1531
  77.2 27.7 %collective-permute-start = (bf16[2,4,96,768]{3,2,1,0:T(8,128)(2,1)S(1)}, bf16[2,4,96,768]{3,2,1,0:T(8,128)(2,1)S(1)}, u32[]{:S(2)}, u32[]{:S(2)}) collective-permute-start(bf16[2,4,96,768]{3,2,1,0:T(8,128)(2,1)S(1)} %get-tuple-element.77.zone_ref), channel_id=1, source_target_pairs={{0,4},{4,0},{8,12},{12,8},{16,20},{20,16},{24,28},{28,24},{1,5},{5... | collective-permute-start | bytes 3538952 | tf_op jit(solution)/shard_map/ppermute | solution.py:1530
  78.0 27.9 %copy-start.18 = (f32[14,768]{1,0:T(8,128)S(1)}, f32[14,768]{1,0:T(8,128)}, u32[]{:S(2)}) copy-start(f32[14,768]{1,0:T(8,128)} %vec_ref.7) | copy-start | bytes 129028
  101.6 1.1 copy-start.13
  103.6 1.2 copy-start.39
  104.9 1.0 copy-start.40
  105.9 65.6 %copy-start.31 = (s32[4]{0:T(128)S(1)}, s32[4]{0:T(128)}, u32[]{:S(2)}) copy-start(s32[4]{0:T(128)} %height_ref.7) | copy-start | bytes 52
  105.9 65.6 %copy-start.33 = (s32[4]{0:T(128)S(1)}, s32[4]{0:T(128)}, u32[]{:S(2)}) copy-start(s32[4]{0:T(128)} %width_ref.7) | copy-start | bytes 52
  167.1 0.6 copy-start.23
  167.8 0.6 copy-start.25
  168.4 1.0 copy-start.38
  169.4 25.3 %copy-start.14 = (bf16[768,768]{1,0:T(8,128)(2,1)}, bf16[768,768]{1,0:T(8,128)(2,1)S(1)}, u32[]{:S(2)}) copy-start(bf16[768,768]{1,0:T(8,128)(2,1)S(1)} %get-tuple-element.113) | copy-start | bytes 3538948
  169.4 28.0 %collective-permute-start.2 = (bf16[2,4,96,768]{3,2,1,0:T(8,128)(2,1)}, bf16[2,4,96,768]{3,2,1,0:T(8,128)(2,1)S(1)}, u32[]{:S(2)}, u32[]{:S(2)}) collective-permute-start(bf16[2,4,96,768]{3,2,1,0:T(8,128)(2,1)} %get-tuple-element.87), channel_id=1, source_target_pairs={{0,4},{4,0},{8,12},{12,8},{16,20},{20,16},{24,28},{28,24},{1,5},{5... | collective-permute-start | bytes 3538952 | tf_op jit(solution)/shard_map/ppermute | solution.py:1549
  169.4 28.0 %collective-permute-start.3 = (bf16[8,96,768]{2,1,0:T(8,128)(2,1)}, bf16[8,96,768]{2,1,0:T(8,128)(2,1)S(1)}, u32[]{:S(2)}, u32[]{:S(2)}) collective-permute-start(bf16[8,96,768]{2,1,0:T(8,128)(2,1)} %copy-done.38), channel_id=1, source_target_pairs={{0,2},{1,3},{2,0},{3,1},{4,6},{5,7},{6,4},{7,5},{8,10},{9,11},{10,... | collective-permute-start | bytes 3538952 | tf_op jit(solution)/shard_map/ppermute | solution.py:1550
  171.5 1.4 copy-start.5
  198.0 24.4 %collective-permute-start.4 = (bf16[4,96,768]{2,1,0:T(8,128)(2,1)S(1)}, bf16[4,96,768]{2,1,0:T(8,128)(2,1)S(1)}, u32[]{:S(2)}, u32[]{:S(2)}) collective-permute-start(bf16[4,96,768]{2,1,0:T(8,128)(2,1)S(1)} %get-tuple-element.109), channel_id=1, source_target_pairs={{0,2},{1,3},{2,0},{3,1},{4,6},{5,7},{6,4},{7,5},{8,10},{9,11},{10,... | collective-permute-start | bytes 1769480 | tf_op jit(solution)/shard_map/ppermute | solution.py:1554
  199.8 23.4 %collective-permute-start.5 = (bf16[4,96,768]{2,1,0:T(8,128)(2,1)S(1)}, bf16[4,96,768]{2,1,0:T(8,128)(2,1)S(1)}, u32[]{:S(2)}, u32[]{:S(2)}) collective-permute-start(bf16[4,96,768]{2,1,0:T(8,128)(2,1)S(1)} %get-tuple-element.111), channel_id=1, source_target_pairs={{0,4},{4,0},{8,12},{12,8},{16,20},{20,16},{24,28},{28,24},{1,5},{5... | collective-permute-start | bytes 1769480 | tf_op jit(solution)/shard_map/ppermute | solution.py:1555
  200.1 24.0 %copy-start.2 = (bf16[1024,768]{1,0:T(8,128)(2,1)S(1)}, bf16[1024,768]{1,0:T(8,128)(2,1)}, u32[]{:S(2)}) copy-start(bf16[1024,768]{1,0:T(8,128)(2,1)} %x_hbm.1) | copy-start | bytes 4718596
  200.1 24.0 %copy-start.12 = (bf16[768,1024]{1,0:T(8,128)(2,1)S(1)}, bf16[768,1024]{1,0:T(8,128)(2,1)}, u32[]{:S(2)}) copy-start(bf16[768,1024]{1,0:T(8,128)(2,1)} %copy-done.11) | copy-start | bytes 4718596
  200.1 24.0 %copy-start.15 = (bf16[768,768]{1,0:T(8,128)(2,1)S(1)}, bf16[768,768]{1,0:T(8,128)(2,1)}, u32[]{:S(2)}) copy-start(bf16[768,768]{1,0:T(8,128)(2,1)} %copy-done.14) | copy-start | bytes 3538948
  200.1 24.0 %copy-start.24 = (f32[32,768]{1,0:T(8,128)S(1)}, f32[32,768]{1,0:T(8,128)}, u32[]{:S(2)}) copy-start(f32[32,768]{1,0:T(8,128)} %copy-done.23) | copy-start | bytes 294916
  200.1 24.0 %copy-start.26 = (f32[4,8,768]{2,1,0:T(8,128)S(1)}, f32[4,8,768]{2,1,0:T(8,128)}, u32[]{:S(2)}) copy-start(f32[4,8,768]{2,1,0:T(8,128)} %copy-done.25) | copy-start | bytes 294916
  200.1 24.0 %copy-start.29 = (s32[4,3]{1,0:T(4,128)S(1)}, s32[4,3]{1,0:T(4,128)}, u32[]{:S(2)}) copy-start(s32[4,3]{1,0:T(4,128)} %owner_ref.5) | copy-start | bytes 148
  222.4 0.8 copy-start.19
  223.3 0.8 copy-start.21
  224.1 1.1 copy-start.20
  225.2 1.1 copy-start.22
  226.2 66.9 %copy-start.4 = (f32[1,1,768,768]{3,2,1,0:T(8,128)S(1)}, f32[1,1,768,768]{3,2,1,0:T(8,128)}, u32[]{:S(2)}) copy-start(f32[1,1,768,768]{3,2,1,0:T(8,128)} %param.22) | copy-start | bytes 7077892
  226.2 66.9 %copy-start.6 = (f32[1,1,768,768]{3,2,1,0:T(8,128)S(1)}, f32[1,1,768,768]{3,2,1,0:T(8,128)}, u32[]{:S(2)}) copy-start(f32[1,1,768,768]{3,2,1,0:T(8,128)} %param.23) | copy-start | bytes 7077892
  226.2 66.9 %copy-start.7 = (f32[1,1,768,768]{3,2,1,0:T(8,128)S(1)}, f32[1,1,768,768]{3,2,1,0:T(8,128)}, u32[]{:S(2)}) copy-start(f32[1,1,768,768]{3,2,1,0:T(8,128)} %param.24) | copy-start | bytes 7077892
  226.2 66.9 %copy-start.8 = (f32[1,1,768,768]{3,2,1,0:T(8,128)S(1)}, f32[1,1,768,768]{3,2,1,0:T(8,128)}, u32[]{:S(2)}) copy-start(f32[1,1,768,768]{3,2,1,0:T(8,128)} %param.25) | copy-start | bytes 7077892
  226.3 66.9 %copy-start.10 = (bf16[1024,768]{1,0:T(8,128)(2,1)S(1)}, bf16[1024,768]{1,0:T(8,128)(2,1)}, u32[]{:S(2)}) copy-start(bf16[1024,768]{1,0:T(8,128)(2,1)} %get-tuple-element.116.y_hbm) | copy-start | bytes 4718596
  226.3 66.9 %copy-start.27 = (f32[14,768]{1,0:T(8,128)S(1)}, f32[14,768]{1,0:T(8,128)}, u32[]{:S(2)}) copy-start(f32[14,768]{1,0:T(8,128)} %moment_ref.1) | copy-start | bytes 129028
  226.3 66.9 %copy-start.37 = (f32[2]{0:T(128)S(1)}, f32[2]{0:T(128)}, u32[]{:S(2)}) copy-start(f32[2]{0:T(128)} %decay_ref.1) | copy-start | bytes 28
  293.2 1.7 copy-start.9

commit v6 on v5

--- a/solution.py
+++ b/solution.py
@@ -370,7 +370,7 @@
             pltpu.SemaphoreType.DMA((3,)),
         ],
         compiler_params=pltpu.CompilerParams(
-            vmem_limit_bytes=31 * 1024 * 1024, collective_id=0, has_side_effects=True
+            vmem_limit_bytes=60 * 1024 * 1024, collective_id=0, has_side_effects=True
         ),
         name="enter",
     )(
@@ -506,7 +506,7 @@
             jax.ShapeDtypeStruct(q.shape, BF),
             jax.ShapeDtypeStruct((8 * HEADS, q.shape[1]), F32),
         ],
-        compiler_params=pltpu.CompilerParams(vmem_limit_bytes=9 * 1024 * 1024),
+        compiler_params=pltpu.CompilerParams(vmem_limit_bytes=60 * 1024 * 1024),
         name="attend",
     )(heights, widths, q, k, v, qmark, kmark)
 

time: 309 us -> 305 us (0.987)
  the two profiles are of different devices: /device:TPU:0 before, /device:TPU:4 now
where the time goes in v6:
time: 305 us; the launch traced here: 301 us
  Pallas kernels  283 us (93%)
  local copies, waits for them, and re-layouts  9.6 us (3%)
  starting transfers between devices  5.26 us (2%)
    pallas_call x1, Pallas kernels, enter(): pl.pallas_call(enter_kernel, in_specs=[smem, smem, smem, hbm] + [vmem] *...  69.5 us
    pallas_call x1, Pallas kernels, leave(): pl.pallas_call(leave_kernel, in_specs=[smem] + [vmem] * 18 + [hbm] * 4, o...  64.9 us
    pallas_call x1, Pallas kernels, center(): pl.pallas_call(center_kernel, in_specs=[vmem] * 4 + [hbm] * 4, out_specs=...  62.9 us
    pallas_call x2, Pallas kernels, attend_back(): pl.pallas_call(attend_back_kernel, grid=(1,), in_specs=[smem, smem, cut(q...  45.2 us
    pallas_call x1, Pallas kernels, attend(): pl.pallas_call(attend_kernel, in_specs=[smem, smem] + [vmem] * 5, out_spe...  28.8 us
    pallas_call x1, Pallas kernels, update(): pl.pallas_call(update_kernel, in_specs=[smem, smem] + [vmem] * 4 + [hbm]...  11 us
    unnamed x72, local copies, waits for them, and re-layouts  9.6 us
  transfers between devices with their start and end apart: 6, of which 2 were waited for; matrix products, arithmetic and copies ran while one was open for 0% of the time, Pallas kernels for 25%

profile of v6, /device:TPU:4, one launch (start us, length us, event | category | flops | bytes accessed | tf_op | source)
XLA Modules:
  0.0 301.4 jit_solution(18348436274717812011)
XLA Ops:
  0.6 69.5 %enter.1 = (bf16[768,1024]{1,0:T(8,128)(2,1)}, bf16[768,1024]{1,0:T(8,128)(2,1)}, bf16[768,1024]{1,0:T(8,128)(2,1)}, bf16[768,1024]{1,0:T(8,128)(2,1)}, f32[384,...) custom-call(s32[4,3]{1,0:T(4,128)} %owner_ref.5, ...), custom_call_target="tpu_custom_call" | custom-call | tf_op jit(solution)/shard_map/enter/pallas_call | solution.py:344
  70.2 0.6 collective-permute-start.1
  70.7 0.5 collective-permute-start
  71.3 28.8 %attend.1 = (bf16[768,1024]{1,0:T(8,128)(2,1)}, f32[96,1024]{1,0:T(8,128)}) custom-call(s32[4]{0:T(128)} %height_ref.7, s32[4]{0:T(128)} %width_ref.7, bf16[768,1024]{1,0:T(8,128)(2,1)} %get-tuple-element.69.q_ref, bf16[768,1024]{1,0:T(8,128)(2,1)} %get-tuple-element.70.k_ref, bf16[768,1024]{1,0:T(8,128)(2,1)} %get-tuple-element.71.v_ref, ...), custom_call_target="tpu_custom_call" | custom-call | tf_op jit(solution)/shard_map/attend/pallas_call | solution.py:501
  100.0 0.0 collective-permute-done.1.yzone_ref
  100.0 0.0 collective-permute-done.xzone_ref
  100.1 0.0 copy-start.35
  100.1 1.0 copy-done.34
  101.1 0.4 copy-done.35
  101.5 0.0 copy-start.12
  101.5 0.0 copy-start.31
  101.5 0.0 copy-start.32
  101.5 62.9 %center.1 = (bf16[1024,768]{1,0:T(8,128)(2,1)}, f32[1024,768]{1,0:T(8,128)}, bf16[768,1024]{1,0:T(8,128)(2,1)}, bf16[768,768]{1,0:T(8,128)(2,1)S(1)}, f32[32,768...) custom-call(bf16[1024,768]{1,0:T(8,128)(2,1)} %x_hbm.1, ...), custom_call_target="tpu_custom_call" | custom-call | tf_op jit(solution)/shard_map/center/pallas_call | solution.py:977
  164.4 0.0 copy-start.25
  164.5 0.6 copy-done.25
  165.1 0.6 copy-done.27
  165.7 0.4 collective-permute-start.2
  166.2 1.6 collective-permute-start.3
  167.8 0.0 copy-done.5
  167.8 0.0 copy-done.6
  167.8 0.0 copy-done.12
  167.8 0.0 copy-done.22
  167.8 0.0 copy-done.23
  167.8 0.0 copy-done.24
  167.8 1.4 copy-done.7
  169.2 22.4 %attend_back.2 = (bf16[384,1024]{1,0:T(8,128)(2,1)S(1)}, bf16[384,1024]{1,0:T(8,128)(2,1)S(1)}, bf16[384,1024]{1,0:T(8,128)(2,1)S(1)}, f32[8,192]{1,0:T(8,128)S(1)}, f32[24,384]{1,0:T(8,128)S(1)}) custom-call(s32[4]{0:T(128)S(1)} %copy-done.31, s32[4]{0:T(128)S(1)} %copy-done.32, bf16[768,1024]{1,0:T(8,128)(2,1)S(1)} %copy-done.1, ...), custom_call_target="tpu_custom_call" | custom-call | tf_op jit(solution)/shard_map/attend_back/pallas_call | solution.py:607
  191.6 2.2 collective-permute-done.2.upgot_ref
  193.9 0.2 collective-permute-done.3.downgot_ref
  194.1 0.5 merge.1
  194.6 1.4 collective-permute-start.4
  196.0 0.7 collective-permute-start.5
  196.8 0.0 copy-start.28
  196.8 0.0 copy-start.30
  196.8 22.8 %attend_back.3 = (bf16[384,1024]{1,0:T(8,128)(2,1)S(1)}, bf16[384,1024]{1,0:T(8,128)(2,1)S(1)}, bf16[384,1024]{1,0:T(8,128)(2,1)S(1)}, f32[8,192]{1,0:T(8,128)S(1)}, f32[24,384]{1,0:T(8,128)S(1)}) custom-call(s32[4]{0:T(128)S(1)} %copy-done.31, s32[4]{0:T(128)S(1)} %copy-done.32, bf16[768,1024]{1,0:T(8,128)(2,1)S(1)} %copy-done.1, ...), custom_call_target="tpu_custom_call" | custom-call | tf_op jit(solution)/shard_map/attend_back/pallas_call | solution.py:607
  219.6 0.0 collective-permute-done.4.upgot_ref
  219.6 0.0 copy-start.18
  219.6 0.8 copy-done.18
  220.4 0.0 collective-permute-done.5.downgot_ref
  220.4 0.8 copy-done.20
  221.3 0.0 copy-start.19
  221.3 1.1 copy-done.19
  222.3 1.1 copy-done.21
  223.4 0.0 copy-start.29
  223.4 0.0 copy-start.33
  223.4 64.9 %leave.1 = (f32[1024,768]{1,0:T(8,128)S(1)}, bf16[8,96,768]{2,1,0:T(8,128)(2,1)S(1)}, f32[14,768]{1,0:T(8,128)S(1)}) custom-call(s32[4,3]{1,0:T(4,128)S(1)} %copy-done.30, bf16[768,1024]{1,0:T(8,128)(2,1)S(1)} %copy-done.14, bf16[384,1024]{1,0:T(8,128)(2,1)S(1)} %get-tuple-element.89.dq0_ref, bf16[384,1024]{1,0:T(8,128)(2,1)S(1)} %get-tuple-element.97.dq1_ref, ...), custom_call_target="tpu_custom_call" | custom-call | tf_op jit(solution)/shard_map/leave/pallas_call | solution.py:1339
  288.4 0.0 copy-start.11
  288.4 1.7 copy-done.11
  290.1 11.0 %update.1 = (f32[14,192]{1,0:T(8,128)}, f32[14,192]{1,0:T(8,128)}, f32[14,192]{1,0:T(8,128)}, f32[768,768]{1,0:T(8,128)}, f32[768,768]{1,0:T(8,128)}, /*index=5*...) custom-call(s32[4,3]{1,0:T(4,128)S(1)} %copy-done.30, f32[2]{0:T(128)S(1)} %copy-done.33, ...), custom_call_target="tpu_custom_call" | custom-call | tf_op jit(solution)/shard_map/update/pallas_call | solution.py:1485
  (44 shorter events, 0.1 us)
Async XLA Ops:
  70.2 29.9 %collective-permute-start.1 = (bf16[2,4,96,768]{3,2,1,0:T(8,128)(2,1)}, bf16[2,4,96,768]{3,2,1,0:T(8,128)(2,1)S(1)}, u32[]{:S(2)}, u32[]{:S(2)}) collective-permute-start(bf16[2,4,96,768]{3,2,1,0:T(8,128)(2,1)} %get-tuple-element.77.zone_ref), channel_id=1, source_target_pairs={{0,2},{1,3},{2,0},{3,1},{4,6},{5,7},{6,4},{7,5},{8,10},{9,11},{10,... | collective-permute-start | bytes 3538952 | tf_op jit(solution)/shard_map/ppermute | solution.py:1531
  70.7 29.3 %collective-permute-start = (bf16[2,4,96,768]{3,2,1,0:T(8,128)(2,1)}, bf16[2,4,96,768]{3,2,1,0:T(8,128)(2,1)S(1)}, u32[]{:S(2)}, u32[]{:S(2)}) collective-permute-start(bf16[2,4,96,768]{3,2,1,0:T(8,128)(2,1)} %get-tuple-element.77.zone_ref), channel_id=1, source_target_pairs={{0,4},{4,0},{8,12},{12,8},{16,20},{20,16},{24,28},{28,24},{1,5},{5... | collective-permute-start | bytes 3538952 | tf_op jit(solution)/shard_map/ppermute | solution.py:1530
  71.3 30.2 %copy-start.17 = (f32[14,768]{1,0:T(8,128)S(1)}, f32[14,768]{1,0:T(8,128)}, u32[]{:S(2)}) copy-start(f32[14,768]{1,0:T(8,128)} %vec_ref.7) | copy-start | bytes 129028
  100.0 1.0 copy-start.34
  100.1 1.4 copy-start.35
  101.4 66.3 %copy-start.1 = (bf16[768,1024]{1,0:T(8,128)(2,1)S(1)}, bf16[768,1024]{1,0:T(8,128)(2,1)}, u32[]{:S(2)}) copy-start(bf16[768,1024]{1,0:T(8,128)(2,1)} %get-tuple-element.69.q_ref) | copy-start | bytes 4718596
  101.5 66.3 %copy-start.2 = (bf16[768,1024]{1,0:T(8,128)(2,1)S(1)}, bf16[768,1024]{1,0:T(8,128)(2,1)}, u32[]{:S(2)}) copy-start(bf16[768,1024]{1,0:T(8,128)(2,1)} %get-tuple-element.70.k_ref) | copy-start | bytes 4718596
  101.5 66.3 %copy-start.3 = (bf16[768,1024]{1,0:T(8,128)(2,1)S(1)}, bf16[768,1024]{1,0:T(8,128)(2,1)}, u32[]{:S(2)}) copy-start(bf16[768,1024]{1,0:T(8,128)(2,1)} %get-tuple-element.71.v_ref) | copy-start | bytes 4718596
  101.5 66.3 %copy-start.5 = (f32[384,1024]{1,0:T(8,128)S(1)}, f32[384,1024]{1,0:T(8,128)}, u32[]{:S(2)}) copy-start(f32[384,1024]{1,0:T(8,128)} %get-tuple-element.80.cos_ref) | copy-start | bytes 4718596
  101.5 66.3 %copy-start.6 = (f32[384,1024]{1,0:T(8,128)S(1)}, f32[384,1024]{1,0:T(8,128)}, u32[]{:S(2)}) copy-start(f32[384,1024]{1,0:T(8,128)} %get-tuple-element.81.sin_ref) | copy-start | bytes 4718596
  101.5 66.3 %copy-start.12 = (f32[96,1024]{1,0:T(8,128)S(1)}, f32[96,1024]{1,0:T(8,128)}, u32[]{:S(2)}) copy-start(f32[96,1024]{1,0:T(8,128)} %get-tuple-element.74.log_ref) | copy-start | bytes 1179652
  101.5 66.3 %copy-start.22 = (bf16[16,1024]{1,0:T(8,128)(2,1)S(1)}, bf16[16,1024]{1,0:T(8,128)(2,1)}, u32[]{:S(2)}) copy-start(bf16[16,1024]{1,0:T(8,128)(2,1)} %get-tuple-element.72.qmark_ref) | copy-start | bytes 98308
  101.5 66.3 %copy-start.23 = (bf16[16,1024]{1,0:T(8,128)(2,1)S(1)}, bf16[16,1024]{1,0:T(8,128)(2,1)}, u32[]{:S(2)}) copy-start(bf16[16,1024]{1,0:T(8,128)(2,1)} %get-tuple-element.73.kmark_ref) | copy-start | bytes 98308
  101.5 66.3 %copy-start.24 = (f32[8,1024]{1,0:T(8,128)S(1)}, f32[8,1024]{1,0:T(8,128)}, u32[]{:S(2)}) copy-start(f32[8,1024]{1,0:T(8,128)} %get-tuple-element.79.pos_ref) | copy-start | bytes 98308
  101.5 66.3 %copy-start.31 = (s32[4]{0:T(128)S(1)}, s32[4]{0:T(128)}, u32[]{:S(2)}) copy-start(s32[4]{0:T(128)} %height_ref.7) | copy-start | bytes 52
  101.5 66.3 %copy-start.32 = (s32[4]{0:T(128)S(1)}, s32[4]{0:T(128)}, u32[]{:S(2)}) copy-start(s32[4]{0:T(128)} %width_ref.7) | copy-start | bytes 52
  164.4 0.6 copy-start.25
  165.1 0.6 copy-start.27
  165.7 25.9 %copy-start.15 = (bf16[768,768]{1,0:T(8,128)(2,1)}, bf16[768,768]{1,0:T(8,128)(2,1)S(1)}, u32[]{:S(2)}) copy-start(bf16[768,768]{1,0:T(8,128)(2,1)S(1)} %get-tuple-element.113) | copy-start | bytes 3538948
  165.7 28.1 %collective-permute-start.2 = (bf16[2,4,96,768]{3,2,1,0:T(8,128)(2,1)}, bf16[2,4,96,768]{3,2,1,0:T(8,128)(2,1)S(1)}, u32[]{:S(2)}, u32[]{:S(2)}) collective-permute-start(bf16[2,4,96,768]{3,2,1,0:T(8,128)(2,1)} %get-tuple-element.87), channel_id=1, source_target_pairs={{0,4},{4,0},{8,12},{12,8},{16,20},{20,16},{24,28},{28,24},{1,5},{5... | collective-permute-start | bytes 3538952 | tf_op jit(solution)/shard_map/ppermute | solution.py:1549
  166.2 27.9 %collective-permute-start.3 = (bf16[8,96,768]{2,1,0:T(8,128)(2,1)S(1)}, bf16[8,96,768]{2,1,0:T(8,128)(2,1)S(1)}, u32[]{:S(2)}, u32[]{:S(2)}) collective-permute-start(bf16[8,96,768]{2,1,0:T(8,128)(2,1)S(1)} %get-tuple-element.88), channel_id=1, source_target_pairs={{0,2},{1,3},{2,0},{3,1},{4,6},{5,7},{6,4},{7,5},{8,10},{9,11},{10,... | collective-permute-start | bytes 3538952 | tf_op jit(solution)/shard_map/ppermute | solution.py:1550
  167.8 1.4 copy-start.7
  194.6 24.9 %collective-permute-start.4 = (bf16[4,96,768]{2,1,0:T(8,128)(2,1)S(1)}, bf16[4,96,768]{2,1,0:T(8,128)(2,1)S(1)}, u32[]{:S(2)}, u32[]{:S(2)}) collective-permute-start(bf16[4,96,768]{2,1,0:T(8,128)(2,1)S(1)} %get-tuple-element.109), channel_id=1, source_target_pairs={{0,2},{1,3},{2,0},{3,1},{4,6},{5,7},{6,4},{7,5},{8,10},{9,11},{10,... | collective-permute-start | bytes 1769480 | tf_op jit(solution)/shard_map/ppermute | solution.py:1554
  196.0 24.4 %collective-permute-start.5 = (bf16[4,96,768]{2,1,0:T(8,128)(2,1)S(1)}, bf16[4,96,768]{2,1,0:T(8,128)(2,1)S(1)}, u32[]{:S(2)}, u32[]{:S(2)}) collective-permute-start(bf16[4,96,768]{2,1,0:T(8,128)(2,1)S(1)} %get-tuple-element.111), channel_id=1, source_target_pairs={{0,4},{4,0},{8,12},{12,8},{16,20},{20,16},{24,28},{28,24},{1,5},{5... | collective-permute-start | bytes 1769480 | tf_op jit(solution)/shard_map/ppermute | solution.py:1555
  196.7 24.5 %copy-start = (bf16[1024,768]{1,0:T(8,128)(2,1)S(1)}, bf16[1024,768]{1,0:T(8,128)(2,1)}, u32[]{:S(2)}) copy-start(bf16[1024,768]{1,0:T(8,128)(2,1)} %x_hbm.1) | copy-start | bytes 4718596
  196.7 24.5 %copy-start.14 = (bf16[768,1024]{1,0:T(8,128)(2,1)S(1)}, bf16[768,1024]{1,0:T(8,128)(2,1)}, u32[]{:S(2)}) copy-start(bf16[768,1024]{1,0:T(8,128)(2,1)} %get-tuple-element.68.n1_ref) | copy-start | bytes 4718596
  196.7 24.5 %copy-start.16 = (bf16[768,768]{1,0:T(8,128)(2,1)S(1)}, bf16[768,768]{1,0:T(8,128)(2,1)}, u32[]{:S(2)}) copy-start(bf16[768,768]{1,0:T(8,128)(2,1)} %copy-done.15) | copy-start | bytes 3538948
  196.7 24.5 %copy-start.26 = (f32[32,768]{1,0:T(8,128)S(1)}, f32[32,768]{1,0:T(8,128)}, u32[]{:S(2)}) copy-start(f32[32,768]{1,0:T(8,128)} %copy-done.25) | copy-start | bytes 294916
  196.8 24.5 %copy-start.28 = (f32[4,8,768]{2,1,0:T(8,128)S(1)}, f32[4,8,768]{2,1,0:T(8,128)}, u32[]{:S(2)}) copy-start(f32[4,8,768]{2,1,0:T(8,128)} %copy-done.27) | copy-start | bytes 294916
  196.8 24.5 %copy-start.30 = (s32[4,3]{1,0:T(4,128)S(1)}, s32[4,3]{1,0:T(4,128)}, u32[]{:S(2)}) copy-start(s32[4,3]{1,0:T(4,128)} %owner_ref.5) | copy-start | bytes 148
  219.6 0.8 copy-start.18
  220.4 0.8 copy-start.20
  221.3 1.1 copy-start.19
  222.3 1.1 copy-start.21
  223.4 65.0 %copy-start.4 = (f32[1,1,768,768]{3,2,1,0:T(8,128)S(1)}, f32[1,1,768,768]{3,2,1,0:T(8,128)}, u32[]{:S(2)}) copy-start(f32[1,1,768,768]{3,2,1,0:T(8,128)} %param.22) | copy-start | bytes 7077892
  223.4 65.0 %copy-start.8 = (f32[1,1,768,768]{3,2,1,0:T(8,128)S(1)}, f32[1,1,768,768]{3,2,1,0:T(8,128)}, u32[]{:S(2)}) copy-start(f32[1,1,768,768]{3,2,1,0:T(8,128)} %param.23) | copy-start | bytes 7077892
  223.4 65.0 %copy-start.9 = (f32[1,1,768,768]{3,2,1,0:T(8,128)S(1)}, f32[1,1,768,768]{3,2,1,0:T(8,128)}, u32[]{:S(2)}) copy-start(f32[1,1,768,768]{3,2,1,0:T(8,128)} %param.24) | copy-start | bytes 7077892
  223.4 65.0 %copy-start.10 = (f32[1,1,768,768]{3,2,1,0:T(8,128)S(1)}, f32[1,1,768,768]{3,2,1,0:T(8,128)}, u32[]{:S(2)}) copy-start(f32[1,1,768,768]{3,2,1,0:T(8,128)} %param.25) | copy-start | bytes 7077892
  223.4 65.0 %copy-start.13 = (bf16[1024,768]{1,0:T(8,128)(2,1)S(1)}, bf16[1024,768]{1,0:T(8,128)(2,1)}, u32[]{:S(2)}) copy-start(bf16[1024,768]{1,0:T(8,128)(2,1)} %get-tuple-element.116.y_hbm) | copy-start | bytes 4718596
  223.4 65.0 %copy-start.29 = (f32[14,768]{1,0:T(8,128)S(1)}, f32[14,768]{1,0:T(8,128)}, u32[]{:S(2)}) copy-start(f32[14,768]{1,0:T(8,128)} %moment_ref.1) | copy-start | bytes 129028
  223.4 65.0 %copy-start.33 = (f32[2]{0:T(128)S(1)}, f32[2]{0:T(128)}, u32[]{:S(2)}) copy-start(f32[2]{0:T(128)} %decay_ref.1) | copy-start | bytes 28
  288.4 1.7 copy-start.11
